TPU v7x, 32 devices: a whole 2x2x4 slice. The times are simulated.
32 devices in a mesh: band: 8 (over z, y), grid: 4 (over x, core).
Axes of the slice: x: 2, y: 2, z: 4, core: 2. Of those that a mesh axis runs over, the one named last changes fastest.
Arguments:
- orbitals: bfloat16 [16, 128, 128, 128], P('band', 'grid'), may hold values from -6 to 6
- occupation: float32 [16], replicated, may hold values from 0.25 to 2
- partner: int32 [8], replicated, may hold values from 0 to 7, as said below
- col_index: int32 [8192], replicated, may hold values from 0 to 16383, as said below
- kernel: float32 [128, 8192], P(None, 'grid'), may hold values from 0.1 to 4
Outputs:
- exchange: float32 [16, 128, 128, 128], P('band', 'grid')
Inputs may be any that keep to these rules, and one draw needn't show every extreme that they name: partner[partner[a]] = a and partner[a] != a for every block a. `col_index`: all entries are distinct; the entries at positions g * 2048 to (g + 1) * 2048 - 1 are columns of the g-th block of 4096 consecutive columns, among them that block's first and last column.
All inputs are finite; a program needn't handle non-finite values.
Results may differ from a plain program's by a relative error of at most 0.0065.
Values may be sent and summed in bfloat16 or wider, within the bound.
No kernel may reach another device: no remote copies, remote signals or barrier semaphores. Data moves between devices by JAX's collectives and lax.ppermute only.
A program may use at most 64 MiB of HBM per device.

v0:
```python
import functools
import math

import jax
import jax.numpy as jnp
from jax import lax
from jax.experimental import pallas as pl
from jax.experimental.pallas import tpu as pltpu
from jax.sharding import PartitionSpec as P


BF16 = jnp.bfloat16
F32 = jnp.float32


def tables(length):
    counter = jnp.arange(length, dtype=jnp.int32)
    product = counter[:, None] * counter[None, :] % length
    angles = product.astype(F32) * (2.0 * math.pi / length)
    return jnp.cos(angles).astype(BF16), jnp.sin(angles).astype(BF16)


def block_tables(length):
    cosine, sine = tables(length)
    left = jnp.concatenate(
        [jnp.concatenate([cosine, sine], 1), jnp.concatenate([-sine, cosine], 1)], 0
    )
    right = jnp.concatenate(
        [jnp.concatenate([cosine, -sine], 1), jnp.concatenate([sine, cosine], 1)], 0
    )
    return left, right


def dot(left_side, right_side):
    return jnp.dot(left_side, right_side, preferred_element_type=F32)


def cost(flops, moved):
    return pl.CostEstimate(flops=int(flops), bytes_accessed=int(moved), transcendentals=0)


def spec(shape, index=None):
    rank = len(shape)
    return pl.BlockSpec(shape, index or (lambda *_: (0,) * rank))


SCALARS = pl.BlockSpec(memory_space=pltpu.SMEM)
WHOLE = pl.BlockSpec(memory_space=pltpu.VMEM)
UNROLL = 8
LANES = 128


def column_row(cols_ref, owner, count):
    return cols_ref[:, pl.ds(pl.multiple_of(owner * count, LANES), count)]


def flip(cols, ny, nz):
    return lax.rem(ny - cols // nz, ny) * nz + lax.rem(nz - cols % nz, nz)


def one_hot(row, base, size):
    position = lax.broadcasted_iota(jnp.int32, (size, row.shape[1]), 0) + base
    return jnp.where(row == position, 1.0, 0.0).astype(BF16)


def dot_t(left_side, right_side):
    dims = (((1,), (1,)), ((), ()))
    return lax.dot_general(left_side, right_side, dims, preferred_element_type=F32)


def mirror_kernel(span, nz, me_ref, kernel_ref, cols_ref, out_ref, first_ref):
    nx, count = kernel_ref.shape
    row = lax.broadcasted_iota(jnp.int32, (nx, nx), 0)
    column = lax.broadcasted_iota(jnp.int32, (nx, nx), 1)
    swap = jnp.where(lax.rem(row + column, nx) == 0, 1.0, 0.0).astype(BF16)
    mirrored = dot(swap, kernel_ref[...].astype(BF16)).astype(BF16)
    out_ref[...] = mirrored
    local_cols = column_row(cols_ref, me_ref[0], count) - me_ref[0] * span
    target = jnp.where(local_cols < nz, lax.rem(nz - local_cols, nz), -1)
    first_ref[...] = dot_t(mirrored, one_hot(target, 0, nz)).astype(BF16)


def mirror(me, kernel, cols, span, nz):
    nx = kernel.shape[0]
    return pl.pallas_call(
        functools.partial(mirror_kernel, span, nz),
        out_shape=[jax.ShapeDtypeStruct(kernel.shape, BF16), jax.ShapeDtypeStruct((nx, nz), BF16)],
        in_specs=[SCALARS, WHOLE, WHOLE],
        out_specs=[WHOLE] * 2,
        cost_estimate=cost(2 * nx * nx * kernel.shape[1], 6 * kernel.size),
        name="mirror",
    )(me, kernel, cols)


def expand_kernel(scale, groups, span, ny, me_ref, own_ref, neg_ref, first_ref, cols_ref, out_ref, hot):
    nx, count = own_ref.shape
    length = out_ref.shape[2]
    wide = 2 * length
    me = me_ref[0]
    both = jnp.concatenate([own_ref[...].astype(BF16), neg_ref[...]], 1)
    mine = column_row(cols_ref, me, count) - me * span
    theirs = flip(column_row(cols_ref, groups - 1 - me, count), ny, length) - me * span
    group = jnp.concatenate([mine, theirs + span], 1) // wide
    group = group - jnp.concatenate(
        [jnp.zeros((1, count), jnp.int32), jnp.full((1, count), span // wide, jnp.int32)], 1
    )
    hot[:, :count] = one_hot(mine & (wide - 1), 0, wide)
    hot[:, count:] = one_hot(theirs & (wide - 1), 0, wide)

    def step(number, carry):
        sides = []
        for k in range(2):
            wanted = jnp.where(group == 2 * number + k, 1.0, 0.0).astype(BF16)
            sides.append(both * wanted)
        total = dot_t(jnp.concatenate(sides, 0), hot[...])
        for k in range(2):
            for half in range(2):
                out_ref[4 * number + 2 * k + half] = (
                    total[k * nx : (k + 1) * nx, half * length : (half + 1) * length] * scale
                )
        return carry

    lax.fori_loop(0, out_ref.shape[0] // 4, step, 0)
    out_ref[0] = out_ref[0] + first_ref[...].astype(F32) * scale


def expand(me, kernel, neg, first, cols, groups, ny, length, scale):
    nx, count = kernel.shape
    rows = ny // groups
    return pl.pallas_call(
        functools.partial(expand_kernel, scale, groups, rows * length, ny),
        out_shape=jax.ShapeDtypeStruct((rows, nx, length), F32),
        in_specs=[SCALARS] + [WHOLE] * 4,
        out_specs=WHOLE,
        scratch_shapes=[pltpu.VMEM((2 * length, 2 * count), BF16)],
        cost_estimate=cost(4 * nx * count * rows * length, 4 * nx * (count + rows * length)),
        name="expand",
    )(me, kernel, neg, first, cols)


def forward_kernel(parts, base, me_ref, grid_ref, own_ref, *refs):
    piece_refs = refs[:parts]
    if parts > 1:
        zt_ref, yt_ref, their_ref = refs[parts : parts + 3]
        per = piece_refs[0].shape[0]
        for slot, piece_ref in enumerate(piece_refs):
            their_ref[pl.ds((me_ref[0] ^ slot) * per, per)] = piece_ref[...]
    else:
        their_ref, zt_ref, yt_ref = refs[:3]
    out_refs, hold = refs[3 + parts - (parts == 1) : -1], refs[-1]
    count, ny, nz = own_ref.shape[1:]
    tiles = ny // their_ref.shape[1]
    zt, yt = zt_ref[...], yt_ref[...]

    def step(pair, carry):
        lines = []
        for k in range(2):
            x = 2 * pair + k
            theirs = their_ref[pl.ds((base + x) * tiles, tiles)].reshape(ny, nz)
            lines.append(jnp.concatenate([own_ref[0, x] * theirs, own_ref[1, x] * theirs], 1))
        first = dot(jnp.concatenate(lines, 0), zt).astype(BF16)
        stack = jnp.concatenate(
            [
                jnp.concatenate([first[:ny, :nz], first[ny:, :nz]], 1),
                jnp.concatenate([first[:ny, nz:], first[ny:, nz:]], 1),
            ],
            0,
        )
        second = dot(yt, stack)
        for k in range(2):
            for c in range(2):
                hold[c, pl.ds(2 * pair + k, ny, stride=count), :] = second[
                    c * ny : (c + 1) * ny, k * nz : (k + 1) * nz
                ]
        return carry

    lax.fori_loop(0, count // 2, step, 0, unroll=min(UNROLL, count // 2))
    part = ny // len(out_refs)
    for slot, out_ref in enumerate(out_refs):
        begin = (grid_ref[0] ^ slot) * (part * count)
        for c in range(2):
            piece = hold[c, pl.ds(begin, part * count), :]
            out_ref[:, c] = piece.astype(BF16).reshape(part, count, nz)


def forward(me, grid_pos, own, pieces, half, count, zt, yt, groups):
    ny, nz = own.shape[2:]
    part = ny // groups
    parts = len(pieces)
    shape = jax.ShapeDtypeStruct((part, 2, count, nz), BF16)
    their = jax.ShapeDtypeStruct((parts * pieces[0].shape[0],) + pieces[0].shape[1:], BF16)
    outs = ([their] if parts > 1 else []) + [shape] * groups
    return pl.pallas_call(
        functools.partial(forward_kernel, parts, half * count),
        grid=(1,),
        out_shape=outs,
        in_specs=[SCALARS, SCALARS, spec((2, count, ny, nz), lambda i: (0, half, 0, 0))]
        + [spec(p.shape) for p in pieces]
        + [spec(zt.shape), spec(yt.shape)],
        out_specs=[spec(o.shape) for o in outs],
        scratch_shapes=[pltpu.VMEM((2, ny * count, nz), F32)],
        cost_estimate=cost(2 * count * ny * nz * 2 * (2 * ny + 2 * nz), 12 * count * ny * nz),
        name="forward",
    )(me, grid_pos, own, *pieces, zt, yt)


def middle_kernel(groups, halves, grid_ref, *refs):
    in_refs = refs[: groups * halves]
    kern_ref, xt_ref, ixt_ref = refs[groups * halves : groups * halves + 3]
    out_refs, hold = refs[groups * halves + 3 : -1], refs[-1]
    count, nx, nz = kern_ref.shape
    xt, ixt = xt_ref[...], ixt_ref[...]

    def step(pair, carry):
        lines, factors = [], []
        for k in range(2):
            line = 2 * pair + k
            lines.append(jnp.concatenate([r[line, c] for c in range(2) for r in in_refs], 0))
            factors.append(kern_ref[line])
        factor = jnp.concatenate(factors, 1)
        spectrum = dot(xt, jnp.concatenate(lines, 1))
        scaled = jnp.concatenate(
            [(spectrum[:nx] * factor).astype(BF16), (spectrum[nx:] * factor).astype(BF16)], 0
        )
        third = dot(ixt, scaled)
        for k in range(2):
            for c in range(2):
                hold[c, pl.ds(2 * pair + k, nx, stride=count), :] = third[
                    c * nx : (c + 1) * nx, k * nz : (k + 1) * nz
                ]
        return carry

    lax.fori_loop(0, count // 2, step, 0, unroll=min(UNROLL, count // 2))
    rows = nx // (groups * halves)
    for number, out_ref in enumerate(out_refs):
        owner = grid_ref[0] ^ (number // halves)
        begin = (owner * halves + number % halves) * (rows * count)
        for c in range(2):
            piece = hold[c, pl.ds(begin, rows * count), :]
            out_ref[:, c] = piece.astype(BF16).reshape(rows, count, nz)


def middle(grid_pos, pieces, kern, xt, ixt, groups, halves):
    count, nx, nz = kern.shape
    rows = nx // (groups * halves)
    shape = jax.ShapeDtypeStruct((rows, 2, count, nz), BF16)
    vmem = pl.BlockSpec(memory_space=pltpu.VMEM)
    return pl.pallas_call(
        functools.partial(middle_kernel, groups, halves),
        out_shape=[shape] * (groups * halves),
        in_specs=[SCALARS] + [vmem] * (groups * halves + 3),
        out_specs=[vmem] * (groups * halves),
        scratch_shapes=[pltpu.VMEM((2, nx * count, nz), F32)],
        cost_estimate=cost(16 * nx * nx * count * nz, 12 * count * nx * nz),
        name="middle",
    )(grid_pos, *pieces, kern, xt, ixt)


def backward_kernel(groups, has_total, base, *refs):
    in_refs = refs[:groups]
    their_ref, weight_ref, yt_ref, zt_ref = refs[groups : groups + 4]
    total_ref = refs[groups + 4] if has_total == 2 else None
    out_ref = refs[-1]
    count, ny, nz = out_ref.shape[1:]
    tiles = ny // their_ref.shape[1]
    zt, yt = zt_ref[...], yt_ref[...]
    weight = weight_ref[0]

    def step(pair, carry):
        lines = []
        for k in range(2):
            x = 2 * pair + k
            lines.append(jnp.concatenate([r[x, c] for c in range(2) for r in in_refs], 0))
        fourth = dot(yt, jnp.concatenate(lines, 1)).astype(BF16)
        stack = jnp.concatenate(
            [
                jnp.concatenate([fourth[:ny, k * nz : (k + 1) * nz], fourth[ny:, k * nz : (k + 1) * nz]], 1)
                for k in range(2)
            ],
            0,
        )
        potential = dot(stack, zt)
        for k in range(2):
            x = 2 * pair + k
            theirs = their_ref[pl.ds((base + x) * tiles, tiles)].reshape(ny, nz).astype(F32) * weight
            for n in range(2):
                term = potential[k * ny : (k + 1) * ny, n * nz : (n + 1) * nz] * theirs
                if total_ref is None:
                    out_ref[n, x] = -term
                else:
                    out_ref[n, x] = total_ref[n, x] - term
        return carry

    lax.fori_loop(0, count // 2, step, 0, unroll=min(UNROLL, count // 2))


def backward(pieces, their, weight, yt, zt, total, accumulate, part_number, slab):
    groups = len(pieces)
    count, ny, nz = pieces[0].shape[0], pieces[0].shape[2] * groups, pieces[0].shape[3]
    block = spec((2, count, ny, nz), lambda i: (0, part_number, 0, 0))
    has_total = 0 if total is None else (2 if accumulate else 1)
    extra = [] if total is None else [total]
    extra_specs = [] if total is None else [block if accumulate else pl.BlockSpec(memory_space=pl.ANY)]
    return pl.pallas_call(
        functools.partial(backward_kernel, groups, has_total, part_number * count),
        grid=(1,),
        out_shape=jax.ShapeDtypeStruct((2, slab, ny, nz), F32),
        in_specs=[spec(p.shape) for p in pieces]
        + [spec(their.shape), pl.BlockSpec(memory_space=pltpu.SMEM), spec(yt.shape), spec(zt.shape)]
        + extra_specs,
        out_specs=block,
        input_output_aliases={groups + 4: 0} if extra else {},
        cost_estimate=cost(2 * count * ny * nz * 2 * (2 * ny + 2 * nz), 24 * count * ny * nz),
        name="backward",
    )(*pieces, their, weight, yt, zt, *extra)


HALVES = (1, 2)
TILE = 16


def after(value, *others):
    return lax.optimization_barrier((value, others))[0]


def shift(value, axis, size, mask):
    return lax.ppermute(value, axis, [(i, i ^ mask) for i in range(size)]) if mask else value


def split_kernel(me_ref, in_ref, *out_refs):
    per = out_refs[0].shape[0]
    for slot, out_ref in enumerate(out_refs):
        out_ref[...] = in_ref[0, pl.ds((me_ref[0] ^ slot) * per, per)]


def split(me, value, band, chunk, tiles, parts):
    shape = jax.ShapeDtypeStruct((tiles // parts,) + value.shape[2:], value.dtype)
    return pl.pallas_call(
        split_kernel,
        grid=(1,),
        out_shape=[shape] * parts,
        in_specs=[SCALARS, spec((1, tiles) + value.shape[2:], lambda i: (band, chunk, 0, 0))],
        out_specs=[spec(shape.shape)] * parts,
        cost_estimate=cost(0, 4 * tiles * TILE * value.shape[3]),
        name="split",
    )(me, value)


def pick_kernel(parts, choice_ref, *refs):
    in_refs, out_refs, hold = refs[:parts], refs[parts:-1], refs[-1]
    for slot, in_ref in enumerate(in_refs):
        hold[slot] = in_ref[...]
    for slot, out_ref in enumerate(out_refs):
        out_ref[...] = hold[choice_ref[slot]]


def pick(choice, pieces):
    parts, shape = len(pieces), pieces[0].shape
    return pl.pallas_call(
        functools.partial(pick_kernel, parts),
        out_shape=[jax.ShapeDtypeStruct(shape, pieces[0].dtype)] * parts,
        in_specs=[SCALARS] + [WHOLE] * parts,
        out_specs=[WHOLE] * parts,
        scratch_shapes=[pltpu.VMEM((parts,) + shape, pieces[0].dtype)],
        cost_estimate=cost(0, 4 * parts * math.prod(shape)),
        name="pick",
    )(choice, *pieces)


def pick_stacked_kernel(parts, choice_ref, *refs):
    in_refs, out_ref, hold = refs[:parts], refs[-2], refs[-1]
    for slot, in_ref in enumerate(in_refs):
        hold[slot] = in_ref[...]
    for number in range(parts):
        out_ref[number] = hold[choice_ref[number]]


def pick_stacked(choice, pieces):
    parts, shape = len(pieces), pieces[0].shape
    return pl.pallas_call(
        functools.partial(pick_stacked_kernel, parts),
        out_shape=jax.ShapeDtypeStruct((parts,) + shape, pieces[0].dtype),
        in_specs=[SCALARS] + [WHOLE] * parts,
        out_specs=WHOLE,
        scratch_shapes=[pltpu.VMEM((parts,) + shape, pieces[0].dtype)],
        cost_estimate=cost(0, 4 * parts * math.prod(shape)),
        name="pick",
    )(choice, *pieces)


def local(orbitals, occupation, partner, col_index, kernel):
    bands, groups = lax.axis_size("band"), lax.axis_size("grid")
    slab, ny, nz = orbitals.shape[1:]
    nx, _ = kernel.shape
    lines = ny // groups
    band_pos, me = lax.axis_index("band"), lax.axis_index("grid")
    band_slots = jnp.arange(bands, dtype=jnp.int32)
    my_band = band_pos.astype(jnp.int32).reshape(1)
    choice = jnp.take(partner, band_slots ^ band_pos) ^ band_pos
    pick_choice = partner ^ band_pos
    tiled = orbitals.reshape(2, slab * ny // TILE, TILE, nz)

    def swap(value, slot):
        return shift(value, "grid", groups, slot)

    def exchange(value):
        return lax.all_to_all(value, "band", split_axis=0, concat_axis=0, tiled=True)

    def slotwise(sent):
        return [shift(piece, "band", bands, slot) for slot, piece in enumerate(sent)]

    my_grid = me.astype(jnp.int32).reshape(1)
    cols = col_index.reshape(1, -1)
    sent = split(my_band, tiled, 0, 0, slab * ny // TILE, bands)
    arrived = slotwise(sent)
    sent1 = split(my_band, after(tiled, *sent), 1, 0, slab * ny // TILE, bands)

    mirror_of = [(i, groups - 1 - i) for i in range(groups)]
    mirror_first = [(i, (groups - i) % groups) for i in range(groups)]
    mirrored, first_line = mirror(my_grid, after(kernel, *sent), cols, lines * nz, nz)
    neg = lax.ppermute(mirrored, "grid", mirror_of)
    first = lax.ppermute(first_line, "grid", mirror_first)

    def slots(table, axis):
        shape = table.shape
        blocks = table.reshape(shape[:axis] + (2, groups, shape[axis] // (2 * groups)) + shape[axis + 1 :])
        order = jnp.arange(groups, dtype=jnp.int32) ^ me
        return jnp.take(blocks, order, axis=axis + 1).reshape(shape)

    xleft, xright = block_tables(nx)
    yleft, yright = block_tables(ny)
    zleft, zright = block_tables(nz)
    x_forward, y_inverse = slots(xleft, 1), slots(yright, 1)
    theirs, answers, counts = [], [], []
    for m in range(2):
        halves = HALVES[m] if slab % (16 * HALVES[m]) == 0 else 1
        rows = slab // halves
        if m == 0:
            picked = pick(choice, after(arrived, mirrored, first_line, *sent1))
            fetched = slotwise(picked)
            kern = expand(
                my_grid, after(kernel, *picked), neg, first, cols, groups, ny, nz, 0.5 / (nx * ny * nz)
            )
            arrived = slotwise(after(sent1, *picked))
            their, *sent = forward(my_band, my_grid, orbitals, fetched, 0, rows, zright, yleft, groups)
        else:
            picked = pick_stacked(pick_choice, after(arrived, *sent))
            their = exchange(picked.reshape(tiled.shape[1:]))
            their = after(their, *answers[0])
            sent = forward(my_band, my_grid, orbitals, [their], 0, rows, zright, yleft, groups)
        pieces = [[swap(value, slot)] for slot, value in enumerate(sent)]
        for h in range(1, halves):
            more = forward(my_band, my_grid, orbitals, [their], h, rows, zright, yleft, groups)
            for slot, value in enumerate(more):
                pieces[slot].append(swap(value, slot))
        flat = [piece for per_slot in pieces for piece in per_slot]
        answers.append(middle(my_grid, flat, kern, x_forward, xright, groups, halves))
        theirs.append(their)
        counts.append(halves)

    total = None
    for m in range(2):
        weight = lax.dynamic_slice_in_dim(occupation, partner[band_pos] * 2 + m, 1, 0)
        for h in range(counts[m]):
            back = [swap(answers[m][slot * counts[m] + h], slot) for slot in range(groups)]
            if m == 0:
                back = after(back, *answers[1])
            total = backward(back, theirs[m], weight, y_inverse, zleft, total, m > 0, h, slab)
    return total


def solution(mesh):
    in_specs = (P("band", "grid", None, None), P(), P(), P(), P(None, "grid"))
    out_specs = P("band", "grid", None, None)
    return jax.shard_map(local, mesh=mesh, in_specs=in_specs, out_specs=out_specs, check_vma=False)
```

profile of v0, /device:TPU:0, one launch (start us, length us, event | category | flops | bytes accessed | tf_op | source)
XLA Modules:
  0.0 224.3 jit_solution(3889092232407942151)
XLA Ops:
  0.0 2.3 %split.2 = (bf16[32,16,128]{2,1,0:T(8,128)(2,1)}, bf16[32,16,128]{2,1,0:T(8,128)(2,1)}, bf16[32,16,128]{2,1,0:T(8,128)(2,1)}, bf16[32,16,128]{2,1,0:T(8,128)(2,1...) custom-call(s32[1]{0:T(128)} %bitcast.1.me_ref, ...), custom_call_target="tpu_custom_call" | custom-call | bytes 2097152 | tf_op jit(solution)/shard_map/split/pallas_call | solution.py:338
  2.3 3.0 %collective-permute-start = (bf16[32,16,128]{2,1,0:T(8,128)(2,1)}, bf16[32,16,128]{2,1,0:T(8,128)(2,1)S(1)}, u32[]{:S(2)}, u32[]{:S(2)}) collective-permute-start(bf16[32,16,128]{2,1,0:T(8,128)(2,1)} %get-tuple-element.90), channel_id=1, source_target_pairs={{0,4},{4,0},{8,12},{12,8},{16,20},{20,16},{24,28},{28,24},{1,5},{5... | collective-permute-start | bytes 393224 | tf_op jit(solution)/shard_map/ppermute | solution.py:327
  6.9 3.0 %collective-permute-start.3 = (bf16[32,16,128]{2,1,0:T(8,128)(2,1)}, bf16[32,16,128]{2,1,0:T(8,128)(2,1)S(1)}, u32[]{:S(2)}, u32[]{:S(2)}) collective-permute-start(bf16[32,16,128]{2,1,0:T(8,128)(2,1)} %get-tuple-element.93), channel_id=1, source_target_pairs={{0,16},{4,20},{8,24},{12,28},{16,0},{20,4},{24,8},{28,12},{1,17},{... | collective-permute-start | bytes 393224 | tf_op jit(solution)/shard_map/ppermute | solution.py:327
  11.1 2.3 %split.3 = (bf16[32,16,128]{2,1,0:T(8,128)(2,1)}, bf16[32,16,128]{2,1,0:T(8,128)(2,1)}, bf16[32,16,128]{2,1,0:T(8,128)(2,1)}, bf16[32,16,128]{2,1,0:T(8,128)(2,1...) custom-call(s32[1]{0:T(128)} %bitcast.1.me_ref, ...), custom_call_target="tpu_custom_call" | custom-call | bytes 2097152 | tf_op jit(solution)/shard_map/split/pallas_call | solution.py:338
  14.1 2.4 %mirror.1 = (bf16[128,2048]{1,0:T(8,128)(2,1)}, bf16[128,128]{1,0:T(8,128)(2,1)}) custom-call(s32[1]{0:T(128)} %bitcast.me_ref.grid_ref, f32[128,2048]{1,0:T(8,128)} %own_ref.4, s32[1,8192]{1,0:T(1,128)} %bitcast.23), custom_call_target="tpu_custom_call" | custom-call | flops 67108864 | bytes 1572864 | tf_op jit(solution)/shard_map/mirror/pallas_call | solution.py:85
  16.5 3.7 %collective-permute-start.5 = (bf16[32,16,128]{2,1,0:T(8,128)(2,1)}, bf16[32,16,128]{2,1,0:T(8,128)(2,1)S(1)}, u32[]{:S(2)}, u32[]{:S(2)}) collective-permute-start(bf16[32,16,128]{2,1,0:T(8,128)(2,1)} %get-tuple-element.95), channel_id=1, source_target_pairs={{0,24},{4,28},{8,16},{12,20},{16,8},{20,12},{24,0},{28,4},{1,25},{... | collective-permute-start | bytes 393224 | tf_op jit(solution)/shard_map/ppermute | solution.py:327
  20.8 8.7 %collective-permute-done.4.refs_5_ = bf16[32,16,128]{2,1,0:T(8,128)(2,1)S(1)} collective-permute-done((bf16[32,16,128]{2,1,0:T(8,128)(2,1)}, bf16[32,16,128]{2,1,0:T(8,128)(2,1)S(1)}, u32[]{:S(2)}, u32[]{:S(2)}) %collective-permute-start.4) | collective-permute-done | bytes 131104 | tf_op jit(solution)/shard_map/ppermute | solution.py:327
  30.3 2.3 %pick.2 = (bf16[32,16,128]{2,1,0:T(8,128)(2,1)}, bf16[32,16,128]{2,1,0:T(8,128)(2,1)}, bf16[32,16,128]{2,1,0:T(8,128)(2,1)}, bf16[32,16,128]{2,1,0:T(8,128)(2,1)...) custom-call(s32[8]{0:T(128)} %get-tuple-element.178.choice_ref, ...), custom_call_target="tpu_custom_call" | custom-call | bytes 2097152 | tf_op jit(solution)/shard_map/pick/pallas_call | solution.py:359
  32.6 5.3 %collective-permute-start.8 = (bf16[32,16,128]{2,1,0:T(8,128)(2,1)}, bf16[32,16,128]{2,1,0:T(8,128)(2,1)S(1)}, u32[]{:S(2)}, u32[]{:S(2)}) collective-permute-start(bf16[32,16,128]{2,1,0:T(8,128)(2,1)} %get-tuple-element.127), channel_id=1, source_target_pairs={{0,8},{4,12},{8,0},{12,4},{16,24},{20,28},{24,16},{28,20},{1,9},{5... | collective-permute-start | bytes 393224 | tf_op jit(solution)/shard_map/ppermute | solution.py:327
  41.4 3.4 %collective-permute-start.17 = (bf16[32,16,128]{2,1,0:T(8,128)(2,1)}, bf16[32,16,128]{2,1,0:T(8,128)(2,1)S(1)}, u32[]{:S(2)}, u32[]{:S(2)}) collective-permute-start(bf16[32,16,128]{2,1,0:T(8,128)(2,1)} %get-tuple-element.121), channel_id=1, source_target_pairs={{0,16},{4,20},{8,24},{12,28},{16,0},{20,4},{24,8},{28,12},{1,17},{... | collective-permute-start | bytes 393224 | tf_op jit(solution)/shard_map/ppermute | solution.py:327
  48.6 3.4 %collective-permute-start.20 = (bf16[32,16,128]{2,1,0:T(8,128)(2,1)}, bf16[32,16,128]{2,1,0:T(8,128)(2,1)S(1)}, u32[]{:S(2)}, u32[]{:S(2)}) collective-permute-start(bf16[32,16,128]{2,1,0:T(8,128)(2,1)} %get-tuple-element.124), channel_id=1, source_target_pairs={{0,28},{4,24},{8,20},{12,16},{16,12},{20,8},{24,4},{28,0},{1,29},{... | collective-permute-start | bytes 393224 | tf_op jit(solution)/shard_map/ppermute | solution.py:327
  52.6 5.5 %collective-permute-done.17.refs_4_ = bf16[32,16,128]{2,1,0:T(8,128)(2,1)S(1)} collective-permute-done((bf16[32,16,128]{2,1,0:T(8,128)(2,1)}, bf16[32,16,128]{2,1,0:T(8,128)(2,1)S(1)}, u32[]{:S(2)}, u32[]{:S(2)}) %collective-permute-start.17) | collective-permute-done | bytes 131104 | tf_op jit(solution)/shard_map/ppermute | solution.py:327
  58.1 13.0 %collective-permute-done.18.refs_5_ = bf16[32,16,128]{2,1,0:T(8,128)(2,1)S(1)} collective-permute-done((bf16[32,16,128]{2,1,0:T(8,128)(2,1)}, bf16[32,16,128]{2,1,0:T(8,128)(2,1)S(1)}, u32[]{:S(2)}, u32[]{:S(2)}) %collective-permute-start.18) | collective-permute-done | bytes 131104 | tf_op jit(solution)/shard_map/ppermute | solution.py:327
  75.7 7.5 %forward.3 = (bf16[256,16,128]{2,1,0:T(8,128)(2,1)}, bf16[32,2,32,128]{3,2,1,0:T(8,128)(2,1)}, bf16[32,2,32,128]{3,2,1,0:T(8,128)(2,1)}, bf16[32,2,32,128]{3,2,1,0:T(8,128)(2,1)}, bf16[32,2,32,128]{3,2,1,0:T(8,128)(2,1)}) custom-call(s32[1]{0:T(128)} %bitcast.1.me_ref, s32[1]{0:T(128)} %bitcast.me_ref.grid_ref, bf16[2,32,128,128]{3,2,1,0:T(8,128)(2,1)} %own_ref.6, ...), custom_call_target="tpu_custom_call" | custom-call | flops 1073741824 | bytes 6291456 | tf_op jit(solution)/shard_map/forward/pallas_call | solution.py:193
  83.2 3.3 %collective-permute-done.11.refs_5_ = bf16[32,16,128]{2,1,0:T(8,128)(2,1)S(1)} collective-permute-done((bf16[32,16,128]{2,1,0:T(8,128)(2,1)}, bf16[32,16,128]{2,1,0:T(8,128)(2,1)S(1)}, u32[]{:S(2)}, u32[]{:S(2)}) %collective-permute-start.11) | collective-permute-done | bytes 131104 | tf_op jit(solution)/shard_map/ppermute | solution.py:327
  87.3 2.4 %pick.3 = bf16[8,32,16,128]{3,2,1,0:T(8,128)(2,1)} custom-call(s32[8]{0:T(128)} %get-tuple-element.179.choice_ref, bf16[32,16,128]{2,1,0:T(8,128)(2,1)} %get-tuple-element.137.refs_0_, bf16[32,16,128]{2,1,0:T(8,128)(2,1)} %copy-done.22, bf16[32,16,128]{2,1,0:T(8,128)(2,1)} %copy-done.23, bf16[32,16,128]{2,1,0:T(8,128)(2,1)} %copy-done.24, ...), custom_call_target="tpu_custom_call" | custom-call | bytes 2097152 | tf_op jit(solution)/shard_map/pick/pallas_call | solution.py:380
  89.7 6.7 %all-to-all-start = ((bf16[256,16,128]{2,1,0:T(8,128)(2,1)}), bf16[256,16,128]{2,1,0:T(8,128)(2,1)S(1)}, u32[]{:S(2)}, u32[]{:S(2)}) async-start(bf16[256,16,128]{2,1,0:T(8,128)(2,1)} %bitcast.18), calls=%async_computation | async-start | bytes 2097152 | tf_op jit(solution)/shard_map/all_to_all | solution.py:407
  103.8 8.9 %collective-permute-done.24.neg_ref = bf16[128,2048]{1,0:T(8,128)(2,1)} collective-permute-done((bf16[128,2048]{1,0:T(8,128)(2,1)S(1)}, bf16[128,2048]{1,0:T(8,128)(2,1)}, u32[]{:S(2)}, u32[]{:S(2)}) %collective-permute-start.24) | collective-permute-done | bytes 524320 | tf_op jit(solution)/shard_map/ppermute | solution.py:421
  112.7 9.5 %expand.1.refs_4_.refs_8_ = f32[32,128,128]{2,1,0:T(8,128)} custom-call(s32[1]{0:T(128)} %bitcast.me_ref.grid_ref, f32[128,2048]{1,0:T(8,128)} %own_ref.4, bf16[128,2048]{1,0:T(8,128)(2,1)} %collective-permute-done.24.neg_ref, bf16[128,128]{1,0:T(8,128)(2,1)} %collective-permute-done.25.first_ref, s32[1,8192]{1,0:T(1,128)} %bitcast.24), custom_call_target="tpu_custom_call" | custom-call | flops 4294967296 | bytes 3145728 | tf_op jit(solution)/shard_map/expand/pallas_call | solution.py:130
  123.9 11.2 %collective-permute-done.23.refs_3_ = bf16[32,2,32,128]{3,2,1,0:T(8,128)(2,1)S(1)} collective-permute-done((bf16[32,2,32,128]{3,2,1,0:T(8,128)(2,1)}, bf16[32,2,32,128]{3,2,1,0:T(8,128)(2,1)S(1)}, u32[]{:S(2)}, u32[]{:S(2)}) %collective-permute-start.23) | collective-permute-done | bytes 524320 | tf_op jit(solution)/shard_map/ppermute | solution.py:327
  135.9 7.7 %middle.2 = (bf16[32,2,32,128]{3,2,1,0:T(8,128)(2,1)}, bf16[32,2,32,128]{3,2,1,0:T(8,128)(2,1)}, bf16[32,2,32,128]{3,2,1,0:T(8,128)(2,1)}, bf16[32,2,32,128]{3,2,1,0:T(8,128)(2,1)}) custom-call(s32[1]{0:T(128)} %bitcast.me_ref.grid_ref, bf16[32,2,32,128]{3,2,1,0:T(8,128)(2,1)} %get-tuple-element.133.refs_0_, bf16[32,2,32,128]{3,2,1,0:T(8,128)(2,1)} %copy-done.4, ...), custom_call_target="tpu_custom_call" | custom-call | flops 1073741824 | bytes 6291456 | tf_op jit(solution)/shard_map/middle/pallas_call | solution.py:248
  144.6 3.7 %forward.5 = (bf16[32,2,16,128]{3,2,1,0:T(8,128)(2,1)}, bf16[32,2,16,128]{3,2,1,0:T(8,128)(2,1)}, bf16[32,2,16,128]{3,2,1,0:T(8,128)(2,1)}, bf16[32,2,16,128]{3,2,1,0:T(8,128)(2,1)}) custom-call(s32[1]{0:T(128)} %bitcast.1.me_ref, s32[1]{0:T(128)} %bitcast.me_ref.grid_ref, bf16[2,32,128,128]{3,2,1,0:T(8,128)(2,1)} %own_ref.6, ...), custom_call_target="tpu_custom_call" | custom-call | flops 536870912 | bytes 3145728 | tf_op jit(solution)/shard_map/forward/pallas_call | solution.py:193
  150.2 3.8 %forward.4 = (bf16[32,2,16,128]{3,2,1,0:T(8,128)(2,1)}, bf16[32,2,16,128]{3,2,1,0:T(8,128)(2,1)}, bf16[32,2,16,128]{3,2,1,0:T(8,128)(2,1)}, bf16[32,2,16,128]{3,2,1,0:T(8,128)(2,1)}) custom-call(s32[1]{0:T(128)} %bitcast.1.me_ref, s32[1]{0:T(128)} %bitcast.me_ref.grid_ref, bf16[2,32,128,128]{3,2,1,0:T(8,128)(2,1)} %own_ref.6, ...), custom_call_target="tpu_custom_call" | custom-call | flops 536870912 | bytes 3145728 | tf_op jit(solution)/shard_map/forward/pallas_call | solution.py:193
  157.8 4.5 %collective-permute-done.31.refs_7_ = bf16[32,2,16,128]{3,2,1,0:T(8,128)(2,1)S(1)} collective-permute-done((bf16[32,2,16,128]{3,2,1,0:T(8,128)(2,1)}, bf16[32,2,16,128]{3,2,1,0:T(8,128)(2,1)S(1)}, u32[]{:S(2)}, u32[]{:S(2)}) %collective-permute-start.31) | collective-permute-done | bytes 262176 | tf_op jit(solution)/shard_map/ppermute | solution.py:327
  164.6 4.4 %collective-permute-done.28.refs_4_ = bf16[32,2,16,128]{3,2,1,0:T(8,128)(2,1)S(1)} collective-permute-done((bf16[32,2,16,128]{3,2,1,0:T(8,128)(2,1)}, bf16[32,2,16,128]{3,2,1,0:T(8,128)(2,1)S(1)}, u32[]{:S(2)}, u32[]{:S(2)}) %collective-permute-start.28) | collective-permute-done | bytes 262176 | tf_op jit(solution)/shard_map/ppermute | solution.py:327
  169.1 4.5 %collective-permute-done.30.refs_6_ = bf16[32,2,16,128]{3,2,1,0:T(8,128)(2,1)S(1)} collective-permute-done((bf16[32,2,16,128]{3,2,1,0:T(8,128)(2,1)}, bf16[32,2,16,128]{3,2,1,0:T(8,128)(2,1)S(1)}, u32[]{:S(2)}, u32[]{:S(2)}) %collective-permute-start.30) | collective-permute-done | bytes 262176 | tf_op jit(solution)/shard_map/ppermute | solution.py:327
  174.2 7.7 %middle.3 = (bf16[16,2,32,128]{3,2,1,0:T(8,128)(2,1)}, bf16[16,2,32,128]{3,2,1,0:T(8,128)(2,1)}, bf16[16,2,32,128]{3,2,1,0:T(8,128)(2,1)}, bf16[16,2,32,128]{3,2...) custom-call(s32[1]{0:T(128)} %bitcast.me_ref.grid_ref, ...), custom_call_target="tpu_custom_call" | custom-call | flops 1073741824 | bytes 6291456 | tf_op jit(solution)/shard_map/middle/pallas_call | solution.py:248
  185.9 10.1 %collective-permute-done.40.refs_3_ = bf16[32,2,32,128]{3,2,1,0:T(8,128)(2,1)S(1)} collective-permute-done((bf16[32,2,32,128]{3,2,1,0:T(8,128)(2,1)}, bf16[32,2,32,128]{3,2,1,0:T(8,128)(2,1)S(1)}, u32[]{:S(2)}, u32[]{:S(2)}) %collective-permute-start.40) | collective-permute-done | bytes 524320 | tf_op jit(solution)/shard_map/ppermute | solution.py:327
  201.0 6.3 %backward.3.refs_8_ = f32[2,32,128,128]{3,2,1,0:T(8,128)} custom-call(bf16[32,2,32,128]{3,2,1,0:T(8,128)(2,1)} %get-tuple-element.167.refs_0_, bf16[32,2,32,128]{3,2,1,0:T(8,128)(2,1)} %copy-done.7, bf16[32,2,32,128]{3,2,1,0:T(8,128)(2,1)} %copy-done.8, bf16[32,2,32,128]{3,2,1,0:T(8,128)(2,1)} %copy-done.9, ...), custom_call_target="tpu_custom_call" | custom-call | flops 1073741824 | bytes 12582912 | tf_op jit(solution)/shard_map/backward/pallas_call | solution.py:304
  208.1 5.1 %backward.4.refs_8_ = f32[2,32,128,128]{3,2,1,0:T(8,128)} custom-call(bf16[16,2,32,128]{3,2,1,0:T(8,128)(2,1)} %get-tuple-element.163.refs_0_, bf16[16,2,32,128]{3,2,1,0:T(8,128)(2,1)} %copy-done.10, bf16[16,2,32,128]{3,2,1,0:T(8,128)(2,1)} %copy-done.12, bf16[16,2,32,128]{3,2,1,0:T(8,128)(2,1)} %copy-done.14, ...), custom_call_target="tpu_custom_call", output_to_operand_aliasing={{}: (8, {})} | custom-call | flops 536870912 | bytes 6291456 | tf_op jit(solution)/shard_map/backward/pallas_call | solution.py:304
  214.0 4.5 %collective-permute-done.34.refs_3_ = bf16[16,2,32,128]{3,2,1,0:T(8,128)(2,1)S(1)} collective-permute-done((bf16[16,2,32,128]{3,2,1,0:T(8,128)(2,1)}, bf16[16,2,32,128]{3,2,1,0:T(8,128)(2,1)S(1)}, u32[]{:S(2)}, u32[]{:S(2)}) %collective-permute-start.34) | collective-permute-done | bytes 262176 | tf_op jit(solution)/shard_map/ppermute | solution.py:327
  219.2 5.1 %backward.5 = f32[2,32,128,128]{3,2,1,0:T(8,128)} custom-call(bf16[16,2,32,128]{3,2,1,0:T(8,128)(2,1)} %get-tuple-element.159.refs_0_, bf16[16,2,32,128]{3,2,1,0:T(8,128)(2,1)} %copy-done.11, bf16[16,2,32,128]{3,2,1,0:T(8,128)(2,1)} %copy-done.13, bf16[16,2,32,128]{3,2,1,0:T(8,128)(2,1)} %copy-done.15, ...), custom_call_target="tpu_custom_call", output_to_operand_aliasing={{}: (8, {})} | custom-call | flops 536870912 | bytes 6291456 | tf_op jit(solution)/shard_map/backward/pallas_call | solution.py:304
  (177 shorter events, 48.2 us)
Async XLA Ops:
  2.3 14.2 %collective-permute-start = (bf16[32,16,128]{2,1,0:T(8,128)(2,1)}, bf16[32,16,128]{2,1,0:T(8,128)(2,1)S(1)}, u32[]{:S(2)}, u32[]{:S(2)}) collective-permute-start(bf16[32,16,128]{2,1,0:T(8,128)(2,1)} %get-tuple-element.90), channel_id=1, source_target_pairs={{0,4},{4,0},{8,12},{12,8},{16,20},{20,16},{24,28},{28,24},{1,5},{5... | collective-permute-start | bytes 393224 | tf_op jit(solution)/shard_map/ppermute | solution.py:327
  5.3 14.9 %collective-permute-start.1 = (bf16[32,16,128]{2,1,0:T(8,128)(2,1)}, bf16[32,16,128]{2,1,0:T(8,128)(2,1)S(1)}, u32[]{:S(2)}, u32[]{:S(2)}) collective-permute-start(bf16[32,16,128]{2,1,0:T(8,128)(2,1)} %get-tuple-element.91), channel_id=1, source_target_pairs={{0,8},{4,12},{8,0},{12,4},{16,24},{20,28},{24,16},{28,20},{1,9},{5... | collective-permute-start | bytes 393224 | tf_op jit(solution)/shard_map/ppermute | solution.py:327
  6.9 13.9 %collective-permute-start.2 = (bf16[32,16,128]{2,1,0:T(8,128)(2,1)}, bf16[32,16,128]{2,1,0:T(8,128)(2,1)S(1)}, u32[]{:S(2)}, u32[]{:S(2)}) collective-permute-start(bf16[32,16,128]{2,1,0:T(8,128)(2,1)} %get-tuple-element.92), channel_id=1, source_target_pairs={{0,12},{4,8},{8,4},{12,0},{16,28},{20,24},{24,20},{28,16},{1,13},{... | collective-permute-start | bytes 393224 | tf_op jit(solution)/shard_map/ppermute | solution.py:327
  6.9 13.9 %collective-permute-start.3 = (bf16[32,16,128]{2,1,0:T(8,128)(2,1)}, bf16[32,16,128]{2,1,0:T(8,128)(2,1)S(1)}, u32[]{:S(2)}, u32[]{:S(2)}) collective-permute-start(bf16[32,16,128]{2,1,0:T(8,128)(2,1)} %get-tuple-element.93), channel_id=1, source_target_pairs={{0,16},{4,20},{8,24},{12,28},{16,0},{20,4},{24,8},{28,12},{1,17},{... | collective-permute-start | bytes 393224 | tf_op jit(solution)/shard_map/ppermute | solution.py:327
  9.8 19.7 %collective-permute-start.4 = (bf16[32,16,128]{2,1,0:T(8,128)(2,1)}, bf16[32,16,128]{2,1,0:T(8,128)(2,1)S(1)}, u32[]{:S(2)}, u32[]{:S(2)}) collective-permute-start(bf16[32,16,128]{2,1,0:T(8,128)(2,1)} %get-tuple-element.94), channel_id=1, source_target_pairs={{0,20},{4,16},{8,28},{12,24},{16,4},{20,0},{24,12},{28,8},{1,21},{... | collective-permute-start | bytes 393224 | tf_op jit(solution)/shard_map/ppermute | solution.py:327
  16.5 13.0 %collective-permute-start.5 = (bf16[32,16,128]{2,1,0:T(8,128)(2,1)}, bf16[32,16,128]{2,1,0:T(8,128)(2,1)S(1)}, u32[]{:S(2)}, u32[]{:S(2)}) collective-permute-start(bf16[32,16,128]{2,1,0:T(8,128)(2,1)} %get-tuple-element.95), channel_id=1, source_target_pairs={{0,24},{4,28},{8,16},{12,20},{16,8},{20,12},{24,0},{28,4},{1,25},{... | collective-permute-start | bytes 393224 | tf_op jit(solution)/shard_map/ppermute | solution.py:327
  41.4 16.7 %collective-permute-start.17 = (bf16[32,16,128]{2,1,0:T(8,128)(2,1)}, bf16[32,16,128]{2,1,0:T(8,128)(2,1)S(1)}, u32[]{:S(2)}, u32[]{:S(2)}) collective-permute-start(bf16[32,16,128]{2,1,0:T(8,128)(2,1)} %get-tuple-element.121), channel_id=1, source_target_pairs={{0,16},{4,20},{8,24},{12,28},{16,0},{20,4},{24,8},{28,12},{1,17},{... | collective-permute-start | bytes 393224 | tf_op jit(solution)/shard_map/ppermute | solution.py:327
  44.9 26.2 %collective-permute-start.18 = (bf16[32,16,128]{2,1,0:T(8,128)(2,1)}, bf16[32,16,128]{2,1,0:T(8,128)(2,1)S(1)}, u32[]{:S(2)}, u32[]{:S(2)}) collective-permute-start(bf16[32,16,128]{2,1,0:T(8,128)(2,1)} %get-tuple-element.122), channel_id=1, source_target_pairs={{0,20},{4,16},{8,28},{12,24},{16,4},{20,0},{24,12},{28,8},{1,21},{... | collective-permute-start | bytes 393224 | tf_op jit(solution)/shard_map/ppermute | solution.py:327
  47.1 24.0 %collective-permute-start.19 = (bf16[32,16,128]{2,1,0:T(8,128)(2,1)}, bf16[32,16,128]{2,1,0:T(8,128)(2,1)S(1)}, u32[]{:S(2)}, u32[]{:S(2)}) collective-permute-start(bf16[32,16,128]{2,1,0:T(8,128)(2,1)} %get-tuple-element.123), channel_id=1, source_target_pairs={{0,24},{4,28},{8,16},{12,20},{16,8},{20,12},{24,0},{28,4},{1,25},{... | collective-permute-start | bytes 393224 | tf_op jit(solution)/shard_map/ppermute | solution.py:327
  48.6 24.7 %collective-permute-start.20 = (bf16[32,16,128]{2,1,0:T(8,128)(2,1)}, bf16[32,16,128]{2,1,0:T(8,128)(2,1)S(1)}, u32[]{:S(2)}, u32[]{:S(2)}) collective-permute-start(bf16[32,16,128]{2,1,0:T(8,128)(2,1)} %get-tuple-element.124), channel_id=1, source_target_pairs={{0,28},{4,24},{8,20},{12,16},{16,12},{20,8},{24,4},{28,0},{1,29},{... | collective-permute-start | bytes 393224 | tf_op jit(solution)/shard_map/ppermute | solution.py:327
  52.5 30.7 %collective-permute-start.9 = (bf16[32,16,128]{2,1,0:T(8,128)(2,1)}, bf16[32,16,128]{2,1,0:T(8,128)(2,1)S(1)}, u32[]{:S(2)}, u32[]{:S(2)}) collective-permute-start(bf16[32,16,128]{2,1,0:T(8,128)(2,1)} %get-tuple-element.128), channel_id=1, source_target_pairs={{0,12},{4,8},{8,4},{12,0},{16,28},{20,24},{24,20},{28,16},{1,13},{... | collective-permute-start | bytes 393224 | tf_op jit(solution)/shard_map/ppermute | solution.py:327
  58.1 25.1 %collective-permute-start.10 = (bf16[32,16,128]{2,1,0:T(8,128)(2,1)}, bf16[32,16,128]{2,1,0:T(8,128)(2,1)S(1)}, u32[]{:S(2)}, u32[]{:S(2)}) collective-permute-start(bf16[32,16,128]{2,1,0:T(8,128)(2,1)} %get-tuple-element.129), channel_id=1, source_target_pairs={{0,16},{4,20},{8,24},{12,28},{16,0},{20,4},{24,8},{28,12},{1,17},{... | collective-permute-start | bytes 393224 | tf_op jit(solution)/shard_map/ppermute | solution.py:327
  71.1 15.4 %collective-permute-start.11 = (bf16[32,16,128]{2,1,0:T(8,128)(2,1)}, bf16[32,16,128]{2,1,0:T(8,128)(2,1)S(1)}, u32[]{:S(2)}, u32[]{:S(2)}) collective-permute-start(bf16[32,16,128]{2,1,0:T(8,128)(2,1)} %get-tuple-element.130), channel_id=1, source_target_pairs={{0,20},{4,16},{8,28},{12,24},{16,4},{20,0},{24,12},{28,8},{1,21},{... | collective-permute-start | bytes 393224 | tf_op jit(solution)/shard_map/ppermute | solution.py:327
  71.1 15.4 %collective-permute-start.12 = (bf16[32,16,128]{2,1,0:T(8,128)(2,1)}, bf16[32,16,128]{2,1,0:T(8,128)(2,1)S(1)}, u32[]{:S(2)}, u32[]{:S(2)}) collective-permute-start(bf16[32,16,128]{2,1,0:T(8,128)(2,1)} %get-tuple-element.131), channel_id=1, source_target_pairs={{0,24},{4,28},{8,16},{12,20},{16,8},{20,12},{24,0},{28,4},{1,25},{... | collective-permute-start | bytes 393224 | tf_op jit(solution)/shard_map/ppermute | solution.py:327
  73.3 13.3 %collective-permute-start.13 = (bf16[32,16,128]{2,1,0:T(8,128)(2,1)}, bf16[32,16,128]{2,1,0:T(8,128)(2,1)S(1)}, u32[]{:S(2)}, u32[]{:S(2)}) collective-permute-start(bf16[32,16,128]{2,1,0:T(8,128)(2,1)} %get-tuple-element.132), channel_id=1, source_target_pairs={{0,28},{4,24},{8,20},{12,16},{16,12},{20,8},{24,4},{28,0},{1,29},{... | collective-permute-start | bytes 393224 | tf_op jit(solution)/shard_map/ppermute | solution.py:327
  89.7 53.9 %all-to-all-start = ((bf16[256,16,128]{2,1,0:T(8,128)(2,1)}), bf16[256,16,128]{2,1,0:T(8,128)(2,1)S(1)}, u32[]{:S(2)}, u32[]{:S(2)}) async-start(bf16[256,16,128]{2,1,0:T(8,128)(2,1)} %bitcast.18), calls=%async_computation | async-start | bytes 2097152 | tf_op jit(solution)/shard_map/all_to_all | solution.py:407
  98.4 14.3 %collective-permute-start.24 = (bf16[128,2048]{1,0:T(8,128)(2,1)S(1)}, bf16[128,2048]{1,0:T(8,128)(2,1)}, u32[]{:S(2)}, u32[]{:S(2)}) collective-permute-start(bf16[128,2048]{1,0:T(8,128)(2,1)S(1)} %copy-done.37), channel_id=1, source_target_pairs={{0,3},{1,2},{2,1},{3,0},{4,7},{5,6},{6,5},{7,4},{8,11},{9,10},{10,... | collective-permute-start | bytes 1572872 | tf_op jit(solution)/shard_map/ppermute | solution.py:421
  99.8 22.3 %collective-permute-start.21 = (bf16[32,2,32,128]{3,2,1,0:T(8,128)(2,1)}, bf16[32,2,32,128]{3,2,1,0:T(8,128)(2,1)S(1)}, u32[]{:S(2)}, u32[]{:S(2)}) collective-permute-start(bf16[32,2,32,128]{3,2,1,0:T(8,128)(2,1)} %get-tuple-element.134), channel_id=1, source_target_pairs={{0,1},{1,0},{2,3},{3,2},{4,5},{5,4},{6,7},{7,6},{8,9},{9,8},{10,11... | collective-permute-start | bytes 1572872 | tf_op jit(solution)/shard_map/ppermute | solution.py:327
  101.5 22.4 %collective-permute-start.22 = (bf16[32,2,32,128]{3,2,1,0:T(8,128)(2,1)}, bf16[32,2,32,128]{3,2,1,0:T(8,128)(2,1)S(1)}, u32[]{:S(2)}, u32[]{:S(2)}) collective-permute-start(bf16[32,2,32,128]{3,2,1,0:T(8,128)(2,1)} %get-tuple-element.135), channel_id=1, source_target_pairs={{0,2},{1,3},{2,0},{3,1},{4,6},{5,7},{6,4},{7,5},{8,10},{9,11},{10,... | collective-permute-start | bytes 1572872 | tf_op jit(solution)/shard_map/ppermute | solution.py:327
  102.0 33.1 %collective-permute-start.23 = (bf16[32,2,32,128]{3,2,1,0:T(8,128)(2,1)}, bf16[32,2,32,128]{3,2,1,0:T(8,128)(2,1)S(1)}, u32[]{:S(2)}, u32[]{:S(2)}) collective-permute-start(bf16[32,2,32,128]{3,2,1,0:T(8,128)(2,1)} %get-tuple-element.136), channel_id=1, source_target_pairs={{0,3},{1,2},{2,1},{3,0},{4,7},{5,6},{6,5},{7,4},{8,11},{9,10},{10,... | collective-permute-start | bytes 1572872 | tf_op jit(solution)/shard_map/ppermute | solution.py:327
  148.9 13.4 %collective-permute-start.31 = (bf16[32,2,16,128]{3,2,1,0:T(8,128)(2,1)}, bf16[32,2,16,128]{3,2,1,0:T(8,128)(2,1)S(1)}, u32[]{:S(2)}, u32[]{:S(2)}) collective-permute-start(bf16[32,2,16,128]{3,2,1,0:T(8,128)(2,1)} %get-tuple-element.158), channel_id=1, source_target_pairs={{0,3},{1,2},{2,1},{3,0},{4,7},{5,6},{6,5},{7,4},{8,11},{9,10},{10,... | collective-permute-start | bytes 786440 | tf_op jit(solution)/shard_map/ppermute | solution.py:327
  154.4 14.7 %collective-permute-start.28 = (bf16[32,2,16,128]{3,2,1,0:T(8,128)(2,1)}, bf16[32,2,16,128]{3,2,1,0:T(8,128)(2,1)S(1)}, u32[]{:S(2)}, u32[]{:S(2)}) collective-permute-start(bf16[32,2,16,128]{3,2,1,0:T(8,128)(2,1)} %get-tuple-element.155), channel_id=1, source_target_pairs={{0,2},{1,3},{2,0},{3,1},{4,6},{5,7},{6,4},{7,5},{8,10},{9,11},{10,... | collective-permute-start | bytes 786440 | tf_op jit(solution)/shard_map/ppermute | solution.py:327
  154.9 18.7 %collective-permute-start.30 = (bf16[32,2,16,128]{3,2,1,0:T(8,128)(2,1)}, bf16[32,2,16,128]{3,2,1,0:T(8,128)(2,1)S(1)}, u32[]{:S(2)}, u32[]{:S(2)}) collective-permute-start(bf16[32,2,16,128]{3,2,1,0:T(8,128)(2,1)} %get-tuple-element.157), channel_id=1, source_target_pairs={{0,3},{1,2},{2,1},{3,0},{4,7},{5,6},{6,5},{7,4},{8,11},{9,10},{10,... | collective-permute-start | bytes 786440 | tf_op jit(solution)/shard_map/ppermute | solution.py:327
  157.8 25.6 %collective-permute-start.38 = (bf16[32,2,32,128]{3,2,1,0:T(8,128)(2,1)}, bf16[32,2,32,128]{3,2,1,0:T(8,128)(2,1)S(1)}, u32[]{:S(2)}, u32[]{:S(2)}) collective-permute-start(bf16[32,2,32,128]{3,2,1,0:T(8,128)(2,1)} %get-tuple-element.147), channel_id=1, source_target_pairs={{0,1},{1,0},{2,3},{3,2},{4,5},{5,4},{6,7},{7,6},{8,9},{9,8},{10,11... | collective-permute-start | bytes 1572872 | tf_op jit(solution)/shard_map/ppermute | solution.py:327
  162.3 23.6 %collective-permute-start.39 = (bf16[32,2,32,128]{3,2,1,0:T(8,128)(2,1)}, bf16[32,2,32,128]{3,2,1,0:T(8,128)(2,1)S(1)}, u32[]{:S(2)}, u32[]{:S(2)}) collective-permute-start(bf16[32,2,32,128]{3,2,1,0:T(8,128)(2,1)} %get-tuple-element.148), channel_id=1, source_target_pairs={{0,2},{1,3},{2,0},{3,1},{4,6},{5,7},{6,4},{7,5},{8,10},{9,11},{10,... | collective-permute-start | bytes 1572872 | tf_op jit(solution)/shard_map/ppermute | solution.py:327
  163.1 32.9 %collective-permute-start.40 = (bf16[32,2,32,128]{3,2,1,0:T(8,128)(2,1)}, bf16[32,2,32,128]{3,2,1,0:T(8,128)(2,1)S(1)}, u32[]{:S(2)}, u32[]{:S(2)}) collective-permute-start(bf16[32,2,32,128]{3,2,1,0:T(8,128)(2,1)} %get-tuple-element.149), channel_id=1, source_target_pairs={{0,3},{1,2},{2,1},{3,0},{4,7},{5,6},{6,5},{7,4},{8,11},{9,10},{10,... | collective-permute-start | bytes 1572872 | tf_op jit(solution)/shard_map/ppermute | solution.py:327
  181.9 14.9 %collective-permute-start.35 = (bf16[16,2,32,128]{3,2,1,0:T(8,128)(2,1)}, bf16[16,2,32,128]{3,2,1,0:T(8,128)(2,1)S(1)}, u32[]{:S(2)}, u32[]{:S(2)}) collective-permute-start(bf16[16,2,32,128]{3,2,1,0:T(8,128)(2,1)} %get-tuple-element.164), channel_id=1, source_target_pairs={{0,1},{1,0},{2,3},{3,2},{4,5},{5,4},{6,7},{7,6},{8,9},{9,8},{10,11... | collective-permute-start | bytes 786440 | tf_op jit(solution)/shard_map/ppermute | solution.py:327
  182.9 24.4 %collective-permute-start.36 = (bf16[16,2,32,128]{3,2,1,0:T(8,128)(2,1)}, bf16[16,2,32,128]{3,2,1,0:T(8,128)(2,1)S(1)}, u32[]{:S(2)}, u32[]{:S(2)}) collective-permute-start(bf16[16,2,32,128]{3,2,1,0:T(8,128)(2,1)} %get-tuple-element.165), channel_id=1, source_target_pairs={{0,2},{1,3},{2,0},{3,1},{4,6},{5,7},{6,4},{7,5},{8,10},{9,11},{10,... | collective-permute-start | bytes 786440 | tf_op jit(solution)/shard_map/ppermute | solution.py:327
  183.4 23.9 %collective-permute-start.37 = (bf16[16,2,32,128]{3,2,1,0:T(8,128)(2,1)}, bf16[16,2,32,128]{3,2,1,0:T(8,128)(2,1)S(1)}, u32[]{:S(2)}, u32[]{:S(2)}) collective-permute-start(bf16[16,2,32,128]{3,2,1,0:T(8,128)(2,1)} %get-tuple-element.166), channel_id=1, source_target_pairs={{0,3},{1,2},{2,1},{3,0},{4,7},{5,6},{6,5},{7,4},{8,11},{9,10},{10,... | collective-permute-start | bytes 786440 | tf_op jit(solution)/shard_map/ppermute | solution.py:327
  185.9 27.2 %collective-permute-start.32 = (bf16[16,2,32,128]{3,2,1,0:T(8,128)(2,1)}, bf16[16,2,32,128]{3,2,1,0:T(8,128)(2,1)S(1)}, u32[]{:S(2)}, u32[]{:S(2)}) collective-permute-start(bf16[16,2,32,128]{3,2,1,0:T(8,128)(2,1)} %get-tuple-element.160), channel_id=1, source_target_pairs={{0,1},{1,0},{2,3},{3,2},{4,5},{5,4},{6,7},{7,6},{8,9},{9,8},{10,11... | collective-permute-start | bytes 786440 | tf_op jit(solution)/shard_map/ppermute | solution.py:327
  196.0 18.0 %collective-permute-start.33 = (bf16[16,2,32,128]{3,2,1,0:T(8,128)(2,1)}, bf16[16,2,32,128]{3,2,1,0:T(8,128)(2,1)S(1)}, u32[]{:S(2)}, u32[]{:S(2)}) collective-permute-start(bf16[16,2,32,128]{3,2,1,0:T(8,128)(2,1)} %get-tuple-element.161), channel_id=1, source_target_pairs={{0,2},{1,3},{2,0},{3,1},{4,6},{5,7},{6,4},{7,5},{8,10},{9,11},{10,... | collective-permute-start | bytes 786440 | tf_op jit(solution)/shard_map/ppermute | solution.py:327
  196.8 21.7 %collective-permute-start.34 = (bf16[16,2,32,128]{3,2,1,0:T(8,128)(2,1)}, bf16[16,2,32,128]{3,2,1,0:T(8,128)(2,1)S(1)}, u32[]{:S(2)}, u32[]{:S(2)}) collective-permute-start(bf16[16,2,32,128]{3,2,1,0:T(8,128)(2,1)} %get-tuple-element.162), channel_id=1, source_target_pairs={{0,3},{1,2},{2,1},{3,0},{4,7},{5,6},{6,5},{7,4},{8,11},{9,10},{10,... | collective-permute-start | bytes 786440 | tf_op jit(solution)/shard_map/ppermute | solution.py:327
  (55 other events, 620.8 us)
where the time goes:
time: 225 us; the launch traced here: 224 us
  waiting for transfers between devices  84.9 us (38%)
  Pallas kernels  68.1 us (30%)
  starting transfers between devices  58.2 us (26%)
  local copies, waits for them, and re-layouts  10.1 us (4%)
    ppermute x39, waiting for transfers between devices, shift(): lax.ppermute(value, axis, [(i, i ^ mask) for i in range(size)])  75.9 us
    ppermute x39, starting transfers between devices, shift(): lax.ppermute(value, axis, [(i, i ^ mask) for i in range(size)])  49.5 us
    pallas_call x3, Pallas kernels, backward(): pl.pallas_call(functools.partial(backward_kernel, groups, has_total, part...  16.4 us
    pallas_call x2, Pallas kernels, middle(): pl.pallas_call(functools.partial(middle_kernel, groups, halves), out_shap...  15.4 us
    pallas_call x3, Pallas kernels, forward(): pl.pallas_call(functools.partial(forward_kernel, parts, half * count), gr...  15 us
    pallas_call x1, Pallas kernels, expand(): pl.pallas_call(functools.partial(expand_kernel, scale, groups, rows * len...  9.45 us
    ppermute x1, waiting for transfers between devices, local(): neg = lax.ppermute(mirrored, 'grid', mirror_of)  8.93 us
    all_to_all x1, starting transfers between devices, exchange(): lax.all_to_all(value, 'band', split_axis=0, concat_axis=0, tiled=True)  6.71 us
  transfers between devices with their start and end apart: 42, of which 16 were waited for; matrix products, arithmetic and copies ran while one was open for 3% of the time, Pallas kernels for 23%

commit v1 on v0

--- a/solution.py
+++ b/solution.py
@@ -138,7 +138,7 @@
     )(me, kernel, neg, first, cols)
 
 
-def forward_kernel(parts, base, me_ref, grid_ref, own_ref, *refs):
+def forward_kernel(parts, base, cuts, me_ref, grid_ref, own_ref, *refs):
     piece_refs = refs[:parts]
     if parts > 1:
         zt_ref, yt_ref, their_ref = refs[parts : parts + 3]
@@ -176,22 +176,23 @@
 
     lax.fori_loop(0, count // 2, step, 0, unroll=min(UNROLL, count // 2))
     part = ny // len(out_refs)
-    for slot, out_ref in enumerate(out_refs):
-        begin = (grid_ref[0] ^ slot) * (part * count)
+    for number, out_ref in enumerate(out_refs):
+        owner = grid_ref[0] ^ (number // cuts)
+        begin = (owner * cuts + number % cuts) * (part * count)
         for c in range(2):
             piece = hold[c, pl.ds(begin, part * count), :]
             out_ref[:, c] = piece.astype(BF16).reshape(part, count, nz)
 
 
-def forward(me, grid_pos, own, pieces, half, count, zt, yt, groups):
+def forward(me, grid_pos, own, pieces, half, count, zt, yt, groups, cuts):
     ny, nz = own.shape[2:]
-    part = ny // groups
+    part = ny // (groups * cuts)
     parts = len(pieces)
     shape = jax.ShapeDtypeStruct((part, 2, count, nz), BF16)
     their = jax.ShapeDtypeStruct((parts * pieces[0].shape[0],) + pieces[0].shape[1:], BF16)
-    outs = ([their] if parts > 1 else []) + [shape] * groups
-    return pl.pallas_call(
-        functools.partial(forward_kernel, parts, half * count),
+    outs = ([their] if parts > 1 else []) + [shape] * (groups * cuts)
+    return pl.pallas_call(
+        functools.partial(forward_kernel, parts, half * count, cuts),
         grid=(1,),
         out_shape=outs,
         in_specs=[SCALARS, SCALARS, spec((2, count, ny, nz), lambda i: (0, half, 0, 0))]
@@ -205,9 +206,9 @@
 
 
 def middle_kernel(groups, halves, grid_ref, *refs):
-    in_refs = refs[: groups * halves]
-    kern_ref, xt_ref, ixt_ref = refs[groups * halves : groups * halves + 3]
-    out_refs, hold = refs[groups * halves + 3 : -1], refs[-1]
+    in_refs = refs[:groups]
+    kern_ref, xt_ref, ixt_ref = refs[groups : groups + 3]
+    out_refs, hold = refs[groups + 3 : -1], refs[-1]
     count, nx, nz = kern_ref.shape
     xt, ixt = xt_ref[...], ixt_ref[...]
 
@@ -240,26 +241,29 @@
             out_ref[:, c] = piece.astype(BF16).reshape(rows, count, nz)
 
 
-def middle(grid_pos, pieces, kern, xt, ixt, groups, halves):
-    count, nx, nz = kern.shape
+def middle(grid_pos, pieces, kern, cut, xt, ixt, halves):
+    groups = len(pieces)
+    count, nx, nz = pieces[0].shape[0], kern.shape[1], kern.shape[2]
     rows = nx // (groups * halves)
     shape = jax.ShapeDtypeStruct((rows, 2, count, nz), BF16)
-    vmem = pl.BlockSpec(memory_space=pltpu.VMEM)
     return pl.pallas_call(
         functools.partial(middle_kernel, groups, halves),
+        grid=(1,),
         out_shape=[shape] * (groups * halves),
-        in_specs=[SCALARS] + [vmem] * (groups * halves + 3),
-        out_specs=[vmem] * (groups * halves),
+        in_specs=[SCALARS]
+        + [spec(p.shape) for p in pieces]
+        + [spec((count, nx, nz), lambda i: (cut, 0, 0)), spec(xt.shape), spec(ixt.shape)],
+        out_specs=[spec(shape.shape)] * (groups * halves),
         scratch_shapes=[pltpu.VMEM((2, nx * count, nz), F32)],
         cost_estimate=cost(16 * nx * nx * count * nz, 12 * count * nx * nz),
         name="middle",
     )(grid_pos, *pieces, kern, xt, ixt)
 
 
-def backward_kernel(groups, has_total, base, *refs):
-    in_refs = refs[:groups]
-    their_ref, weight_ref, yt_ref, zt_ref = refs[groups : groups + 4]
-    total_ref = refs[groups + 4] if has_total == 2 else None
+def backward_kernel(bases, has_total, base, *refs):
+    in_refs = refs[: len(bases)]
+    their_ref, weight_ref, yt_ref, zt_ref = refs[len(bases) : len(bases) + 4]
+    total_ref = refs[len(bases) + 4] if has_total == 2 else None
     out_ref = refs[-1]
     count, ny, nz = out_ref.shape[1:]
     tiles = ny // their_ref.shape[1]
@@ -270,7 +274,7 @@
         lines = []
         for k in range(2):
             x = 2 * pair + k
-            lines.append(jnp.concatenate([r[x, c] for c in range(2) for r in in_refs], 0))
+            lines.append(jnp.concatenate([r[x + b, c] for c in range(2) for r, b in zip(in_refs, bases)], 0))
         fourth = dot(yt, jnp.concatenate(lines, 1)).astype(BF16)
         stack = jnp.concatenate(
             [
@@ -294,28 +298,27 @@
     lax.fori_loop(0, count // 2, step, 0, unroll=min(UNROLL, count // 2))
 
 
-def backward(pieces, their, weight, yt, zt, total, accumulate, part_number, slab):
-    groups = len(pieces)
-    count, ny, nz = pieces[0].shape[0], pieces[0].shape[2] * groups, pieces[0].shape[3]
+def backward(pieces, bases, their, weight, yt, zt, total, accumulate, part_number, count, slab):
+    ny, nz = sum(p.shape[2] for p in pieces), pieces[0].shape[3]
+    number = len(pieces)
     block = spec((2, count, ny, nz), lambda i: (0, part_number, 0, 0))
     has_total = 0 if total is None else (2 if accumulate else 1)
     extra = [] if total is None else [total]
     extra_specs = [] if total is None else [block if accumulate else pl.BlockSpec(memory_space=pl.ANY)]
     return pl.pallas_call(
-        functools.partial(backward_kernel, groups, has_total, part_number * count),
+        functools.partial(backward_kernel, bases, has_total, part_number * count),
         grid=(1,),
         out_shape=jax.ShapeDtypeStruct((2, slab, ny, nz), F32),
         in_specs=[spec(p.shape) for p in pieces]
-        + [spec(their.shape), pl.BlockSpec(memory_space=pltpu.SMEM), spec(yt.shape), spec(zt.shape)]
+        + [spec(their.shape), SCALARS, spec(yt.shape), spec(zt.shape)]
         + extra_specs,
         out_specs=block,
-        input_output_aliases={groups + 4: 0} if extra else {},
+        input_output_aliases={number + 4: 0} if extra else {},
         cost_estimate=cost(2 * count * ny * nz * 2 * (2 * ny + 2 * nz), 24 * count * ny * nz),
         name="backward",
     )(*pieces, their, weight, yt, zt, *extra)
 
 
-HALVES = (1, 2)
 TILE = 16
 
 
@@ -431,41 +434,62 @@
     yleft, yright = block_tables(ny)
     zleft, zright = block_tables(nz)
     x_forward, y_inverse = slots(xleft, 1), slots(yright, 1)
-    theirs, answers, counts = [], [], []
-    for m in range(2):
-        halves = HALVES[m] if slab % (16 * HALVES[m]) == 0 else 1
-        rows = slab // halves
-        if m == 0:
-            picked = pick(choice, after(arrived, mirrored, first_line, *sent1))
-            fetched = slotwise(picked)
-            kern = expand(
-                my_grid, after(kernel, *picked), neg, first, cols, groups, ny, nz, 0.5 / (nx * ny * nz)
-            )
-            arrived = slotwise(after(sent1, *picked))
-            their, *sent = forward(my_band, my_grid, orbitals, fetched, 0, rows, zright, yleft, groups)
-        else:
-            picked = pick_stacked(pick_choice, after(arrived, *sent))
-            their = exchange(picked.reshape(tiled.shape[1:]))
-            their = after(their, *answers[0])
-            sent = forward(my_band, my_grid, orbitals, [their], 0, rows, zright, yleft, groups)
-        pieces = [[swap(value, slot)] for slot, value in enumerate(sent)]
-        for h in range(1, halves):
-            more = forward(my_band, my_grid, orbitals, [their], h, rows, zright, yleft, groups)
-            for slot, value in enumerate(more):
-                pieces[slot].append(swap(value, slot))
-        flat = [piece for per_slot in pieces for piece in per_slot]
-        answers.append(middle(my_grid, flat, kern, x_forward, xright, groups, halves))
-        theirs.append(their)
-        counts.append(halves)
-
-    total = None
-    for m in range(2):
-        weight = lax.dynamic_slice_in_dim(occupation, partner[band_pos] * 2 + m, 1, 0)
-        for h in range(counts[m]):
-            back = [swap(answers[m][slot * counts[m] + h], slot) for slot in range(groups)]
-            if m == 0:
-                back = after(back, *answers[1])
-            total = backward(back, theirs[m], weight, y_inverse, zleft, total, m > 0, h, slab)
+    cuts = 2 if lines % 32 == 0 else 1
+    parts = 2 if slab % 32 == 0 else 1
+
+    picked = pick(choice, after(arrived, mirrored, first_line, *sent1))
+    fetched = slotwise(picked)
+    arrived = slotwise(after(sent1, *picked))
+
+    def outward(pieces):
+        outs = forward(my_band, my_grid, orbitals, pieces, 0, slab, zright, yleft, groups, cuts)
+        their, sent = (outs[0], outs[1:]) if len(pieces) > 1 else (pieces[0], outs)
+        moved = [
+            [swap(sent[slot * cuts + cut], slot) for slot in range(groups)]
+            for cut in range(cuts)
+        ]
+        return their, sent, moved
+
+    their0, sent, moved0 = outward(fetched)
+    picked = pick_stacked(pick_choice, after(arrived, *sent))
+    their1 = exchange(picked.reshape(tiled.shape[1:]))
+    kern = expand(
+        my_grid, after(kernel, picked), neg, first, cols, groups, ny, nz, 0.5 / (nx * ny * nz)
+    )
+
+    def inward(moved, halves):
+        answers, back = [], []
+        for cut in range(cuts):
+            answers.append(middle(my_grid, moved[cut], kern, cut, x_forward, xright, halves[cut]))
+            back.append([
+                swap(value, number // halves[cut])
+                for number, value in enumerate(answers[cut])
+            ])
+        split_rows = max(halves)
+        result = []
+        for h in range(split_rows):
+            pieces, bases = [], []
+            for slot in range(groups):
+                for cut in range(cuts):
+                    whole = halves[cut] == 1
+                    pieces.append(back[cut][slot if whole else slot * halves[cut] + h])
+                    bases.append(h * (slab // split_rows) if whole else 0)
+            result.append((pieces, bases))
+        return answers, result
+
+    answers0, back0 = inward(moved0, (1,) * cuts)
+    their1, _, moved1 = outward([after(their1, *answers0[-1])])
+    _, back1 = inward(moved1, (1,) * (cuts - 1) + (parts,))
+
+    def weight(m):
+        return lax.dynamic_slice_in_dim(occupation, partner[band_pos] * 2 + m, 1, 0)
+
+    pieces, bases = back0[0]
+    total = backward(pieces, bases, their0, weight(0), y_inverse, zleft, None, False, 0, slab, slab)
+    for h, (pieces, bases) in enumerate(back1):
+        total = backward(
+            pieces, bases, their1, weight(1), y_inverse, zleft, total, True, h, slab // len(back1), slab
+        )
     return total
 
 

time: 225 us -> 223 us (level)
  waiting for transfers between devices: 84.9 us -> 76.6 us
  starting transfers between devices: 58.2 us -> 64.1 us
    ppermute x39 -> x48, waiting for transfers between devices: 75.9 us -> 68.3 us  [shift(): lax.ppermute(value, axis, [(i, i ^ mask) for i in range(size)])]
    ppermute x39 -> x48, starting transfers between devices: 49.5 us -> 56.4 us  [shift(): lax.ppermute(value, axis, [(i, i ^ mask) for i in range(size)])]
    pallas_call x8 -> x9, Pallas kernels: 46.9 us -> 47 us  [the longest x3 17.1 us: backward(): pl.pallas_call(functools.partial(backward_kernel, bases, has_total, part_...]
    unnamed x90 -> x114, local copies, waits for them, and re-layouts: 5.44 us -> 5.51 us
  transfers between devices with their start and end apart: 42 -> 51, of which waited for: 16 -> 17; matrix products, arithmetic and copies ran while one was open for 3% -> 3% of each run, Pallas kernels for 23% -> 25%
where the time goes in v1:
time: 223 us; the launch traced here: 222 us
  waiting for transfers between devices  76.6 us (34%)
  Pallas kernels  68 us (30%)
  starting transfers between devices  64.1 us (29%)
  local copies, waits for them, and re-layouts  10.2 us (5%)
    ppermute x48, waiting for transfers between devices, shift(): lax.ppermute(value, axis, [(i, i ^ mask) for i in range(size)])  68.3 us
    ppermute x48, starting transfers between devices, shift(): lax.ppermute(value, axis, [(i, i ^ mask) for i in range(size)])  56.4 us
    pallas_call x3, Pallas kernels, backward(): pl.pallas_call(functools.partial(backward_kernel, bases, has_total, part_...  17.1 us
    pallas_call x4, Pallas kernels, middle(): pl.pallas_call(functools.partial(middle_kernel, groups, halves), grid=(1,...  15 us
    pallas_call x2, Pallas kernels, forward(): pl.pallas_call(functools.partial(forward_kernel, parts, half * count, cut...  14.8 us
    pallas_call x1, Pallas kernels, expand(): pl.pallas_call(functools.partial(expand_kernel, scale, groups, rows * len...  9.27 us
    ppermute x1, waiting for transfers between devices, local(): neg = lax.ppermute(mirrored, 'grid', mirror_of)  8.28 us
    all_to_all x1, starting transfers between devices, exchange(): lax.all_to_all(value, 'band', split_axis=0, concat_axis=0, tiled=True)  6.73 us
  transfers between devices with their start and end apart: 51, of which 17 were waited for; matrix products, arithmetic and copies ran while one was open for 3% of the time, Pallas kernels for 25%

profile of v1, /device:TPU:0, one launch (start us, length us, event | category | flops | bytes accessed | tf_op | source)
XLA Modules:
  0.0 222.1 jit_solution(396683283161329711)
XLA Ops:
  0.0 2.3 %split.2 = (bf16[32,16,128]{2,1,0:T(8,128)(2,1)}, bf16[32,16,128]{2,1,0:T(8,128)(2,1)}, bf16[32,16,128]{2,1,0:T(8,128)(2,1)}, bf16[32,16,128]{2,1,0:T(8,128)(2,1...) custom-call(s32[1]{0:T(128)} %bitcast.1.me_ref, ...), custom_call_target="tpu_custom_call" | custom-call | bytes 2097152 | tf_op jit(solution)/shard_map/split/pallas_call | solution.py:341
  2.3 3.0 %collective-permute-start = (bf16[32,16,128]{2,1,0:T(8,128)(2,1)}, bf16[32,16,128]{2,1,0:T(8,128)(2,1)S(1)}, u32[]{:S(2)}, u32[]{:S(2)}) collective-permute-start(bf16[32,16,128]{2,1,0:T(8,128)(2,1)} %get-tuple-element.98), channel_id=1, source_target_pairs={{0,4},{4,0},{8,12},{12,8},{16,20},{20,16},{24,28},{28,24},{1,5},{5... | collective-permute-start | bytes 393224 | tf_op jit(solution)/shard_map/ppermute | solution.py:330
  6.9 3.0 %collective-permute-start.3 = (bf16[32,16,128]{2,1,0:T(8,128)(2,1)}, bf16[32,16,128]{2,1,0:T(8,128)(2,1)S(1)}, u32[]{:S(2)}, u32[]{:S(2)}) collective-permute-start(bf16[32,16,128]{2,1,0:T(8,128)(2,1)} %get-tuple-element.101), channel_id=1, source_target_pairs={{0,16},{4,20},{8,24},{12,28},{16,0},{20,4},{24,8},{28,12},{1,17},{... | collective-permute-start | bytes 393224 | tf_op jit(solution)/shard_map/ppermute | solution.py:330
  14.1 2.4 %mirror.1 = (bf16[128,2048]{1,0:T(8,128)(2,1)}, bf16[128,128]{1,0:T(8,128)(2,1)}) custom-call(s32[1]{0:T(128)} %bitcast.me_ref.grid_ref, f32[128,2048]{1,0:T(8,128)} %own_ref.3, s32[1,8192]{1,0:T(1,128)} %bitcast.23), custom_call_target="tpu_custom_call" | custom-call | flops 67108864 | bytes 1572864 | tf_op jit(solution)/shard_map/mirror/pallas_call | solution.py:85
  16.5 3.7 %collective-permute-start.5 = (bf16[32,16,128]{2,1,0:T(8,128)(2,1)}, bf16[32,16,128]{2,1,0:T(8,128)(2,1)S(1)}, u32[]{:S(2)}, u32[]{:S(2)}) collective-permute-start(bf16[32,16,128]{2,1,0:T(8,128)(2,1)} %get-tuple-element.103), channel_id=1, source_target_pairs={{0,24},{4,28},{8,16},{12,20},{16,8},{20,12},{24,0},{28,4},{1,25},{... | collective-permute-start | bytes 393224 | tf_op jit(solution)/shard_map/ppermute | solution.py:330
  20.8 8.7 %collective-permute-done.4.refs_5_ = bf16[32,16,128]{2,1,0:T(8,128)(2,1)S(1)} collective-permute-done((bf16[32,16,128]{2,1,0:T(8,128)(2,1)}, bf16[32,16,128]{2,1,0:T(8,128)(2,1)S(1)}, u32[]{:S(2)}, u32[]{:S(2)}) %collective-permute-start.4) | collective-permute-done | bytes 131104 | tf_op jit(solution)/shard_map/ppermute | solution.py:330
  30.3 2.4 %pick.2 = (bf16[32,16,128]{2,1,0:T(8,128)(2,1)}, bf16[32,16,128]{2,1,0:T(8,128)(2,1)}, bf16[32,16,128]{2,1,0:T(8,128)(2,1)}, bf16[32,16,128]{2,1,0:T(8,128)(2,1)...) custom-call(s32[8]{0:T(128)} %get-tuple-element.194.choice_ref, ...), custom_call_target="tpu_custom_call" | custom-call | bytes 2097152 | tf_op jit(solution)/shard_map/pick/pallas_call | solution.py:362
  32.6 5.3 %collective-permute-start.8 = (bf16[32,16,128]{2,1,0:T(8,128)(2,1)}, bf16[32,16,128]{2,1,0:T(8,128)(2,1)S(1)}, u32[]{:S(2)}, u32[]{:S(2)}) collective-permute-start(bf16[32,16,128]{2,1,0:T(8,128)(2,1)} %get-tuple-element.135), channel_id=1, source_target_pairs={{0,8},{4,12},{8,0},{12,4},{16,24},{20,28},{24,16},{28,20},{1,9},{5... | collective-permute-start | bytes 393224 | tf_op jit(solution)/shard_map/ppermute | solution.py:330
  41.5 3.4 %collective-permute-start.17 = (bf16[32,16,128]{2,1,0:T(8,128)(2,1)}, bf16[32,16,128]{2,1,0:T(8,128)(2,1)S(1)}, u32[]{:S(2)}, u32[]{:S(2)}) collective-permute-start(bf16[32,16,128]{2,1,0:T(8,128)(2,1)} %get-tuple-element.129), channel_id=1, source_target_pairs={{0,16},{4,20},{8,24},{12,28},{16,0},{20,4},{24,8},{28,12},{1,17},{... | collective-permute-start | bytes 393224 | tf_op jit(solution)/shard_map/ppermute | solution.py:330
  48.6 3.4 %collective-permute-start.20 = (bf16[32,16,128]{2,1,0:T(8,128)(2,1)}, bf16[32,16,128]{2,1,0:T(8,128)(2,1)S(1)}, u32[]{:S(2)}, u32[]{:S(2)}) collective-permute-start(bf16[32,16,128]{2,1,0:T(8,128)(2,1)} %get-tuple-element.132), channel_id=1, source_target_pairs={{0,28},{4,24},{8,20},{12,16},{16,12},{20,8},{24,4},{28,0},{1,29},{... | collective-permute-start | bytes 393224 | tf_op jit(solution)/shard_map/ppermute | solution.py:330
  52.7 5.5 %collective-permute-done.17.refs_4_ = bf16[32,16,128]{2,1,0:T(8,128)(2,1)S(1)} collective-permute-done((bf16[32,16,128]{2,1,0:T(8,128)(2,1)}, bf16[32,16,128]{2,1,0:T(8,128)(2,1)S(1)}, u32[]{:S(2)}, u32[]{:S(2)}) %collective-permute-start.17) | collective-permute-done | bytes 131104 | tf_op jit(solution)/shard_map/ppermute | solution.py:330
  58.2 13.0 %collective-permute-done.18.refs_5_ = bf16[32,16,128]{2,1,0:T(8,128)(2,1)S(1)} collective-permute-done((bf16[32,16,128]{2,1,0:T(8,128)(2,1)}, bf16[32,16,128]{2,1,0:T(8,128)(2,1)S(1)}, u32[]{:S(2)}, u32[]{:S(2)}) %collective-permute-start.18) | collective-permute-done | bytes 131104 | tf_op jit(solution)/shard_map/ppermute | solution.py:330
  75.8 7.5 %forward.2 = (bf16[256,16,128]{2,1,0:T(8,128)(2,1)}, bf16[16,2,32,128]{3,2,1,0:T(8,128)(2,1)}, bf16[16,2,32,128]{3,2,1,0:T(8,128)(2,1)}, bf16[16,2,32,128]{3,2,1...) custom-call(s32[1]{0:T(128)} %bitcast.1.me_ref, ...), custom_call_target="tpu_custom_call" | custom-call | flops 1073741824 | bytes 6291456 | tf_op jit(solution)/shard_map/forward/pallas_call | solution.py:194
  83.3 3.2 %collective-permute-done.11.refs_5_ = bf16[32,16,128]{2,1,0:T(8,128)(2,1)S(1)} collective-permute-done((bf16[32,16,128]{2,1,0:T(8,128)(2,1)}, bf16[32,16,128]{2,1,0:T(8,128)(2,1)S(1)}, u32[]{:S(2)}, u32[]{:S(2)}) %collective-permute-start.11) | collective-permute-done | bytes 131104 | tf_op jit(solution)/shard_map/ppermute | solution.py:330
  87.3 2.4 %pick.3 = bf16[8,32,16,128]{3,2,1,0:T(8,128)(2,1)} custom-call(s32[8]{0:T(128)} %get-tuple-element.195.choice_ref, bf16[32,16,128]{2,1,0:T(8,128)(2,1)} %get-tuple-element.149.refs_0_, bf16[32,16,128]{2,1,0:T(8,128)(2,1)} %copy-done.31, bf16[32,16,128]{2,1,0:T(8,128)(2,1)} %copy-done.32, bf16[32,16,128]{2,1,0:T(8,128)(2,1)} %copy-done.33, ...), custom_call_target="tpu_custom_call" | custom-call | bytes 2097152 | tf_op jit(solution)/shard_map/pick/pallas_call | solution.py:383
  89.7 6.7 %all-to-all-start = ((bf16[256,16,128]{2,1,0:T(8,128)(2,1)}), bf16[256,16,128]{2,1,0:T(8,128)(2,1)S(1)}, u32[]{:S(2)}, u32[]{:S(2)}) async-start(bf16[256,16,128]{2,1,0:T(8,128)(2,1)} %bitcast.18), calls=%async_computation | async-start | bytes 2097152 | tf_op jit(solution)/shard_map/all_to_all | solution.py:410
  103.3 8.3 %collective-permute-done.24.neg_ref = bf16[128,2048]{1,0:T(8,128)(2,1)S(1)} collective-permute-done((bf16[128,2048]{1,0:T(8,128)(2,1)S(1)}, bf16[128,2048]{1,0:T(8,128)(2,1)S(1)}, u32[]{:S(2)}, u32[]{:S(2)}) %collective-permute-start.24) | collective-permute-done | bytes 524320 | tf_op jit(solution)/shard_map/ppermute | solution.py:424
  112.4 9.3 %expand.1.refs_4_ = f32[32,128,128]{2,1,0:T(8,128)} custom-call(s32[1]{0:T(128)} %bitcast.me_ref.grid_ref, f32[128,2048]{1,0:T(8,128)} %own_ref.3, bf16[128,2048]{1,0:T(8,128)(2,1)} %copy-done.47, bf16[128,128]{1,0:T(8,128)(2,1)} %copy-done.56, s32[1,8192]{1,0:T(1,128)} %bitcast.24), custom_call_target="tpu_custom_call" | custom-call | flops 4294967296 | bytes 3145728 | tf_op jit(solution)/shard_map/expand/pallas_call | solution.py:130
  122.9 5.5 %collective-permute-done.23.refs_3_ = bf16[16,2,32,128]{3,2,1,0:T(8,128)(2,1)S(1)} collective-permute-done((bf16[16,2,32,128]{3,2,1,0:T(8,128)(2,1)}, bf16[16,2,32,128]{3,2,1,0:T(8,128)(2,1)S(1)}, u32[]{:S(2)}, u32[]{:S(2)}) %collective-permute-start.23) | collective-permute-done | bytes 262176 | tf_op jit(solution)/shard_map/ppermute | solution.py:330
  129.1 3.7 %middle.4 = (bf16[32,2,16,128]{3,2,1,0:T(8,128)(2,1)}, bf16[32,2,16,128]{3,2,1,0:T(8,128)(2,1)}, bf16[32,2,16,128]{3,2,1,0:T(8,128)(2,1)}, bf16[32,2,16,128]{3,2,1,0:T(8,128)(2,1)}) custom-call(s32[1]{0:T(128)} %bitcast.me_ref.grid_ref, bf16[16,2,32,128]{3,2,1,0:T(8,128)(2,1)} %get-tuple-element.142.refs_0_, bf16[16,2,32,128]{3,2,1,0:T(8,128)(2,1)} %copy-done.22, ...), custom_call_target="tpu_custom_call" | custom-call | flops 536870912 | bytes 3145728 | tf_op jit(solution)/shard_map/middle/pallas_call | solution.py:249
  135.3 7.3 %forward.3 = (bf16[16,2,32,128]{3,2,1,0:T(8,128)(2,1)}, bf16[16,2,32,128]{3,2,1,0:T(8,128)(2,1)}, bf16[16,2,32,128]{3,2,1,0:T(8,128)(2,1)}, bf16[16,2,32,128]{3,...) custom-call(s32[1]{0:T(128)} %bitcast.1.me_ref, ...), custom_call_target="tpu_custom_call" | custom-call | flops 1073741824 | bytes 6291456 | tf_op jit(solution)/shard_map/forward/pallas_call | solution.py:194
  146.8 5.5 %collective-permute-done.27.refs_2_ = bf16[16,2,32,128]{3,2,1,0:T(8,128)(2,1)S(1)} collective-permute-done((bf16[16,2,32,128]{3,2,1,0:T(8,128)(2,1)}, bf16[16,2,32,128]{3,2,1,0:T(8,128)(2,1)S(1)}, u32[]{:S(2)}, u32[]{:S(2)}) %collective-permute-start.27) | collective-permute-done | bytes 262176 | tf_op jit(solution)/shard_map/ppermute | solution.py:330
  152.4 3.8 %middle.7 = (bf16[32,2,16,128]{3,2,1,0:T(8,128)(2,1)}, bf16[32,2,16,128]{3,2,1,0:T(8,128)(2,1)}, bf16[32,2,16,128]{3,2,1,0:T(8,128)(2,1)}, bf16[32,2,16,128]{3,2,1,0:T(8,128)(2,1)}) custom-call(s32[1]{0:T(128)} %bitcast.me_ref.grid_ref, bf16[16,2,32,128]{3,2,1,0:T(8,128)(2,1)} %get-tuple-element.141.refs_0_, bf16[16,2,32,128]{3,2,1,0:T(8,128)(2,1)} %copy-done.13, ...), custom_call_target="tpu_custom_call" | custom-call | flops 536870912 | bytes 3145728 | tf_op jit(solution)/shard_map/middle/pallas_call | solution.py:249
  158.5 3.7 %collective-permute-done.31.refs_3_ = bf16[16,2,32,128]{3,2,1,0:T(8,128)(2,1)S(1)} collective-permute-done((bf16[16,2,32,128]{3,2,1,0:T(8,128)(2,1)}, bf16[16,2,32,128]{3,2,1,0:T(8,128)(2,1)S(1)}, u32[]{:S(2)}, u32[]{:S(2)}) %collective-permute-start.31) | collective-permute-done | bytes 262176 | tf_op jit(solution)/shard_map/ppermute | solution.py:330
  163.9 3.8 %middle.6 = (bf16[16,2,16,128]{3,2,1,0:T(8,128)(2,1)}, bf16[16,2,16,128]{3,2,1,0:T(8,128)(2,1)}, bf16[16,2,16,128]{3,2,1,0:T(8,128)(2,1)}, bf16[16,2,16,128]{3,2...) custom-call(s32[1]{0:T(128)} %bitcast.me_ref.grid_ref, ...), custom_call_target="tpu_custom_call" | custom-call | flops 536870912 | bytes 3145728 | tf_op jit(solution)/shard_map/middle/pallas_call | solution.py:249
  169.3 3.7 %middle.5 = (bf16[32,2,16,128]{3,2,1,0:T(8,128)(2,1)}, bf16[32,2,16,128]{3,2,1,0:T(8,128)(2,1)}, bf16[32,2,16,128]{3,2,1,0:T(8,128)(2,1)}, bf16[32,2,16,128]{3,2,1,0:T(8,128)(2,1)}) custom-call(s32[1]{0:T(128)} %bitcast.me_ref.grid_ref, bf16[16,2,32,128]{3,2,1,0:T(8,128)(2,1)} %get-tuple-element.163.refs_0_, bf16[16,2,32,128]{3,2,1,0:T(8,128)(2,1)} %copy-done.15, ...), custom_call_target="tpu_custom_call" | custom-call | flops 536870912 | bytes 3145728 | tf_op jit(solution)/shard_map/middle/pallas_call | solution.py:249
  175.2 5.2 %collective-permute-done.46.refs_4_ = bf16[32,2,16,128]{3,2,1,0:T(8,128)(2,1)S(1)} collective-permute-done((bf16[32,2,16,128]{3,2,1,0:T(8,128)(2,1)}, bf16[32,2,16,128]{3,2,1,0:T(8,128)(2,1)S(1)}, u32[]{:S(2)}, u32[]{:S(2)}) %collective-permute-start.46) | collective-permute-done | bytes 262176 | tf_op jit(solution)/shard_map/ppermute | solution.py:330
  180.4 4.2 %collective-permute-done.48.refs_6_ = bf16[32,2,16,128]{3,2,1,0:T(8,128)(2,1)S(1)} collective-permute-done((bf16[32,2,16,128]{3,2,1,0:T(8,128)(2,1)}, bf16[32,2,16,128]{3,2,1,0:T(8,128)(2,1)S(1)}, u32[]{:S(2)}, u32[]{:S(2)}) %collective-permute-start.48) | collective-permute-done | bytes 262176 | tf_op jit(solution)/shard_map/ppermute | solution.py:330
  189.9 10.2 %collective-permute-done.39.refs_5_ = bf16[16,2,16,128]{3,2,1,0:T(8,128)(2,1)S(1)} collective-permute-done((bf16[16,2,16,128]{3,2,1,0:T(8,128)(2,1)}, bf16[16,2,16,128]{3,2,1,0:T(8,128)(2,1)S(1)}, u32[]{:S(2)}, u32[]{:S(2)}) %collective-permute-start.39) | collective-permute-done | bytes 131104 | tf_op jit(solution)/shard_map/ppermute | solution.py:330
  203.4 6.3 %backward.3.refs_12_ = f32[2,32,128,128]{3,2,1,0:T(8,128)} custom-call(bf16[32,2,16,128]{3,2,1,0:T(8,128)(2,1)} %get-tuple-element.183.refs_0_, bf16[32,2,16,128]{3,2,1,0:T(8,128)(2,1)} %get-tuple-element.158.refs_1_, bf16[32,2,16,128]{3,2,1,0:T(8,128)(2,1)} %copy-done.10, bf16[32,2,16,128]{3,2,1,0:T(8,128)(2,1)} %copy-done.7, ...), custom_call_target="tpu_custom_call" | custom-call | flops 1073741824 | bytes 12582912 | tf_op jit(solution)/shard_map/backward/pallas_call | solution.py:308
  210.6 5.4 %backward.4.refs_12_ = f32[2,32,128,128]{3,2,1,0:T(8,128)} custom-call(bf16[32,2,16,128]{3,2,1,0:T(8,128)(2,1)} %get-tuple-element.167.refs_0_, bf16[16,2,16,128]{3,2,1,0:T(8,128)(2,1)} %get-tuple-element.179.refs_1_, bf16[32,2,16,128]{3,2,1,0:T(8,128)(2,1)} %copy-done.4, bf16[16,2,16,128]{3,2,1,0:T(8,128)(2,1)} %copy-done.25, ...), custom_call_target="tpu_custom_call", output_to_operand_aliasing={{}: (12, {})} | custom-call | flops 536870912 | bytes 6291456 | tf_op jit(solution)/shard_map/backward/pallas_call | solution.py:308
  216.7 5.4 %backward.5 = f32[2,32,128,128]{3,2,1,0:T(8,128)} custom-call(bf16[32,2,16,128]{3,2,1,0:T(8,128)(2,1)} %get-tuple-element.167.refs_0_, bf16[16,2,16,128]{3,2,1,0:T(8,128)(2,1)} %get-tuple-element.172.refs_1_, bf16[32,2,16,128]{3,2,1,0:T(8,128)(2,1)} %copy-done.4, bf16[16,2,16,128]{3,2,1,0:T(8,128)(2,1)} %copy-done.28, ...), custom_call_target="tpu_custom_call", output_to_operand_aliasing={{}: (12, {})} | custom-call | flops 536870912 | bytes 6291456 | tf_op jit(solution)/shard_map/backward/pallas_call | solution.py:308
  (220 shorter events, 53.7 us)
Async XLA Ops:
  5.3 14.9 %collective-permute-start.1 = (bf16[32,16,128]{2,1,0:T(8,128)(2,1)}, bf16[32,16,128]{2,1,0:T(8,128)(2,1)S(1)}, u32[]{:S(2)}, u32[]{:S(2)}) collective-permute-start(bf16[32,16,128]{2,1,0:T(8,128)(2,1)} %get-tuple-element.99), channel_id=1, source_target_pairs={{0,8},{4,12},{8,0},{12,4},{16,24},{20,28},{24,16},{28,20},{1,9},{5... | collective-permute-start | bytes 393224 | tf_op jit(solution)/shard_map/ppermute | solution.py:330
  9.8 19.7 %collective-permute-start.4 = (bf16[32,16,128]{2,1,0:T(8,128)(2,1)}, bf16[32,16,128]{2,1,0:T(8,128)(2,1)S(1)}, u32[]{:S(2)}, u32[]{:S(2)}) collective-permute-start(bf16[32,16,128]{2,1,0:T(8,128)(2,1)} %get-tuple-element.102), channel_id=1, source_target_pairs={{0,20},{4,16},{8,28},{12,24},{16,4},{20,0},{24,12},{28,8},{1,21},{... | collective-permute-start | bytes 393224 | tf_op jit(solution)/shard_map/ppermute | solution.py:330
  41.5 16.7 %collective-permute-start.17 = (bf16[32,16,128]{2,1,0:T(8,128)(2,1)}, bf16[32,16,128]{2,1,0:T(8,128)(2,1)S(1)}, u32[]{:S(2)}, u32[]{:S(2)}) collective-permute-start(bf16[32,16,128]{2,1,0:T(8,128)(2,1)} %get-tuple-element.129), channel_id=1, source_target_pairs={{0,16},{4,20},{8,24},{12,28},{16,0},{20,4},{24,8},{28,12},{1,17},{... | collective-permute-start | bytes 393224 | tf_op jit(solution)/shard_map/ppermute | solution.py:330
  44.9 26.2 %collective-permute-start.18 = (bf16[32,16,128]{2,1,0:T(8,128)(2,1)}, bf16[32,16,128]{2,1,0:T(8,128)(2,1)S(1)}, u32[]{:S(2)}, u32[]{:S(2)}) collective-permute-start(bf16[32,16,128]{2,1,0:T(8,128)(2,1)} %get-tuple-element.130), channel_id=1, source_target_pairs={{0,20},{4,16},{8,28},{12,24},{16,4},{20,0},{24,12},{28,8},{1,21},{... | collective-permute-start | bytes 393224 | tf_op jit(solution)/shard_map/ppermute | solution.py:330
  47.1 24.0 %collective-permute-start.19 = (bf16[32,16,128]{2,1,0:T(8,128)(2,1)}, bf16[32,16,128]{2,1,0:T(8,128)(2,1)S(1)}, u32[]{:S(2)}, u32[]{:S(2)}) collective-permute-start(bf16[32,16,128]{2,1,0:T(8,128)(2,1)} %get-tuple-element.131), channel_id=1, source_target_pairs={{0,24},{4,28},{8,16},{12,20},{16,8},{20,12},{24,0},{28,4},{1,25},{... | collective-permute-start | bytes 393224 | tf_op jit(solution)/shard_map/ppermute | solution.py:330
  48.6 24.7 %collective-permute-start.20 = (bf16[32,16,128]{2,1,0:T(8,128)(2,1)}, bf16[32,16,128]{2,1,0:T(8,128)(2,1)S(1)}, u32[]{:S(2)}, u32[]{:S(2)}) collective-permute-start(bf16[32,16,128]{2,1,0:T(8,128)(2,1)} %get-tuple-element.132), channel_id=1, source_target_pairs={{0,28},{4,24},{8,20},{12,16},{16,12},{20,8},{24,4},{28,0},{1,29},{... | collective-permute-start | bytes 393224 | tf_op jit(solution)/shard_map/ppermute | solution.py:330
  52.6 30.7 %collective-permute-start.9 = (bf16[32,16,128]{2,1,0:T(8,128)(2,1)}, bf16[32,16,128]{2,1,0:T(8,128)(2,1)S(1)}, u32[]{:S(2)}, u32[]{:S(2)}) collective-permute-start(bf16[32,16,128]{2,1,0:T(8,128)(2,1)} %get-tuple-element.136), channel_id=1, source_target_pairs={{0,12},{4,8},{8,4},{12,0},{16,28},{20,24},{24,20},{28,16},{1,13},{... | collective-permute-start | bytes 393224 | tf_op jit(solution)/shard_map/ppermute | solution.py:330
  58.2 25.2 %collective-permute-start.10 = (bf16[32,16,128]{2,1,0:T(8,128)(2,1)}, bf16[32,16,128]{2,1,0:T(8,128)(2,1)S(1)}, u32[]{:S(2)}, u32[]{:S(2)}) collective-permute-start(bf16[32,16,128]{2,1,0:T(8,128)(2,1)} %get-tuple-element.137), channel_id=1, source_target_pairs={{0,16},{4,20},{8,24},{12,28},{16,0},{20,4},{24,8},{28,12},{1,17},{... | collective-permute-start | bytes 393224 | tf_op jit(solution)/shard_map/ppermute | solution.py:330
  71.1 15.4 %collective-permute-start.11 = (bf16[32,16,128]{2,1,0:T(8,128)(2,1)}, bf16[32,16,128]{2,1,0:T(8,128)(2,1)S(1)}, u32[]{:S(2)}, u32[]{:S(2)}) collective-permute-start(bf16[32,16,128]{2,1,0:T(8,128)(2,1)} %get-tuple-element.138), channel_id=1, source_target_pairs={{0,20},{4,16},{8,28},{12,24},{16,4},{20,0},{24,12},{28,8},{1,21},{... | collective-permute-start | bytes 393224 | tf_op jit(solution)/shard_map/ppermute | solution.py:330
  71.1 15.4 %collective-permute-start.12 = (bf16[32,16,128]{2,1,0:T(8,128)(2,1)}, bf16[32,16,128]{2,1,0:T(8,128)(2,1)S(1)}, u32[]{:S(2)}, u32[]{:S(2)}) collective-permute-start(bf16[32,16,128]{2,1,0:T(8,128)(2,1)} %get-tuple-element.139), channel_id=1, source_target_pairs={{0,24},{4,28},{8,16},{12,20},{16,8},{20,12},{24,0},{28,4},{1,25},{... | collective-permute-start | bytes 393224 | tf_op jit(solution)/shard_map/ppermute | solution.py:330
  89.7 44.6 %all-to-all-start = ((bf16[256,16,128]{2,1,0:T(8,128)(2,1)}), bf16[256,16,128]{2,1,0:T(8,128)(2,1)S(1)}, u32[]{:S(2)}, u32[]{:S(2)}) async-start(bf16[256,16,128]{2,1,0:T(8,128)(2,1)} %bitcast.18), calls=%async_computation | async-start | bytes 2097152 | tf_op jit(solution)/shard_map/all_to_all | solution.py:410
  99.7 43.0 %collective-permute-start.41 = (bf16[16,2,32,128]{3,2,1,0:T(8,128)(2,1)}, bf16[16,2,32,128]{3,2,1,0:T(8,128)(2,1)S(1)}, u32[]{:S(2)}, u32[]{:S(2)}) collective-permute-start(bf16[16,2,32,128]{3,2,1,0:T(8,128)(2,1)} %get-tuple-element.143), channel_id=1, source_target_pairs={{0,1},{1,0},{2,3},{3,2},{4,5},{5,4},{6,7},{7,6},{8,9},{9,8},{10,11... | collective-permute-start | bytes 786440 | tf_op jit(solution)/shard_map/ppermute | solution.py:330
  101.2 20.4 %collective-permute-start.21 = (bf16[16,2,32,128]{3,2,1,0:T(8,128)(2,1)}, bf16[16,2,32,128]{3,2,1,0:T(8,128)(2,1)S(1)}, u32[]{:S(2)}, u32[]{:S(2)}) collective-permute-start(bf16[16,2,32,128]{3,2,1,0:T(8,128)(2,1)} %get-tuple-element.144), channel_id=1, source_target_pairs={{0,1},{1,0},{2,3},{3,2},{4,5},{5,4},{6,7},{7,6},{8,9},{9,8},{10,11... | collective-permute-start | bytes 786440 | tf_op jit(solution)/shard_map/ppermute | solution.py:330
  101.2 41.7 %collective-permute-start.42 = (bf16[16,2,32,128]{3,2,1,0:T(8,128)(2,1)}, bf16[16,2,32,128]{3,2,1,0:T(8,128)(2,1)S(1)}, u32[]{:S(2)}, u32[]{:S(2)}) collective-permute-start(bf16[16,2,32,128]{3,2,1,0:T(8,128)(2,1)} %get-tuple-element.145), channel_id=1, source_target_pairs={{0,2},{1,3},{2,0},{3,1},{4,6},{5,7},{6,4},{7,5},{8,10},{9,11},{10,... | collective-permute-start | bytes 786440 | tf_op jit(solution)/shard_map/ppermute | solution.py:330
  101.8 21.1 %collective-permute-start.22 = (bf16[16,2,32,128]{3,2,1,0:T(8,128)(2,1)}, bf16[16,2,32,128]{3,2,1,0:T(8,128)(2,1)S(1)}, u32[]{:S(2)}, u32[]{:S(2)}) collective-permute-start(bf16[16,2,32,128]{3,2,1,0:T(8,128)(2,1)} %get-tuple-element.146), channel_id=1, source_target_pairs={{0,2},{1,3},{2,0},{3,1},{4,6},{5,7},{6,4},{7,5},{8,10},{9,11},{10,... | collective-permute-start | bytes 786440 | tf_op jit(solution)/shard_map/ppermute | solution.py:330
  111.6 16.9 %collective-permute-start.23 = (bf16[16,2,32,128]{3,2,1,0:T(8,128)(2,1)}, bf16[16,2,32,128]{3,2,1,0:T(8,128)(2,1)S(1)}, u32[]{:S(2)}, u32[]{:S(2)}) collective-permute-start(bf16[16,2,32,128]{3,2,1,0:T(8,128)(2,1)} %get-tuple-element.148), channel_id=1, source_target_pairs={{0,3},{1,2},{2,1},{3,0},{4,7},{5,6},{6,5},{7,4},{8,11},{9,10},{10,... | collective-permute-start | bytes 786440 | tf_op jit(solution)/shard_map/ppermute | solution.py:330
  121.6 21.9 %collective-permute-start.43 = (bf16[16,2,32,128]{3,2,1,0:T(8,128)(2,1)}, bf16[16,2,32,128]{3,2,1,0:T(8,128)(2,1)S(1)}, u32[]{:S(2)}, u32[]{:S(2)}) collective-permute-start(bf16[16,2,32,128]{3,2,1,0:T(8,128)(2,1)} %get-tuple-element.147), channel_id=1, source_target_pairs={{0,3},{1,2},{2,1},{3,0},{4,7},{5,6},{6,5},{7,4},{8,11},{9,10},{10,... | collective-permute-start | bytes 786440 | tf_op jit(solution)/shard_map/ppermute | solution.py:330
  143.7 14.3 %collective-permute-start.30 = (bf16[16,2,32,128]{3,2,1,0:T(8,128)(2,1)}, bf16[16,2,32,128]{3,2,1,0:T(8,128)(2,1)S(1)}, u32[]{:S(2)}, u32[]{:S(2)}) collective-permute-start(bf16[16,2,32,128]{3,2,1,0:T(8,128)(2,1)} %get-tuple-element.170), channel_id=1, source_target_pairs={{0,2},{1,3},{2,0},{3,1},{4,6},{5,7},{6,4},{7,5},{8,10},{9,11},{10,... | collective-permute-start | bytes 786440 | tf_op jit(solution)/shard_map/ppermute | solution.py:330
  145.1 17.1 %collective-permute-start.31 = (bf16[16,2,32,128]{3,2,1,0:T(8,128)(2,1)}, bf16[16,2,32,128]{3,2,1,0:T(8,128)(2,1)S(1)}, u32[]{:S(2)}, u32[]{:S(2)}) collective-permute-start(bf16[16,2,32,128]{3,2,1,0:T(8,128)(2,1)} %get-tuple-element.171), channel_id=1, source_target_pairs={{0,3},{1,2},{2,1},{3,0},{4,7},{5,6},{6,5},{7,4},{8,11},{9,10},{10,... | collective-permute-start | bytes 786440 | tf_op jit(solution)/shard_map/ppermute | solution.py:330
  145.4 22.4 %collective-permute-start.28 = (bf16[16,2,32,128]{3,2,1,0:T(8,128)(2,1)}, bf16[16,2,32,128]{3,2,1,0:T(8,128)(2,1)S(1)}, u32[]{:S(2)}, u32[]{:S(2)}) collective-permute-start(bf16[16,2,32,128]{3,2,1,0:T(8,128)(2,1)} %get-tuple-element.166), channel_id=1, source_target_pairs={{0,3},{1,2},{2,1},{3,0},{4,7},{5,6},{6,5},{7,4},{8,11},{9,10},{10,... | collective-permute-start | bytes 786440 | tf_op jit(solution)/shard_map/ppermute | solution.py:330
  152.4 21.1 %collective-permute-start.49 = (bf16[32,2,16,128]{3,2,1,0:T(8,128)(2,1)}, bf16[32,2,16,128]{3,2,1,0:T(8,128)(2,1)S(1)}, u32[]{:S(2)}, u32[]{:S(2)}) collective-permute-start(bf16[32,2,16,128]{3,2,1,0:T(8,128)(2,1)} %get-tuple-element.161), channel_id=1, source_target_pairs={{0,3},{1,2},{2,1},{3,0},{4,7},{5,6},{6,5},{7,4},{8,11},{9,10},{10,... | collective-permute-start | bytes 786440 | tf_op jit(solution)/shard_map/ppermute | solution.py:330
  156.2 18.4 %collective-permute-start.44 = (bf16[32,2,16,128]{3,2,1,0:T(8,128)(2,1)}, bf16[32,2,16,128]{3,2,1,0:T(8,128)(2,1)S(1)}, u32[]{:S(2)}, u32[]{:S(2)}) collective-permute-start(bf16[32,2,16,128]{3,2,1,0:T(8,128)(2,1)} %get-tuple-element.184), channel_id=1, source_target_pairs={{0,1},{1,0},{2,3},{3,2},{4,5},{5,4},{6,7},{7,6},{8,9},{9,8},{10,11... | collective-permute-start | bytes 786440 | tf_op jit(solution)/shard_map/ppermute | solution.py:330
  158.0 22.5 %collective-permute-start.46 = (bf16[32,2,16,128]{3,2,1,0:T(8,128)(2,1)}, bf16[32,2,16,128]{3,2,1,0:T(8,128)(2,1)S(1)}, u32[]{:S(2)}, u32[]{:S(2)}) collective-permute-start(bf16[32,2,16,128]{3,2,1,0:T(8,128)(2,1)} %get-tuple-element.185), channel_id=1, source_target_pairs={{0,2},{1,3},{2,0},{3,1},{4,6},{5,7},{6,4},{7,5},{8,10},{9,11},{10,... | collective-permute-start | bytes 786440 | tf_op jit(solution)/shard_map/ppermute | solution.py:330
  162.2 22.5 %collective-permute-start.48 = (bf16[32,2,16,128]{3,2,1,0:T(8,128)(2,1)}, bf16[32,2,16,128]{3,2,1,0:T(8,128)(2,1)S(1)}, u32[]{:S(2)}, u32[]{:S(2)}) collective-permute-start(bf16[32,2,16,128]{3,2,1,0:T(8,128)(2,1)} %get-tuple-element.186), channel_id=1, source_target_pairs={{0,3},{1,2},{2,1},{3,0},{4,7},{5,6},{6,5},{7,4},{8,11},{9,10},{10,... | collective-permute-start | bytes 786440 | tf_op jit(solution)/shard_map/ppermute | solution.py:330
  167.8 17.9 %collective-permute-start.38 = (bf16[16,2,16,128]{3,2,1,0:T(8,128)(2,1)}, bf16[16,2,16,128]{3,2,1,0:T(8,128)(2,1)S(1)}, u32[]{:S(2)}, u32[]{:S(2)}) collective-permute-start(bf16[16,2,16,128]{3,2,1,0:T(8,128)(2,1)} %get-tuple-element.180), channel_id=1, source_target_pairs={{0,1},{1,0},{2,3},{3,2},{4,5},{5,4},{6,7},{7,6},{8,9},{9,8},{10,11... | collective-permute-start | bytes 393224 | tf_op jit(solution)/shard_map/ppermute | solution.py:330
  173.4 28.9 %collective-permute-start.32 = (bf16[32,2,16,128]{3,2,1,0:T(8,128)(2,1)}, bf16[32,2,16,128]{3,2,1,0:T(8,128)(2,1)S(1)}, u32[]{:S(2)}, u32[]{:S(2)}) collective-permute-start(bf16[32,2,16,128]{3,2,1,0:T(8,128)(2,1)} %get-tuple-element.173), channel_id=1, source_target_pairs={{0,1},{1,0},{2,3},{3,2},{4,5},{5,4},{6,7},{7,6},{8,9},{9,8},{10,11... | collective-permute-start | bytes 786440 | tf_op jit(solution)/shard_map/ppermute | solution.py:330
  174.6 35.1 %collective-permute-start.34 = (bf16[32,2,16,128]{3,2,1,0:T(8,128)(2,1)}, bf16[32,2,16,128]{3,2,1,0:T(8,128)(2,1)S(1)}, u32[]{:S(2)}, u32[]{:S(2)}) collective-permute-start(bf16[32,2,16,128]{3,2,1,0:T(8,128)(2,1)} %get-tuple-element.175), channel_id=1, source_target_pairs={{0,2},{1,3},{2,0},{3,1},{4,6},{5,7},{6,4},{7,5},{8,10},{9,11},{10,... | collective-permute-start | bytes 786440 | tf_op jit(solution)/shard_map/ppermute | solution.py:330
  180.4 29.3 %collective-permute-start.36 = (bf16[32,2,16,128]{3,2,1,0:T(8,128)(2,1)}, bf16[32,2,16,128]{3,2,1,0:T(8,128)(2,1)S(1)}, u32[]{:S(2)}, u32[]{:S(2)}) collective-permute-start(bf16[32,2,16,128]{3,2,1,0:T(8,128)(2,1)} %get-tuple-element.177), channel_id=1, source_target_pairs={{0,3},{1,2},{2,1},{3,0},{4,7},{5,6},{6,5},{7,4},{8,11},{9,10},{10,... | collective-permute-start | bytes 786440 | tf_op jit(solution)/shard_map/ppermute | solution.py:330
  184.7 15.4 %collective-permute-start.39 = (bf16[16,2,16,128]{3,2,1,0:T(8,128)(2,1)}, bf16[16,2,16,128]{3,2,1,0:T(8,128)(2,1)S(1)}, u32[]{:S(2)}, u32[]{:S(2)}) collective-permute-start(bf16[16,2,16,128]{3,2,1,0:T(8,128)(2,1)} %get-tuple-element.181), channel_id=1, source_target_pairs={{0,2},{1,3},{2,0},{3,1},{4,6},{5,7},{6,4},{7,5},{8,10},{9,11},{10,... | collective-permute-start | bytes 393224 | tf_op jit(solution)/shard_map/ppermute | solution.py:330
  185.7 15.8 %collective-permute-start.40 = (bf16[16,2,16,128]{3,2,1,0:T(8,128)(2,1)}, bf16[16,2,16,128]{3,2,1,0:T(8,128)(2,1)S(1)}, u32[]{:S(2)}, u32[]{:S(2)}) collective-permute-start(bf16[16,2,16,128]{3,2,1,0:T(8,128)(2,1)} %get-tuple-element.182), channel_id=1, source_target_pairs={{0,3},{1,2},{2,1},{3,0},{4,7},{5,6},{6,5},{7,4},{8,11},{9,10},{10,... | collective-permute-start | bytes 393224 | tf_op jit(solution)/shard_map/ppermute | solution.py:330
  200.1 15.8 %collective-permute-start.33 = (bf16[16,2,16,128]{3,2,1,0:T(8,128)(2,1)}, bf16[16,2,16,128]{3,2,1,0:T(8,128)(2,1)S(1)}, u32[]{:S(2)}, u32[]{:S(2)}) collective-permute-start(bf16[16,2,16,128]{3,2,1,0:T(8,128)(2,1)} %get-tuple-element.174), channel_id=1, source_target_pairs={{0,1},{1,0},{2,3},{3,2},{4,5},{5,4},{6,7},{7,6},{8,9},{9,8},{10,11... | collective-permute-start | bytes 393224 | tf_op jit(solution)/shard_map/ppermute | solution.py:330
  201.5 14.4 %collective-permute-start.35 = (bf16[16,2,16,128]{3,2,1,0:T(8,128)(2,1)}, bf16[16,2,16,128]{3,2,1,0:T(8,128)(2,1)S(1)}, u32[]{:S(2)}, u32[]{:S(2)}) collective-permute-start(bf16[16,2,16,128]{3,2,1,0:T(8,128)(2,1)} %get-tuple-element.176), channel_id=1, source_target_pairs={{0,2},{1,3},{2,0},{3,1},{4,6},{5,7},{6,4},{7,5},{8,10},{9,11},{10,... | collective-permute-start | bytes 393224 | tf_op jit(solution)/shard_map/ppermute | solution.py:330
  (76 other events, 911.4 us)

commit v2 on v1

--- a/solution.py
+++ b/solution.py
@@ -414,7 +414,10 @@
 
     my_grid = me.astype(jnp.int32).reshape(1)
     cols = col_index.reshape(1, -1)
-    sent = split(my_band, tiled, 0, 0, slab * ny // TILE, bands)
+    blocks = tiled[0].reshape(bands, -1, TILE, nz)
+    sent = [
+        lax.dynamic_index_in_dim(blocks, band_pos ^ slot, 0, keepdims=False) for slot in range(bands)
+    ]
     arrived = slotwise(sent)
     sent1 = split(my_band, after(tiled, *sent), 1, 0, slab * ny // TILE, bands)
 
@@ -439,57 +442,54 @@
 
     picked = pick(choice, after(arrived, mirrored, first_line, *sent1))
     fetched = slotwise(picked)
-    arrived = slotwise(after(sent1, *picked))
+    kern = expand(
+        my_grid, after(kernel, *picked), neg, first, cols, groups, ny, nz, 0.5 / (nx * ny * nz)
+    )
+    arrived = slotwise(after(sent1, kern))
 
     def outward(pieces):
         outs = forward(my_band, my_grid, orbitals, pieces, 0, slab, zright, yleft, groups, cuts)
         their, sent = (outs[0], outs[1:]) if len(pieces) > 1 else (pieces[0], outs)
-        moved = [
-            [swap(sent[slot * cuts + cut], slot) for slot in range(groups)]
-            for cut in range(cuts)
-        ]
+        moved = [[swap(sent[slot * cuts + cut], slot) for slot in range(groups)] for cut in range(cuts)]
         return their, sent, moved
 
     their0, sent, moved0 = outward(fetched)
     picked = pick_stacked(pick_choice, after(arrived, *sent))
     their1 = exchange(picked.reshape(tiled.shape[1:]))
-    kern = expand(
-        my_grid, after(kernel, picked), neg, first, cols, groups, ny, nz, 0.5 / (nx * ny * nz)
-    )
-
-    def inward(moved, halves):
-        answers, back = [], []
-        for cut in range(cuts):
-            answers.append(middle(my_grid, moved[cut], kern, cut, x_forward, xright, halves[cut]))
-            back.append([
-                swap(value, number // halves[cut])
-                for number, value in enumerate(answers[cut])
-            ])
-        split_rows = max(halves)
-        result = []
-        for h in range(split_rows):
-            pieces, bases = [], []
-            for slot in range(groups):
-                for cut in range(cuts):
-                    whole = halves[cut] == 1
-                    pieces.append(back[cut][slot if whole else slot * halves[cut] + h])
-                    bases.append(h * (slab // split_rows) if whole else 0)
-            result.append((pieces, bases))
-        return answers, result
-
-    answers0, back0 = inward(moved0, (1,) * cuts)
-    their1, _, moved1 = outward([after(their1, *answers0[-1])])
-    _, back1 = inward(moved1, (1,) * (cuts - 1) + (parts,))
-
-    def weight(m):
-        return lax.dynamic_slice_in_dim(occupation, partner[band_pos] * 2 + m, 1, 0)
-
-    pieces, bases = back0[0]
-    total = backward(pieces, bases, their0, weight(0), y_inverse, zleft, None, False, 0, slab, slab)
-    for h, (pieces, bases) in enumerate(back1):
-        total = backward(
-            pieces, bases, their1, weight(1), y_inverse, zleft, total, True, h, slab // len(back1), slab
+
+    def centre(cut, moved, halves):
+        return middle(my_grid, moved[cut], kern, cut, x_forward, xright, halves)
+
+    def home(values):
+        return [swap(value, slot) for slot, value in enumerate(values)]
+
+    def ending(m, total, back, bases, h, count, their):
+        weight = lax.dynamic_slice_in_dim(occupation, partner[band_pos] * 2 + m, 1, 0)
+        pieces = [piece for by_cut in zip(*back) for piece in by_cut]
+        return backward(
+            pieces, bases * groups, their, weight, y_inverse, zleft, total, m > 0, h, count, slab
         )
+
+    answers = [centre(cut, moved0, 1) for cut in range(cuts)]
+    back0 = [home(answers[cut]) for cut in range(cuts)]
+    their1, _, moved1 = outward([after(their1, *answers[-1])])
+
+    last = cuts - 1
+    answers = [centre(cut, moved1, parts if cut == last else 1) for cut in range(cuts)]
+    early = [home(answers[cut]) for cut in range(last)]
+    rows = slab // parts
+    late = [answers[last][h::parts] for h in range(parts)]
+    late[0] = home(late[0])
+    total = None
+    for h in range(parts):
+        if h == parts - 1:
+            back0[0] = after(back0[0], *answers[last])
+        total = ending(0, total, back0, (h * rows,) * cuts, h, rows, their0)
+    for h in range(1, parts):
+        late[h] = home(after(late[h], total))
+    for h in range(parts):
+        bases = (h * rows,) * last + (0,)
+        total = ending(1, total, early + [late[h]], bases, h, rows, their1)
     return total
 
 

time: 223 us -> 214 us (0.960)
  waiting for transfers between devices: 76.6 us -> 41.5 us
  starting transfers between devices: 64.1 us -> 86.9 us
  local copies, waits for them, and re-layouts: 10.2 us -> 13.4 us
    ppermute x48, waiting for transfers between devices: 68.3 us -> 41.5 us  [shift(): lax.ppermute(value, axis, [(i, i ^ mask) for i in range(size)])]
    ppermute x48, starting transfers between devices: 56.4 us -> 75.9 us  [shift(): lax.ppermute(value, axis, [(i, i ^ mask) for i in range(size)])]
    ppermute x1, waiting for transfers between devices: 8.28 us -> 0.01 us  [local(): neg = lax.ppermute(mirrored, 'grid', mirror_of)]
    pallas_call x3 -> x4, Pallas kernels: 17.1 us -> 20.2 us  [backward(): pl.pallas_call(functools.partial(backward_kernel, bases, has_total, part_...]
    ppermute x1, starting transfers between devices: 0.07 us -> 2.41 us  [local(): neg = lax.ppermute(mirrored, 'grid', mirror_of)]
    pallas_call x2 -> x1, Pallas kernels: 4.57 us -> 2.3 us  [split(): pl.pallas_call(split_kernel, grid=(1,), out_shape=[shape] * parts, in_spe...]
    unnamed x114 -> x140, local copies, waits for them, and re-layouts: 5.51 us -> 6.48 us
  transfers between devices with their start and end apart: 51 -> 51, of which waited for: 17 -> 17; matrix products, arithmetic and copies ran while one was open for 3% -> 3% of each run, Pallas kernels for 25% -> 27%
where the time goes in v2:
time: 214 us
  starting transfers between devices  86.9 us (41%)
  Pallas kernels  68.9 us (32%)
  waiting for transfers between devices  41.5 us (19%)
  local copies, waits for them, and re-layouts  13.4 us (6%)
    ppermute x48, starting transfers between devices, shift(): lax.ppermute(value, axis, [(i, i ^ mask) for i in range(size)])  75.9 us
    ppermute x48, waiting for transfers between devices, shift(): lax.ppermute(value, axis, [(i, i ^ mask) for i in range(size)])  41.5 us
    pallas_call x4, Pallas kernels, backward(): pl.pallas_call(functools.partial(backward_kernel, bases, has_total, part_...  20.2 us
    pallas_call x2, Pallas kernels, forward(): pl.pallas_call(functools.partial(forward_kernel, parts, half * count, cut...  15 us
    pallas_call x4, Pallas kernels, middle(): pl.pallas_call(functools.partial(middle_kernel, groups, halves), grid=(1,...  14.9 us
    pallas_call x1, Pallas kernels, expand(): pl.pallas_call(functools.partial(expand_kernel, scale, groups, rows * len...  9.28 us
    all_to_all x1, starting transfers between devices, exchange(): lax.all_to_all(value, 'band', split_axis=0, concat_axis=0, tiled=True)  7.14 us
    unnamed x140, local copies, waits for them, and re-layouts  6.48 us
  transfers between devices with their start and end apart: 51, of which 17 were waited for; matrix products, arithmetic and copies ran while one was open for 3% of the time, Pallas kernels for 27%

profile of v2, /device:TPU:0, one launch (start us, length us, event | category | flops | bytes accessed | tf_op | source)
XLA Modules:
  0.0 213.8 jit_solution(2417932215430327577)
XLA Ops:
  2.2 2.4 %mirror.1 = (bf16[128,2048]{1,0:T(8,128)(2,1)}, bf16[128,128]{1,0:T(8,128)(2,1)}) custom-call(s32[1]{0:T(128)} %bitcast.me_ref.grid_ref, f32[128,2048]{1,0:T(8,128)} %own_ref.2, s32[1,8192]{1,0:T(1,128)} %bitcast.40), custom_call_target="tpu_custom_call" | custom-call | flops 67108864 | bytes 1572864 | tf_op jit(solution)/shard_map/mirror/pallas_call | solution.py:85
  4.6 2.4 %collective-permute-start.7 = (bf16[128,2048]{1,0:T(8,128)(2,1)}, bf16[128,2048]{1,0:T(8,128)(2,1)S(1)}, u32[]{:S(2)}, u32[]{:S(2)}) collective-permute-start(bf16[128,2048]{1,0:T(8,128)(2,1)} %get-tuple-element.107), channel_id=1, source_target_pairs={{0,3},{1,2},{2,1},{3,0},{4,7},{5,6},{6,5},{7,4},{8,11},{9,10},{10,... | collective-permute-start | bytes 1572872 | tf_op jit(solution)/shard_map/ppermute | solution.py:427
  7.0 4.6 %collective-permute-start.6 = (bf16[32,16,128]{2,1,0:T(8,128)(2,1)S(1)}, bf16[32,16,128]{2,1,0:T(8,128)(2,1)S(1)}, u32[]{:S(2)}, u32[]{:S(2)}) collective-permute-start(bf16[32,16,128]{2,1,0:T(8,128)(2,1)S(1)} %get-tuple-element.188), channel_id=1, source_target_pairs={{0,28},{4,24},{8,20},{12,16},{16,12},{20,8},{24,4},{28,0},{1,29},{... | collective-permute-start | bytes 393224 | tf_op jit(solution)/shard_map/ppermute | solution.py:330
  16.0 12.0 %collective-permute-start.2 = (bf16[32,16,128]{2,1,0:T(8,128)(2,1)S(1)}, bf16[32,16,128]{2,1,0:T(8,128)(2,1)S(1)}, u32[]{:S(2)}, u32[]{:S(2)}) collective-permute-start(bf16[32,16,128]{2,1,0:T(8,128)(2,1)S(1)} %get-tuple-element.192), channel_id=1, source_target_pairs={{0,12},{4,8},{8,4},{12,0},{16,28},{20,24},{24,20},{28,16},{1,13},{... | collective-permute-start | bytes 393224 | tf_op jit(solution)/shard_map/ppermute | solution.py:330
  43.3 2.4 %collective-permute-start.18 = (bf16[32,16,128]{2,1,0:T(8,128)(2,1)}, bf16[32,16,128]{2,1,0:T(8,128)(2,1)S(1)}, u32[]{:S(2)}, u32[]{:S(2)}) collective-permute-start(bf16[32,16,128]{2,1,0:T(8,128)(2,1)} %get-tuple-element.120), channel_id=1, source_target_pairs={{0,12},{4,8},{8,4},{12,0},{16,28},{20,24},{24,20},{28,16},{1,13},{... | collective-permute-start | bytes 393224 | tf_op jit(solution)/shard_map/ppermute | solution.py:330
  46.9 2.5 %collective-permute-start.20 = (bf16[32,16,128]{2,1,0:T(8,128)(2,1)}, bf16[32,16,128]{2,1,0:T(8,128)(2,1)S(1)}, u32[]{:S(2)}, u32[]{:S(2)}) collective-permute-start(bf16[32,16,128]{2,1,0:T(8,128)(2,1)} %get-tuple-element.122), channel_id=1, source_target_pairs={{0,20},{4,16},{8,28},{12,24},{16,4},{20,0},{24,12},{28,8},{1,21},{... | collective-permute-start | bytes 393224 | tf_op jit(solution)/shard_map/ppermute | solution.py:330
  49.3 9.3 %expand.1.refs_4_ = f32[32,128,128]{2,1,0:T(8,128)} custom-call(s32[1]{0:T(128)} %bitcast.me_ref.grid_ref, f32[128,2048]{1,0:T(8,128)} %own_ref.2, bf16[128,2048]{1,0:T(8,128)(2,1)} %copy-done.46, bf16[128,128]{1,0:T(8,128)(2,1)} %copy-done.69, s32[1,8192]{1,0:T(1,128)} %bitcast.41), custom_call_target="tpu_custom_call" | custom-call | flops 4294967296 | bytes 3145728 | tf_op jit(solution)/shard_map/expand/pallas_call | solution.py:130
  58.6 2.5 %collective-permute-start.21 = (bf16[32,16,128]{2,1,0:T(8,128)(2,1)S(1)}, bf16[32,16,128]{2,1,0:T(8,128)(2,1)S(1)}, u32[]{:S(2)}, u32[]{:S(2)}) collective-permute-start(bf16[32,16,128]{2,1,0:T(8,128)(2,1)S(1)} %copy-done.67), channel_id=1, source_target_pairs={{0,24},{4,28},{8,16},{12,20},{16,8},{20,12},{24,0},{28,4},{1,25},{... | collective-permute-start | bytes 393224 | tf_op jit(solution)/shard_map/ppermute | solution.py:330
  64.8 2.4 %collective-permute-start.11 = (bf16[32,16,128]{2,1,0:T(8,128)(2,1)S(1)}, bf16[32,16,128]{2,1,0:T(8,128)(2,1)S(1)}, u32[]{:S(2)}, u32[]{:S(2)}) collective-permute-start(bf16[32,16,128]{2,1,0:T(8,128)(2,1)S(1)} %copy-done.54), channel_id=1, source_target_pairs={{0,12},{4,8},{8,4},{12,0},{16,28},{20,24},{24,20},{28,16},{1,13},{... | collective-permute-start | bytes 393224 | tf_op jit(solution)/shard_map/ppermute | solution.py:330
  67.2 4.4 %collective-permute-start.12 = (bf16[32,16,128]{2,1,0:T(8,128)(2,1)S(1)}, bf16[32,16,128]{2,1,0:T(8,128)(2,1)S(1)}, u32[]{:S(2)}, u32[]{:S(2)}) collective-permute-start(bf16[32,16,128]{2,1,0:T(8,128)(2,1)S(1)} %copy-done.53), channel_id=1, source_target_pairs={{0,16},{4,20},{8,24},{12,28},{16,0},{20,4},{24,8},{28,12},{1,17},{... | collective-permute-start | bytes 393224 | tf_op jit(solution)/shard_map/ppermute | solution.py:330
  71.6 4.9 %collective-permute-start.13 = (bf16[32,16,128]{2,1,0:T(8,128)(2,1)S(1)}, bf16[32,16,128]{2,1,0:T(8,128)(2,1)S(1)}, u32[]{:S(2)}, u32[]{:S(2)}) collective-permute-start(bf16[32,16,128]{2,1,0:T(8,128)(2,1)S(1)} %copy-done.52), channel_id=1, source_target_pairs={{0,20},{4,16},{8,28},{12,24},{16,4},{20,0},{24,12},{28,8},{1,21},{... | collective-permute-start | bytes 393224 | tf_op jit(solution)/shard_map/ppermute | solution.py:330
  77.0 4.2 %collective-permute-start.15 = (bf16[32,16,128]{2,1,0:T(8,128)(2,1)S(1)}, bf16[32,16,128]{2,1,0:T(8,128)(2,1)S(1)}, u32[]{:S(2)}, u32[]{:S(2)}) collective-permute-start(bf16[32,16,128]{2,1,0:T(8,128)(2,1)S(1)} %copy-done.50), channel_id=1, source_target_pairs={{0,28},{4,24},{8,20},{12,16},{16,12},{20,8},{24,4},{28,0},{1,29},{... | collective-permute-start | bytes 393224 | tf_op jit(solution)/shard_map/ppermute | solution.py:330
  82.0 7.5 %forward.2 = (bf16[256,16,128]{2,1,0:T(8,128)(2,1)}, bf16[16,2,32,128]{3,2,1,0:T(8,128)(2,1)}, bf16[16,2,32,128]{3,2,1,0:T(8,128)(2,1)}, bf16[16,2,32,128]{3,2,1...) custom-call(s32[1]{0:T(128)} %bitcast.1.me_ref, ...), custom_call_target="tpu_custom_call" | custom-call | flops 1073741824 | bytes 6291456 | tf_op jit(solution)/shard_map/forward/pallas_call | solution.py:194
  91.4 2.4 %pick.3 = bf16[8,32,16,128]{3,2,1,0:T(8,128)(2,1)} custom-call(s32[8]{0:T(128)} %get-tuple-element.203.choice_ref, bf16[32,16,128]{2,1,0:T(8,128)(2,1)} %get-tuple-element.142.refs_0_, bf16[32,16,128]{2,1,0:T(8,128)(2,1)} %copy-done.31, bf16[32,16,128]{2,1,0:T(8,128)(2,1)} %copy-done.32, bf16[32,16,128]{2,1,0:T(8,128)(2,1)} %copy-done.33, ...), custom_call_target="tpu_custom_call" | custom-call | bytes 2097152 | tf_op jit(solution)/shard_map/pick/pallas_call | solution.py:383
  93.8 7.1 %all-to-all-start = ((bf16[256,16,128]{2,1,0:T(8,128)(2,1)}), bf16[256,16,128]{2,1,0:T(8,128)(2,1)S(1)}, u32[]{:S(2)}, u32[]{:S(2)}) async-start(bf16[256,16,128]{2,1,0:T(8,128)(2,1)} %bitcast.34), calls=%async_computation | async-start | bytes 2097152 | tf_op jit(solution)/shard_map/all_to_all | solution.py:410
  107.8 2.9 %collective-permute-done.33.refs_2_ = bf16[16,2,32,128]{3,2,1,0:T(8,128)(2,1)S(1)} collective-permute-done((bf16[16,2,32,128]{3,2,1,0:T(8,128)(2,1)}, bf16[16,2,32,128]{3,2,1,0:T(8,128)(2,1)S(1)}, u32[]{:S(2)}, u32[]{:S(2)}) %collective-permute-start.33) | collective-permute-done | bytes 262176 | tf_op jit(solution)/shard_map/ppermute | solution.py:330
  110.7 5.2 %collective-permute-done.34.refs_3_ = bf16[16,2,32,128]{3,2,1,0:T(8,128)(2,1)S(1)} collective-permute-done((bf16[16,2,32,128]{3,2,1,0:T(8,128)(2,1)S(1)}, bf16[16,2,32,128]{3,2,1,0:T(8,128)(2,1)S(1)}, u32[]{:S(2)}, u32[]{:S(2)}) %collective-permute-start.34) | collective-permute-done | bytes 262176 | tf_op jit(solution)/shard_map/ppermute | solution.py:330
  116.6 3.7 %middle.7 = (bf16[32,2,16,128]{3,2,1,0:T(8,128)(2,1)}, bf16[32,2,16,128]{3,2,1,0:T(8,128)(2,1)}, bf16[32,2,16,128]{3,2,1,0:T(8,128)(2,1)}, bf16[32,2,16,128]{3,2,1,0:T(8,128)(2,1)}) custom-call(s32[1]{0:T(128)} %bitcast.me_ref.grid_ref, bf16[16,2,32,128]{3,2,1,0:T(8,128)(2,1)} %get-tuple-element.134.refs_0_, bf16[16,2,32,128]{3,2,1,0:T(8,128)(2,1)} %copy-done.19, ...), custom_call_target="tpu_custom_call" | custom-call | flops 536870912 | bytes 3145728 | tf_op jit(solution)/shard_map/middle/pallas_call | solution.py:249
  122.9 4.3 %collective-permute-done.25.refs_3_ = bf16[16,2,32,128]{3,2,1,0:T(8,128)(2,1)S(1)} collective-permute-done((bf16[16,2,32,128]{3,2,1,0:T(8,128)(2,1)}, bf16[16,2,32,128]{3,2,1,0:T(8,128)(2,1)S(1)}, u32[]{:S(2)}, u32[]{:S(2)}) %collective-permute-start.25) | collective-permute-done | bytes 262176 | tf_op jit(solution)/shard_map/ppermute | solution.py:330
  127.9 3.7 %middle.4 = (bf16[32,2,16,128]{3,2,1,0:T(8,128)(2,1)}, bf16[32,2,16,128]{3,2,1,0:T(8,128)(2,1)}, bf16[32,2,16,128]{3,2,1,0:T(8,128)(2,1)}, bf16[32,2,16,128]{3,2,1,0:T(8,128)(2,1)}) custom-call(s32[1]{0:T(128)} %bitcast.me_ref.grid_ref, bf16[16,2,32,128]{3,2,1,0:T(8,128)(2,1)} %get-tuple-element.135.refs_0_, bf16[16,2,32,128]{3,2,1,0:T(8,128)(2,1)} %copy-done.17, ...), custom_call_target="tpu_custom_call" | custom-call | flops 536870912 | bytes 3145728 | tf_op jit(solution)/shard_map/middle/pallas_call | solution.py:249
  132.6 7.6 %forward.3 = (bf16[16,2,32,128]{3,2,1,0:T(8,128)(2,1)}, bf16[16,2,32,128]{3,2,1,0:T(8,128)(2,1)}, bf16[16,2,32,128]{3,2,1,0:T(8,128)(2,1)}, bf16[16,2,32,128]{3,...) custom-call(s32[1]{0:T(128)} %bitcast.1.me_ref, ...), custom_call_target="tpu_custom_call" | custom-call | flops 1073741824 | bytes 6291456 | tf_op jit(solution)/shard_map/forward/pallas_call | solution.py:194
  144.3 5.4 %collective-permute-done.27.refs_2_ = bf16[16,2,32,128]{3,2,1,0:T(8,128)(2,1)S(1)} collective-permute-done((bf16[16,2,32,128]{3,2,1,0:T(8,128)(2,1)}, bf16[16,2,32,128]{3,2,1,0:T(8,128)(2,1)S(1)}, u32[]{:S(2)}, u32[]{:S(2)}) %collective-permute-start.27) | collective-permute-done | bytes 262176 | tf_op jit(solution)/shard_map/ppermute | solution.py:330
  151.9 3.5 %collective-permute-done.30.refs_2_ = bf16[16,2,32,128]{3,2,1,0:T(8,128)(2,1)S(1)} collective-permute-done((bf16[16,2,32,128]{3,2,1,0:T(8,128)(2,1)}, bf16[16,2,32,128]{3,2,1,0:T(8,128)(2,1)S(1)}, u32[]{:S(2)}, u32[]{:S(2)}) %collective-permute-start.30) | collective-permute-done | bytes 262176 | tf_op jit(solution)/shard_map/ppermute | solution.py:330
  157.4 3.2 %collective-permute-done.31.refs_3_ = bf16[16,2,32,128]{3,2,1,0:T(8,128)(2,1)S(1)} collective-permute-done((bf16[16,2,32,128]{3,2,1,0:T(8,128)(2,1)}, bf16[16,2,32,128]{3,2,1,0:T(8,128)(2,1)S(1)}, u32[]{:S(2)}, u32[]{:S(2)}) %collective-permute-start.31) | collective-permute-done | bytes 262176 | tf_op jit(solution)/shard_map/ppermute | solution.py:330
  162.7 3.7 %middle.6 = (bf16[16,2,16,128]{3,2,1,0:T(8,128)(2,1)}, bf16[16,2,16,128]{3,2,1,0:T(8,128)(2,1)}, bf16[16,2,16,128]{3,2,1,0:T(8,128)(2,1)}, bf16[16,2,16,128]{3,2...) custom-call(s32[1]{0:T(128)} %bitcast.me_ref.grid_ref, ...), custom_call_target="tpu_custom_call" | custom-call | flops 536870912 | bytes 3145728 | tf_op jit(solution)/shard_map/middle/pallas_call | solution.py:249
  167.2 3.7 %middle.5 = (bf16[32,2,16,128]{3,2,1,0:T(8,128)(2,1)}, bf16[32,2,16,128]{3,2,1,0:T(8,128)(2,1)}, bf16[32,2,16,128]{3,2,1,0:T(8,128)(2,1)}, bf16[32,2,16,128]{3,2,1,0:T(8,128)(2,1)}) custom-call(s32[1]{0:T(128)} %bitcast.me_ref.grid_ref, bf16[16,2,32,128]{3,2,1,0:T(8,128)(2,1)} %get-tuple-element.155.refs_0_, bf16[16,2,32,128]{3,2,1,0:T(8,128)(2,1)} %copy-done.13, ...), custom_call_target="tpu_custom_call" | custom-call | flops 536870912 | bytes 3145728 | tf_op jit(solution)/shard_map/middle/pallas_call | solution.py:249
  174.1 3.8 %collective-permute-done.39.refs_5_ = bf16[32,2,16,128]{3,2,1,0:T(8,128)(2,1)S(1)} collective-permute-done((bf16[32,2,16,128]{3,2,1,0:T(8,128)(2,1)}, bf16[32,2,16,128]{3,2,1,0:T(8,128)(2,1)S(1)}, u32[]{:S(2)}, u32[]{:S(2)}) %collective-permute-start.39) | collective-permute-done | bytes 262176 | tf_op jit(solution)/shard_map/ppermute | solution.py:330
  177.8 5.3 %collective-permute-done.40.refs_7_ = bf16[32,2,16,128]{3,2,1,0:T(8,128)(2,1)S(1)} collective-permute-done((bf16[32,2,16,128]{3,2,1,0:T(8,128)(2,1)}, bf16[32,2,16,128]{3,2,1,0:T(8,128)(2,1)S(1)}, u32[]{:S(2)}, u32[]{:S(2)}) %collective-permute-start.40) | collective-permute-done | bytes 262176 | tf_op jit(solution)/shard_map/ppermute | solution.py:330
  187.7 4.8 %backward.4.refs_12_ = f32[2,32,128,128]{3,2,1,0:T(8,128)} custom-call(bf16[32,2,16,128]{3,2,1,0:T(8,128)(2,1)} %get-tuple-element.176.refs_0_, bf16[32,2,16,128]{3,2,1,0:T(8,128)(2,1)} %get-tuple-element.150.refs_1_, bf16[32,2,16,128]{3,2,1,0:T(8,128)(2,1)} %copy-done.4, bf16[32,2,16,128]{3,2,1,0:T(8,128)(2,1)} %copy-done.8, ...), custom_call_target="tpu_custom_call" | custom-call | flops 536870912 | bytes 6291456 | tf_op jit(solution)/shard_map/backward/pallas_call | solution.py:308
  192.5 4.8 %backward.5.refs_12_ = f32[2,32,128,128]{3,2,1,0:T(8,128)} custom-call(bf16[32,2,16,128]{3,2,1,0:T(8,128)(2,1)} %get-tuple-element.176.refs_0_, bf16[32,2,16,128]{3,2,1,0:T(8,128)(2,1)} %get-tuple-element.150.refs_1_, bf16[32,2,16,128]{3,2,1,0:T(8,128)(2,1)} %copy-done.4, bf16[32,2,16,128]{3,2,1,0:T(8,128)(2,1)} %copy-done.8, ...), custom_call_target="tpu_custom_call", output_to_operand_aliasing={{}: (12, {})} | custom-call | flops 536870912 | bytes 6291456 | tf_op jit(solution)/shard_map/backward/pallas_call | solution.py:308
  201.8 5.3 %backward.6.refs_12_ = f32[2,32,128,128]{3,2,1,0:T(8,128)} custom-call(bf16[32,2,16,128]{3,2,1,0:T(8,128)(2,1)} %get-tuple-element.159.refs_0_, bf16[16,2,16,128]{3,2,1,0:T(8,128)(2,1)} %get-tuple-element.172.refs_1_, bf16[32,2,16,128]{3,2,1,0:T(8,128)(2,1)} %copy-done.7, bf16[16,2,16,128]{3,2,1,0:T(8,128)(2,1)} %copy-done.25, ...), custom_call_target="tpu_custom_call", output_to_operand_aliasing={{}: (12, {})} | custom-call | flops 536870912 | bytes 6291456 | tf_op jit(solution)/shard_map/backward/pallas_call | solution.py:308
  208.5 5.3 %backward.7 = f32[2,32,128,128]{3,2,1,0:T(8,128)} custom-call(bf16[32,2,16,128]{3,2,1,0:T(8,128)(2,1)} %get-tuple-element.159.refs_0_, bf16[16,2,16,128]{3,2,1,0:T(8,128)(2,1)} %get-tuple-element.181.refs_1_, bf16[32,2,16,128]{3,2,1,0:T(8,128)(2,1)} %copy-done.7, bf16[16,2,16,128]{3,2,1,0:T(8,128)(2,1)} %copy-done.28, ...), custom_call_target="tpu_custom_call", output_to_operand_aliasing={{}: (12, {})} | custom-call | flops 536870912 | bytes 6291456 | tf_op jit(solution)/shard_map/backward/pallas_call | solution.py:308
  (248 shorter events, 65.4 us)
Async XLA Ops:
  4.6 42.3 %collective-permute-start.7 = (bf16[128,2048]{1,0:T(8,128)(2,1)}, bf16[128,2048]{1,0:T(8,128)(2,1)S(1)}, u32[]{:S(2)}, u32[]{:S(2)}) collective-permute-start(bf16[128,2048]{1,0:T(8,128)(2,1)} %get-tuple-element.107), channel_id=1, source_target_pairs={{0,3},{1,2},{2,1},{3,0},{4,7},{5,6},{6,5},{7,4},{8,11},{9,10},{10,... | collective-permute-start | bytes 1572872 | tf_op jit(solution)/shard_map/ppermute | solution.py:427
  11.6 16.5 %collective-permute-start.5 = (bf16[32,16,128]{2,1,0:T(8,128)(2,1)S(1)}, bf16[32,16,128]{2,1,0:T(8,128)(2,1)S(1)}, u32[]{:S(2)}, u32[]{:S(2)}) collective-permute-start(bf16[32,16,128]{2,1,0:T(8,128)(2,1)S(1)} %get-tuple-element.189), channel_id=1, source_target_pairs={{0,24},{4,28},{8,16},{12,20},{16,8},{20,12},{24,0},{28,4},{1,25},{... | collective-permute-start | bytes 393224 | tf_op jit(solution)/shard_map/ppermute | solution.py:330
  11.8 20.5 %collective-permute-start.4 = (bf16[32,16,128]{2,1,0:T(8,128)(2,1)S(1)}, bf16[32,16,128]{2,1,0:T(8,128)(2,1)S(1)}, u32[]{:S(2)}, u32[]{:S(2)}) collective-permute-start(bf16[32,16,128]{2,1,0:T(8,128)(2,1)S(1)} %get-tuple-element.190), channel_id=1, source_target_pairs={{0,20},{4,16},{8,28},{12,24},{16,4},{20,0},{24,12},{28,8},{1,21},{... | collective-permute-start | bytes 393224 | tf_op jit(solution)/shard_map/ppermute | solution.py:330
  12.5 22.3 %collective-permute-start.3 = (bf16[32,16,128]{2,1,0:T(8,128)(2,1)S(1)}, bf16[32,16,128]{2,1,0:T(8,128)(2,1)S(1)}, u32[]{:S(2)}, u32[]{:S(2)}) collective-permute-start(bf16[32,16,128]{2,1,0:T(8,128)(2,1)S(1)} %get-tuple-element.191), channel_id=1, source_target_pairs={{0,16},{4,20},{8,24},{12,28},{16,0},{20,4},{24,8},{28,12},{1,17},{... | collective-permute-start | bytes 393224 | tf_op jit(solution)/shard_map/ppermute | solution.py:330
  16.0 23.0 %collective-permute-start.2 = (bf16[32,16,128]{2,1,0:T(8,128)(2,1)S(1)}, bf16[32,16,128]{2,1,0:T(8,128)(2,1)S(1)}, u32[]{:S(2)}, u32[]{:S(2)}) collective-permute-start(bf16[32,16,128]{2,1,0:T(8,128)(2,1)S(1)} %get-tuple-element.192), channel_id=1, source_target_pairs={{0,12},{4,8},{8,4},{12,0},{16,28},{20,24},{24,20},{28,16},{1,13},{... | collective-permute-start | bytes 393224 | tf_op jit(solution)/shard_map/ppermute | solution.py:330
  42.2 16.4 %collective-permute-start.16 = (bf16[32,16,128]{2,1,0:T(8,128)(2,1)}, bf16[32,16,128]{2,1,0:T(8,128)(2,1)S(1)}, u32[]{:S(2)}, u32[]{:S(2)}) collective-permute-start(bf16[32,16,128]{2,1,0:T(8,128)(2,1)} %get-tuple-element.118), channel_id=1, source_target_pairs={{0,4},{4,0},{8,12},{12,8},{16,20},{20,16},{24,28},{28,24},{1,5},{5... | collective-permute-start | bytes 393224 | tf_op jit(solution)/shard_map/ppermute | solution.py:330
  43.3 17.8 %collective-permute-start.17 = (bf16[32,16,128]{2,1,0:T(8,128)(2,1)}, bf16[32,16,128]{2,1,0:T(8,128)(2,1)S(1)}, u32[]{:S(2)}, u32[]{:S(2)}) collective-permute-start(bf16[32,16,128]{2,1,0:T(8,128)(2,1)} %get-tuple-element.119), channel_id=1, source_target_pairs={{0,8},{4,12},{8,0},{12,4},{16,24},{20,28},{24,16},{28,20},{1,9},{5... | collective-permute-start | bytes 393224 | tf_op jit(solution)/shard_map/ppermute | solution.py:330
  43.3 19.6 %collective-permute-start.18 = (bf16[32,16,128]{2,1,0:T(8,128)(2,1)}, bf16[32,16,128]{2,1,0:T(8,128)(2,1)S(1)}, u32[]{:S(2)}, u32[]{:S(2)}) collective-permute-start(bf16[32,16,128]{2,1,0:T(8,128)(2,1)} %get-tuple-element.120), channel_id=1, source_target_pairs={{0,12},{4,8},{8,4},{12,0},{16,28},{20,24},{24,20},{28,16},{1,13},{... | collective-permute-start | bytes 393224 | tf_op jit(solution)/shard_map/ppermute | solution.py:330
  45.8 18.3 %collective-permute-start.19 = (bf16[32,16,128]{2,1,0:T(8,128)(2,1)}, bf16[32,16,128]{2,1,0:T(8,128)(2,1)S(1)}, u32[]{:S(2)}, u32[]{:S(2)}) collective-permute-start(bf16[32,16,128]{2,1,0:T(8,128)(2,1)} %get-tuple-element.121), channel_id=1, source_target_pairs={{0,16},{4,20},{8,24},{12,28},{16,0},{20,4},{24,8},{28,12},{1,17},{... | collective-permute-start | bytes 393224 | tf_op jit(solution)/shard_map/ppermute | solution.py:330
  46.9 17.9 %collective-permute-start.20 = (bf16[32,16,128]{2,1,0:T(8,128)(2,1)}, bf16[32,16,128]{2,1,0:T(8,128)(2,1)S(1)}, u32[]{:S(2)}, u32[]{:S(2)}) collective-permute-start(bf16[32,16,128]{2,1,0:T(8,128)(2,1)} %get-tuple-element.122), channel_id=1, source_target_pairs={{0,20},{4,16},{8,28},{12,24},{16,4},{20,0},{24,12},{28,8},{1,21},{... | collective-permute-start | bytes 393224 | tf_op jit(solution)/shard_map/ppermute | solution.py:330
  64.8 24.7 %collective-permute-start.11 = (bf16[32,16,128]{2,1,0:T(8,128)(2,1)S(1)}, bf16[32,16,128]{2,1,0:T(8,128)(2,1)S(1)}, u32[]{:S(2)}, u32[]{:S(2)}) collective-permute-start(bf16[32,16,128]{2,1,0:T(8,128)(2,1)S(1)} %copy-done.54), channel_id=1, source_target_pairs={{0,12},{4,8},{8,4},{12,0},{16,28},{20,24},{24,20},{28,16},{1,13},{... | collective-permute-start | bytes 393224 | tf_op jit(solution)/shard_map/ppermute | solution.py:330
  67.2 22.3 %collective-permute-start.12 = (bf16[32,16,128]{2,1,0:T(8,128)(2,1)S(1)}, bf16[32,16,128]{2,1,0:T(8,128)(2,1)S(1)}, u32[]{:S(2)}, u32[]{:S(2)}) collective-permute-start(bf16[32,16,128]{2,1,0:T(8,128)(2,1)S(1)} %copy-done.53), channel_id=1, source_target_pairs={{0,16},{4,20},{8,24},{12,28},{16,0},{20,4},{24,8},{28,12},{1,17},{... | collective-permute-start | bytes 393224 | tf_op jit(solution)/shard_map/ppermute | solution.py:330
  71.6 19.0 %collective-permute-start.13 = (bf16[32,16,128]{2,1,0:T(8,128)(2,1)S(1)}, bf16[32,16,128]{2,1,0:T(8,128)(2,1)S(1)}, u32[]{:S(2)}, u32[]{:S(2)}) collective-permute-start(bf16[32,16,128]{2,1,0:T(8,128)(2,1)S(1)} %copy-done.52), channel_id=1, source_target_pairs={{0,20},{4,16},{8,28},{12,24},{16,4},{20,0},{24,12},{28,8},{1,21},{... | collective-permute-start | bytes 393224 | tf_op jit(solution)/shard_map/ppermute | solution.py:330
  76.5 14.1 %collective-permute-start.14 = (bf16[32,16,128]{2,1,0:T(8,128)(2,1)S(1)}, bf16[32,16,128]{2,1,0:T(8,128)(2,1)S(1)}, u32[]{:S(2)}, u32[]{:S(2)}) collective-permute-start(bf16[32,16,128]{2,1,0:T(8,128)(2,1)S(1)} %copy-done.51), channel_id=1, source_target_pairs={{0,24},{4,28},{8,16},{12,20},{16,8},{20,12},{24,0},{28,4},{1,25},{... | collective-permute-start | bytes 393224 | tf_op jit(solution)/shard_map/ppermute | solution.py:330
  93.8 37.8 %all-to-all-start = ((bf16[256,16,128]{2,1,0:T(8,128)(2,1)}), bf16[256,16,128]{2,1,0:T(8,128)(2,1)S(1)}, u32[]{:S(2)}, u32[]{:S(2)}) async-start(bf16[256,16,128]{2,1,0:T(8,128)(2,1)} %bitcast.34), calls=%async_computation | async-start | bytes 2097152 | tf_op jit(solution)/shard_map/all_to_all | solution.py:410
  104.8 18.0 %collective-permute-start.23 = (bf16[16,2,32,128]{3,2,1,0:T(8,128)(2,1)}, bf16[16,2,32,128]{3,2,1,0:T(8,128)(2,1)S(1)}, u32[]{:S(2)}, u32[]{:S(2)}) collective-permute-start(bf16[16,2,32,128]{3,2,1,0:T(8,128)(2,1)} %get-tuple-element.137), channel_id=1, source_target_pairs={{0,1},{1,0},{2,3},{3,2},{4,5},{5,4},{6,7},{7,6},{8,9},{9,8},{10,11... | collective-permute-start | bytes 786440 | tf_op jit(solution)/shard_map/ppermute | solution.py:330
  104.9 17.9 %collective-permute-start.24 = (bf16[16,2,32,128]{3,2,1,0:T(8,128)(2,1)}, bf16[16,2,32,128]{3,2,1,0:T(8,128)(2,1)S(1)}, u32[]{:S(2)}, u32[]{:S(2)}) collective-permute-start(bf16[16,2,32,128]{3,2,1,0:T(8,128)(2,1)} %get-tuple-element.139), channel_id=1, source_target_pairs={{0,2},{1,3},{2,0},{3,1},{4,6},{5,7},{6,4},{7,5},{8,10},{9,11},{10,... | collective-permute-start | bytes 786440 | tf_op jit(solution)/shard_map/ppermute | solution.py:330
  106.9 20.3 %collective-permute-start.25 = (bf16[16,2,32,128]{3,2,1,0:T(8,128)(2,1)}, bf16[16,2,32,128]{3,2,1,0:T(8,128)(2,1)S(1)}, u32[]{:S(2)}, u32[]{:S(2)}) collective-permute-start(bf16[16,2,32,128]{3,2,1,0:T(8,128)(2,1)} %get-tuple-element.141), channel_id=1, source_target_pairs={{0,3},{1,2},{2,1},{3,0},{4,7},{5,6},{6,5},{7,4},{8,11},{9,10},{10,... | collective-permute-start | bytes 786440 | tf_op jit(solution)/shard_map/ppermute | solution.py:330
  120.3 22.1 %collective-permute-start.35 = (bf16[32,2,16,128]{3,2,1,0:T(8,128)(2,1)}, bf16[32,2,16,128]{3,2,1,0:T(8,128)(2,1)S(1)}, u32[]{:S(2)}, u32[]{:S(2)}) collective-permute-start(bf16[32,2,16,128]{3,2,1,0:T(8,128)(2,1)} %get-tuple-element.169), channel_id=1, source_target_pairs={{0,1},{1,0},{2,3},{3,2},{4,5},{5,4},{6,7},{7,6},{8,9},{9,8},{10,11... | collective-permute-start | bytes 786440 | tf_op jit(solution)/shard_map/ppermute | solution.py:330
  120.8 21.7 %collective-permute-start.36 = (bf16[32,2,16,128]{3,2,1,0:T(8,128)(2,1)}, bf16[32,2,16,128]{3,2,1,0:T(8,128)(2,1)S(1)}, u32[]{:S(2)}, u32[]{:S(2)}) collective-permute-start(bf16[32,2,16,128]{3,2,1,0:T(8,128)(2,1)} %get-tuple-element.170), channel_id=1, source_target_pairs={{0,2},{1,3},{2,0},{3,1},{4,6},{5,7},{6,4},{7,5},{8,10},{9,11},{10,... | collective-permute-start | bytes 786440 | tf_op jit(solution)/shard_map/ppermute | solution.py:330
  142.5 18.1 %collective-permute-start.31 = (bf16[16,2,32,128]{3,2,1,0:T(8,128)(2,1)}, bf16[16,2,32,128]{3,2,1,0:T(8,128)(2,1)S(1)}, u32[]{:S(2)}, u32[]{:S(2)}) collective-permute-start(bf16[16,2,32,128]{3,2,1,0:T(8,128)(2,1)} %get-tuple-element.163), channel_id=1, source_target_pairs={{0,3},{1,2},{2,1},{3,0},{4,7},{5,6},{6,5},{7,4},{8,11},{9,10},{10,... | collective-permute-start | bytes 786440 | tf_op jit(solution)/shard_map/ppermute | solution.py:330
  144.3 22.2 %collective-permute-start.28 = (bf16[16,2,32,128]{3,2,1,0:T(8,128)(2,1)}, bf16[16,2,32,128]{3,2,1,0:T(8,128)(2,1)S(1)}, u32[]{:S(2)}, u32[]{:S(2)}) collective-permute-start(bf16[16,2,32,128]{3,2,1,0:T(8,128)(2,1)} %get-tuple-element.158), channel_id=1, source_target_pairs={{0,3},{1,2},{2,1},{3,0},{4,7},{5,6},{6,5},{7,4},{8,11},{9,10},{10,... | collective-permute-start | bytes 786440 | tf_op jit(solution)/shard_map/ppermute | solution.py:330
  149.7 22.0 %collective-permute-start.37 = (bf16[32,2,16,128]{3,2,1,0:T(8,128)(2,1)S(1)}, bf16[32,2,16,128]{3,2,1,0:T(8,128)(2,1)S(1)}, u32[]{:S(2)}, u32[]{:S(2)}) collective-permute-start(bf16[32,2,16,128]{3,2,1,0:T(8,128)(2,1)S(1)} %copy-done.47), channel_id=1, source_target_pairs={{0,3},{1,2},{2,1},{3,0},{4,7},{5,6},{6,5},{7,4},{8,11},{9,10},{10,... | collective-permute-start | bytes 786440 | tf_op jit(solution)/shard_map/ppermute | solution.py:330
  149.8 22.3 %collective-permute-start.38 = (bf16[32,2,16,128]{3,2,1,0:T(8,128)(2,1)}, bf16[32,2,16,128]{3,2,1,0:T(8,128)(2,1)S(1)}, u32[]{:S(2)}, u32[]{:S(2)}) collective-permute-start(bf16[32,2,16,128]{3,2,1,0:T(8,128)(2,1)} %get-tuple-element.151), channel_id=1, source_target_pairs={{0,1},{1,0},{2,3},{3,2},{4,5},{5,4},{6,7},{7,6},{8,9},{9,8},{10,11... | collective-permute-start | bytes 786440 | tf_op jit(solution)/shard_map/ppermute | solution.py:330
  155.4 22.5 %collective-permute-start.39 = (bf16[32,2,16,128]{3,2,1,0:T(8,128)(2,1)}, bf16[32,2,16,128]{3,2,1,0:T(8,128)(2,1)S(1)}, u32[]{:S(2)}, u32[]{:S(2)}) collective-permute-start(bf16[32,2,16,128]{3,2,1,0:T(8,128)(2,1)} %get-tuple-element.152), channel_id=1, source_target_pairs={{0,2},{1,3},{2,0},{3,1},{4,6},{5,7},{6,4},{7,5},{8,10},{9,11},{10,... | collective-permute-start | bytes 786440 | tf_op jit(solution)/shard_map/ppermute | solution.py:330
  160.6 22.5 %collective-permute-start.40 = (bf16[32,2,16,128]{3,2,1,0:T(8,128)(2,1)}, bf16[32,2,16,128]{3,2,1,0:T(8,128)(2,1)S(1)}, u32[]{:S(2)}, u32[]{:S(2)}) collective-permute-start(bf16[32,2,16,128]{3,2,1,0:T(8,128)(2,1)} %get-tuple-element.153), channel_id=1, source_target_pairs={{0,3},{1,2},{2,1},{3,0},{4,7},{5,6},{6,5},{7,4},{8,11},{9,10},{10,... | collective-permute-start | bytes 786440 | tf_op jit(solution)/shard_map/ppermute | solution.py:330
  166.5 17.2 %collective-permute-start.47 = (bf16[16,2,16,128]{3,2,1,0:T(8,128)(2,1)}, bf16[16,2,16,128]{3,2,1,0:T(8,128)(2,1)S(1)}, u32[]{:S(2)}, u32[]{:S(2)}) collective-permute-start(bf16[16,2,16,128]{3,2,1,0:T(8,128)(2,1)} %get-tuple-element.173), channel_id=1, source_target_pairs={{0,1},{1,0},{2,3},{3,2},{4,5},{5,4},{6,7},{7,6},{8,9},{9,8},{10,11... | collective-permute-start | bytes 393224 | tf_op jit(solution)/shard_map/ppermute | solution.py:330
  171.8 28.8 %collective-permute-start.41 = (bf16[32,2,16,128]{3,2,1,0:T(8,128)(2,1)}, bf16[32,2,16,128]{3,2,1,0:T(8,128)(2,1)S(1)}, u32[]{:S(2)}, u32[]{:S(2)}) collective-permute-start(bf16[32,2,16,128]{3,2,1,0:T(8,128)(2,1)} %get-tuple-element.182), channel_id=1, source_target_pairs={{0,1},{1,0},{2,3},{3,2},{4,5},{5,4},{6,7},{7,6},{8,9},{9,8},{10,11... | collective-permute-start | bytes 786440 | tf_op jit(solution)/shard_map/ppermute | solution.py:330
  172.0 28.9 %collective-permute-start.43 = (bf16[32,2,16,128]{3,2,1,0:T(8,128)(2,1)}, bf16[32,2,16,128]{3,2,1,0:T(8,128)(2,1)S(1)}, u32[]{:S(2)}, u32[]{:S(2)}) collective-permute-start(bf16[32,2,16,128]{3,2,1,0:T(8,128)(2,1)} %get-tuple-element.184), channel_id=1, source_target_pairs={{0,2},{1,3},{2,0},{3,1},{4,6},{5,7},{6,4},{7,5},{8,10},{9,11},{10,... | collective-permute-start | bytes 786440 | tf_op jit(solution)/shard_map/ppermute | solution.py:330
  177.8 23.1 %collective-permute-start.45 = (bf16[32,2,16,128]{3,2,1,0:T(8,128)(2,1)}, bf16[32,2,16,128]{3,2,1,0:T(8,128)(2,1)S(1)}, u32[]{:S(2)}, u32[]{:S(2)}) collective-permute-start(bf16[32,2,16,128]{3,2,1,0:T(8,128)(2,1)} %get-tuple-element.186), channel_id=1, source_target_pairs={{0,3},{1,2},{2,1},{3,0},{4,7},{5,6},{6,5},{7,4},{8,11},{9,10},{10,... | collective-permute-start | bytes 786440 | tf_op jit(solution)/shard_map/ppermute | solution.py:330
  183.1 14.4 %collective-permute-start.48 = (bf16[16,2,16,128]{3,2,1,0:T(8,128)(2,1)}, bf16[16,2,16,128]{3,2,1,0:T(8,128)(2,1)S(1)}, u32[]{:S(2)}, u32[]{:S(2)}) collective-permute-start(bf16[16,2,16,128]{3,2,1,0:T(8,128)(2,1)} %get-tuple-element.174), channel_id=1, source_target_pairs={{0,2},{1,3},{2,0},{3,1},{4,6},{5,7},{6,4},{7,5},{8,10},{9,11},{10,... | collective-permute-start | bytes 393224 | tf_op jit(solution)/shard_map/ppermute | solution.py:330
  183.7 15.4 %collective-permute-start.49 = (bf16[16,2,16,128]{3,2,1,0:T(8,128)(2,1)}, bf16[16,2,16,128]{3,2,1,0:T(8,128)(2,1)S(1)}, u32[]{:S(2)}, u32[]{:S(2)}) collective-permute-start(bf16[16,2,16,128]{3,2,1,0:T(8,128)(2,1)} %get-tuple-element.175), channel_id=1, source_target_pairs={{0,3},{1,2},{2,1},{3,0},{4,7},{5,6},{6,5},{7,4},{8,11},{9,10},{10,... | collective-permute-start | bytes 393224 | tf_op jit(solution)/shard_map/ppermute | solution.py:330
  (89 other events, 1011.5 us)

commit v3 on v2

--- a/solution.py
+++ b/solution.py
@@ -47,6 +47,7 @@
 SCALARS = pl.BlockSpec(memory_space=pltpu.SMEM)
 WHOLE = pl.BlockSpec(memory_space=pltpu.VMEM)
 UNROLL = 8
+STEP = 8
 LANES = 128
 
 
@@ -138,6 +139,20 @@
     )(me, kernel, neg, first, cols)
 
 
+PAD = 1
+
+
+def unload(hold, first, out_ref):
+    lines, _, count, _ = out_ref.shape
+
+    def step(line, carry):
+        for c in range(2):
+            out_ref[line, c] = hold[c, pl.ds((first + line) * (count + PAD), count), :].astype(BF16)
+        return carry
+
+    lax.fori_loop(0, lines, step, 0, unroll=min(8, lines))
+
+
 def forward_kernel(parts, base, cuts, me_ref, grid_ref, own_ref, *refs):
     piece_refs = refs[:parts]
     if parts > 1:
@@ -169,7 +184,7 @@
         second = dot(yt, stack)
         for k in range(2):
             for c in range(2):
-                hold[c, pl.ds(2 * pair + k, ny, stride=count), :] = second[
+                hold[c, pl.ds(2 * pair + k, ny, stride=count + PAD), :] = second[
                     c * ny : (c + 1) * ny, k * nz : (k + 1) * nz
                 ]
         return carry
@@ -178,10 +193,7 @@
     part = ny // len(out_refs)
     for number, out_ref in enumerate(out_refs):
         owner = grid_ref[0] ^ (number // cuts)
-        begin = (owner * cuts + number % cuts) * (part * count)
-        for c in range(2):
-            piece = hold[c, pl.ds(begin, part * count), :]
-            out_ref[:, c] = piece.astype(BF16).reshape(part, count, nz)
+        unload(hold, (owner * cuts + number % cuts) * part, out_ref)
 
 
 def forward(me, grid_pos, own, pieces, half, count, zt, yt, groups, cuts):
@@ -199,7 +211,7 @@
         + [spec(p.shape) for p in pieces]
         + [spec(zt.shape), spec(yt.shape)],
         out_specs=[spec(o.shape) for o in outs],
-        scratch_shapes=[pltpu.VMEM((2, ny * count, nz), F32)],
+        scratch_shapes=[pltpu.VMEM((2, ny * (count + PAD), nz), F32)],
         cost_estimate=cost(2 * count * ny * nz * 2 * (2 * ny + 2 * nz), 12 * count * ny * nz),
         name="forward",
     )(me, grid_pos, own, *pieces, zt, yt)
@@ -226,7 +238,7 @@
         third = dot(ixt, scaled)
         for k in range(2):
             for c in range(2):
-                hold[c, pl.ds(2 * pair + k, nx, stride=count), :] = third[
+                hold[c, pl.ds(2 * pair + k, nx, stride=count + PAD), :] = third[
                     c * nx : (c + 1) * nx, k * nz : (k + 1) * nz
                 ]
         return carry
@@ -235,10 +247,7 @@
     rows = nx // (groups * halves)
     for number, out_ref in enumerate(out_refs):
         owner = grid_ref[0] ^ (number // halves)
-        begin = (owner * halves + number % halves) * (rows * count)
-        for c in range(2):
-            piece = hold[c, pl.ds(begin, rows * count), :]
-            out_ref[:, c] = piece.astype(BF16).reshape(rows, count, nz)
+        unload(hold, (owner * halves + number % halves) * rows, out_ref)
 
 
 def middle(grid_pos, pieces, kern, cut, xt, ixt, halves):
@@ -254,16 +263,16 @@
         + [spec(p.shape) for p in pieces]
         + [spec((count, nx, nz), lambda i: (cut, 0, 0)), spec(xt.shape), spec(ixt.shape)],
         out_specs=[spec(shape.shape)] * (groups * halves),
-        scratch_shapes=[pltpu.VMEM((2, nx * count, nz), F32)],
+        scratch_shapes=[pltpu.VMEM((2, nx * (count + PAD), nz), F32)],
         cost_estimate=cost(16 * nx * nx * count * nz, 12 * count * nx * nz),
         name="middle",
     )(grid_pos, *pieces, kern, xt, ixt)
 
 
-def backward_kernel(bases, has_total, base, *refs):
-    in_refs = refs[: len(bases)]
-    their_ref, weight_ref, yt_ref, zt_ref = refs[len(bases) : len(bases) + 4]
-    total_ref = refs[len(bases) + 4] if has_total == 2 else None
+def backward_kernel(number, has_total, *refs):
+    in_refs = refs[:number]
+    their_ref, weight_ref, yt_ref, zt_ref = refs[number : number + 4]
+    total_ref = refs[number + 4] if has_total == 2 else None
     out_ref = refs[-1]
     count, ny, nz = out_ref.shape[1:]
     tiles = ny // their_ref.shape[1]
@@ -274,7 +283,7 @@
         lines = []
         for k in range(2):
             x = 2 * pair + k
-            lines.append(jnp.concatenate([r[x + b, c] for c in range(2) for r, b in zip(in_refs, bases)], 0))
+            lines.append(jnp.concatenate([r[x, c] for c in range(2) for r in in_refs], 0))
         fourth = dot(yt, jnp.concatenate(lines, 1)).astype(BF16)
         stack = jnp.concatenate(
             [
@@ -286,7 +295,7 @@
         potential = dot(stack, zt)
         for k in range(2):
             x = 2 * pair + k
-            theirs = their_ref[pl.ds((base + x) * tiles, tiles)].reshape(ny, nz).astype(F32) * weight
+            theirs = their_ref[pl.ds(x * tiles, tiles)].reshape(ny, nz).astype(F32) * weight
             for n in range(2):
                 term = potential[k * ny : (k + 1) * ny, n * nz : (n + 1) * nz] * theirs
                 if total_ref is None:
@@ -301,16 +310,25 @@
 def backward(pieces, bases, their, weight, yt, zt, total, accumulate, part_number, count, slab):
     ny, nz = sum(p.shape[2] for p in pieces), pieces[0].shape[3]
     number = len(pieces)
-    block = spec((2, count, ny, nz), lambda i: (0, part_number, 0, 0))
+    step = min(STEP, count)
+    steps = count // step
+    begin = part_number * steps
+    tiles = ny // their.shape[1]
+    block = spec((2, step, ny, nz), lambda i: (0, begin + i, 0, 0))
     has_total = 0 if total is None else (2 if accumulate else 1)
     extra = [] if total is None else [total]
     extra_specs = [] if total is None else [block if accumulate else pl.BlockSpec(memory_space=pl.ANY)]
-    return pl.pallas_call(
-        functools.partial(backward_kernel, bases, has_total, part_number * count),
-        grid=(1,),
+
+    def rows_of(piece, base):
+        return spec((step,) + piece.shape[1:], lambda i: (base // step + i, 0, 0, 0))
+
+    return pl.pallas_call(
+        functools.partial(backward_kernel, number, has_total),
+        grid=(steps,),
         out_shape=jax.ShapeDtypeStruct((2, slab, ny, nz), F32),
-        in_specs=[spec(p.shape) for p in pieces]
-        + [spec(their.shape), SCALARS, spec(yt.shape), spec(zt.shape)]
+        in_specs=[rows_of(p, b) for p, b in zip(pieces, bases)]
+        + [spec((step * tiles,) + their.shape[1:], lambda i: (begin + i, 0, 0))]
+        + [SCALARS, spec(yt.shape), spec(zt.shape)]
         + extra_specs,
         out_specs=block,
         input_output_aliases={number + 4: 0} if extra else {},
@@ -450,7 +468,10 @@
     def outward(pieces):
         outs = forward(my_band, my_grid, orbitals, pieces, 0, slab, zright, yleft, groups, cuts)
         their, sent = (outs[0], outs[1:]) if len(pieces) > 1 else (pieces[0], outs)
-        moved = [[swap(sent[slot * cuts + cut], slot) for slot in range(groups)] for cut in range(cuts)]
+        moved = [
+            [swap(sent[slot * cuts + cut], slot) for slot in range(groups)]
+            for cut in range(cuts)
+        ]
         return their, sent, moved
 
     their0, sent, moved0 = outward(fetched)

time: 214 us -> 211 us (0.986)
  Pallas kernels: 68.9 us -> 61.9 us
  waiting for transfers between devices: 41.5 us -> 45.4 us
    ppermute x48, waiting for transfers between devices: 41.5 us -> 45.4 us  [shift(): lax.ppermute(value, axis, [(i, i ^ mask) for i in range(size)])]
    pallas_call x2, Pallas kernels: 15 us -> 11.3 us  [forward(): pl.pallas_call(functools.partial(forward_kernel, parts, half * count, cut...]
    pallas_call x4, Pallas kernels: 20.2 us -> 17.4 us  [backward(): pl.pallas_call(functools.partial(backward_kernel, number, has_total), gri...]
  transfers between devices with their start and end apart: 51 -> 51, of which waited for: 17 -> 17; matrix products, arithmetic and copies ran while one was open for 3% -> 3% of each run, Pallas kernels for 27% -> 25%
where the time goes in v3:
time: 211 us; the launch traced here: 210 us
  starting transfers between devices  86.8 us (41%)
  Pallas kernels  61.9 us (29%)
  waiting for transfers between devices  45.4 us (22%)
  local copies, waits for them, and re-layouts  12.6 us (6%)
    ppermute x48, starting transfers between devices, shift(): lax.ppermute(value, axis, [(i, i ^ mask) for i in range(size)])  75.9 us
    ppermute x48, waiting for transfers between devices, shift(): lax.ppermute(value, axis, [(i, i ^ mask) for i in range(size)])  45.4 us
    pallas_call x4, Pallas kernels, backward(): pl.pallas_call(functools.partial(backward_kernel, number, has_total), gri...  17.4 us
    pallas_call x4, Pallas kernels, middle(): pl.pallas_call(functools.partial(middle_kernel, groups, halves), grid=(1,...  14.5 us
    pallas_call x2, Pallas kernels, forward(): pl.pallas_call(functools.partial(forward_kernel, parts, half * count, cut...  11.3 us
    pallas_call x1, Pallas kernels, expand(): pl.pallas_call(functools.partial(expand_kernel, scale, groups, rows * len...  9.28 us
    all_to_all x1, starting transfers between devices, exchange(): lax.all_to_all(value, 'band', split_axis=0, concat_axis=0, tiled=True)  7.14 us
    unnamed x140, local copies, waits for them, and re-layouts  5.77 us
  transfers between devices with their start and end apart: 51, of which 17 were waited for; matrix products, arithmetic and copies ran while one was open for 3% of the time, Pallas kernels for 25%

profile of v3, /device:TPU:0, one launch (start us, length us, event | category | flops | bytes accessed | tf_op | source)
XLA Modules:
  0.0 210.0 jit_solution(2601742720516270674)
XLA Ops:
  2.2 2.4 %mirror.1 = (bf16[128,2048]{1,0:T(8,128)(2,1)}, bf16[128,128]{1,0:T(8,128)(2,1)}) custom-call(s32[1]{0:T(128)} %bitcast.me_ref.grid_ref, f32[128,2048]{1,0:T(8,128)} %own_ref.2, s32[1,8192]{1,0:T(1,128)} %bitcast.40), custom_call_target="tpu_custom_call" | custom-call | flops 67108864 | bytes 1572864 | tf_op jit(solution)/shard_map/mirror/pallas_call | solution.py:86
  4.6 2.4 %collective-permute-start.7 = (bf16[128,2048]{1,0:T(8,128)(2,1)}, bf16[128,2048]{1,0:T(8,128)(2,1)S(1)}, u32[]{:S(2)}, u32[]{:S(2)}) collective-permute-start(bf16[128,2048]{1,0:T(8,128)(2,1)} %get-tuple-element.107), channel_id=1, source_target_pairs={{0,3},{1,2},{2,1},{3,0},{4,7},{5,6},{6,5},{7,4},{8,11},{9,10},{10,... | collective-permute-start | bytes 1572872 | tf_op jit(solution)/shard_map/ppermute | solution.py:445
  7.0 4.6 %collective-permute-start.6 = (bf16[32,16,128]{2,1,0:T(8,128)(2,1)S(1)}, bf16[32,16,128]{2,1,0:T(8,128)(2,1)S(1)}, u32[]{:S(2)}, u32[]{:S(2)}) collective-permute-start(bf16[32,16,128]{2,1,0:T(8,128)(2,1)S(1)} %get-tuple-element.188), channel_id=1, source_target_pairs={{0,28},{4,24},{8,20},{12,16},{16,12},{20,8},{24,4},{28,0},{1,29},{... | collective-permute-start | bytes 393224 | tf_op jit(solution)/shard_map/ppermute | solution.py:348
  16.0 12.0 %collective-permute-start.2 = (bf16[32,16,128]{2,1,0:T(8,128)(2,1)S(1)}, bf16[32,16,128]{2,1,0:T(8,128)(2,1)S(1)}, u32[]{:S(2)}, u32[]{:S(2)}) collective-permute-start(bf16[32,16,128]{2,1,0:T(8,128)(2,1)S(1)} %get-tuple-element.192), channel_id=1, source_target_pairs={{0,12},{4,8},{8,4},{12,0},{16,28},{20,24},{24,20},{28,16},{1,13},{... | collective-permute-start | bytes 393224 | tf_op jit(solution)/shard_map/ppermute | solution.py:348
  46.9 2.5 %collective-permute-start.20 = (bf16[32,16,128]{2,1,0:T(8,128)(2,1)}, bf16[32,16,128]{2,1,0:T(8,128)(2,1)S(1)}, u32[]{:S(2)}, u32[]{:S(2)}) collective-permute-start(bf16[32,16,128]{2,1,0:T(8,128)(2,1)} %get-tuple-element.122), channel_id=1, source_target_pairs={{0,20},{4,16},{8,28},{12,24},{16,4},{20,0},{24,12},{28,8},{1,21},{... | collective-permute-start | bytes 393224 | tf_op jit(solution)/shard_map/ppermute | solution.py:348
  49.3 9.3 %expand.1.refs_4_ = f32[32,128,128]{2,1,0:T(8,128)} custom-call(s32[1]{0:T(128)} %bitcast.me_ref.grid_ref, f32[128,2048]{1,0:T(8,128)} %own_ref.2, bf16[128,2048]{1,0:T(8,128)(2,1)} %copy-done.46, bf16[128,128]{1,0:T(8,128)(2,1)} %copy-done.69, s32[1,8192]{1,0:T(1,128)} %bitcast.41), custom_call_target="tpu_custom_call" | custom-call | flops 4294967296 | bytes 3145728 | tf_op jit(solution)/shard_map/expand/pallas_call | solution.py:131
  58.6 2.5 %collective-permute-start.21 = (bf16[32,16,128]{2,1,0:T(8,128)(2,1)S(1)}, bf16[32,16,128]{2,1,0:T(8,128)(2,1)S(1)}, u32[]{:S(2)}, u32[]{:S(2)}) collective-permute-start(bf16[32,16,128]{2,1,0:T(8,128)(2,1)S(1)} %copy-done.67), channel_id=1, source_target_pairs={{0,24},{4,28},{8,16},{12,20},{16,8},{20,12},{24,0},{28,4},{1,25},{... | collective-permute-start | bytes 393224 | tf_op jit(solution)/shard_map/ppermute | solution.py:348
  64.8 2.4 %collective-permute-start.11 = (bf16[32,16,128]{2,1,0:T(8,128)(2,1)S(1)}, bf16[32,16,128]{2,1,0:T(8,128)(2,1)S(1)}, u32[]{:S(2)}, u32[]{:S(2)}) collective-permute-start(bf16[32,16,128]{2,1,0:T(8,128)(2,1)S(1)} %copy-done.54), channel_id=1, source_target_pairs={{0,12},{4,8},{8,4},{12,0},{16,28},{20,24},{24,20},{28,16},{1,13},{... | collective-permute-start | bytes 393224 | tf_op jit(solution)/shard_map/ppermute | solution.py:348
  67.2 4.4 %collective-permute-start.12 = (bf16[32,16,128]{2,1,0:T(8,128)(2,1)S(1)}, bf16[32,16,128]{2,1,0:T(8,128)(2,1)S(1)}, u32[]{:S(2)}, u32[]{:S(2)}) collective-permute-start(bf16[32,16,128]{2,1,0:T(8,128)(2,1)S(1)} %copy-done.53), channel_id=1, source_target_pairs={{0,16},{4,20},{8,24},{12,28},{16,0},{20,4},{24,8},{28,12},{1,17},{... | collective-permute-start | bytes 393224 | tf_op jit(solution)/shard_map/ppermute | solution.py:348
  71.6 4.9 %collective-permute-start.13 = (bf16[32,16,128]{2,1,0:T(8,128)(2,1)S(1)}, bf16[32,16,128]{2,1,0:T(8,128)(2,1)S(1)}, u32[]{:S(2)}, u32[]{:S(2)}) collective-permute-start(bf16[32,16,128]{2,1,0:T(8,128)(2,1)S(1)} %copy-done.52), channel_id=1, source_target_pairs={{0,20},{4,16},{8,28},{12,24},{16,4},{20,0},{24,12},{28,8},{1,21},{... | collective-permute-start | bytes 393224 | tf_op jit(solution)/shard_map/ppermute | solution.py:348
  77.0 4.2 %collective-permute-start.15 = (bf16[32,16,128]{2,1,0:T(8,128)(2,1)S(1)}, bf16[32,16,128]{2,1,0:T(8,128)(2,1)S(1)}, u32[]{:S(2)}, u32[]{:S(2)}) collective-permute-start(bf16[32,16,128]{2,1,0:T(8,128)(2,1)S(1)} %copy-done.50), channel_id=1, source_target_pairs={{0,28},{4,24},{8,20},{12,16},{16,12},{20,8},{24,4},{28,0},{1,29},{... | collective-permute-start | bytes 393224 | tf_op jit(solution)/shard_map/ppermute | solution.py:348
  82.0 5.9 %forward.2 = (bf16[256,16,128]{2,1,0:T(8,128)(2,1)}, bf16[16,2,32,128]{3,2,1,0:T(8,128)(2,1)}, bf16[16,2,32,128]{3,2,1,0:T(8,128)(2,1)}, bf16[16,2,32,128]{3,2,1...) custom-call(s32[1]{0:T(128)} %bitcast.1.me_ref, ...), custom_call_target="tpu_custom_call" | custom-call | flops 1073741824 | bytes 6291456 | tf_op jit(solution)/shard_map/forward/pallas_call | solution.py:206
  87.9 2.7 %collective-permute-done.13.refs_5_ = bf16[32,16,128]{2,1,0:T(8,128)(2,1)S(1)} collective-permute-done((bf16[32,16,128]{2,1,0:T(8,128)(2,1)S(1)}, bf16[32,16,128]{2,1,0:T(8,128)(2,1)S(1)}, u32[]{:S(2)}, u32[]{:S(2)}) %collective-permute-start.13) | collective-permute-done | bytes 131104 | tf_op jit(solution)/shard_map/ppermute | solution.py:348
  91.4 2.4 %pick.3 = bf16[8,32,16,128]{3,2,1,0:T(8,128)(2,1)} custom-call(s32[8]{0:T(128)} %get-tuple-element.203.choice_ref, bf16[32,16,128]{2,1,0:T(8,128)(2,1)} %get-tuple-element.142.refs_0_, bf16[32,16,128]{2,1,0:T(8,128)(2,1)} %copy-done.31, bf16[32,16,128]{2,1,0:T(8,128)(2,1)} %copy-done.32, bf16[32,16,128]{2,1,0:T(8,128)(2,1)} %copy-done.33, ...), custom_call_target="tpu_custom_call" | custom-call | bytes 2097152 | tf_op jit(solution)/shard_map/pick/pallas_call | solution.py:401
  93.8 7.1 %all-to-all-start = ((bf16[256,16,128]{2,1,0:T(8,128)(2,1)}), bf16[256,16,128]{2,1,0:T(8,128)(2,1)S(1)}, u32[]{:S(2)}, u32[]{:S(2)}) async-start(bf16[256,16,128]{2,1,0:T(8,128)(2,1)} %bitcast.34), calls=%async_computation | async-start | bytes 2097152 | tf_op jit(solution)/shard_map/all_to_all | solution.py:428
  107.8 2.9 %collective-permute-done.33.refs_2_ = bf16[16,2,32,128]{3,2,1,0:T(8,128)(2,1)S(1)} collective-permute-done((bf16[16,2,32,128]{3,2,1,0:T(8,128)(2,1)}, bf16[16,2,32,128]{3,2,1,0:T(8,128)(2,1)S(1)}, u32[]{:S(2)}, u32[]{:S(2)}) %collective-permute-start.33) | collective-permute-done | bytes 262176 | tf_op jit(solution)/shard_map/ppermute | solution.py:348
  110.7 5.2 %collective-permute-done.34.refs_3_ = bf16[16,2,32,128]{3,2,1,0:T(8,128)(2,1)S(1)} collective-permute-done((bf16[16,2,32,128]{3,2,1,0:T(8,128)(2,1)S(1)}, bf16[16,2,32,128]{3,2,1,0:T(8,128)(2,1)S(1)}, u32[]{:S(2)}, u32[]{:S(2)}) %collective-permute-start.34) | collective-permute-done | bytes 262176 | tf_op jit(solution)/shard_map/ppermute | solution.py:348
  116.6 3.6 %middle.7 = (bf16[32,2,16,128]{3,2,1,0:T(8,128)(2,1)}, bf16[32,2,16,128]{3,2,1,0:T(8,128)(2,1)}, bf16[32,2,16,128]{3,2,1,0:T(8,128)(2,1)}, bf16[32,2,16,128]{3,2,1,0:T(8,128)(2,1)}) custom-call(s32[1]{0:T(128)} %bitcast.me_ref.grid_ref, bf16[16,2,32,128]{3,2,1,0:T(8,128)(2,1)} %get-tuple-element.134.refs_0_, bf16[16,2,32,128]{3,2,1,0:T(8,128)(2,1)} %copy-done.19, ...), custom_call_target="tpu_custom_call" | custom-call | flops 536870912 | bytes 3145728 | tf_op jit(solution)/shard_map/middle/pallas_call | solution.py:258
  122.8 4.4 %collective-permute-done.25.refs_3_ = bf16[16,2,32,128]{3,2,1,0:T(8,128)(2,1)S(1)} collective-permute-done((bf16[16,2,32,128]{3,2,1,0:T(8,128)(2,1)}, bf16[16,2,32,128]{3,2,1,0:T(8,128)(2,1)S(1)}, u32[]{:S(2)}, u32[]{:S(2)}) %collective-permute-start.25) | collective-permute-done | bytes 262176 | tf_op jit(solution)/shard_map/ppermute | solution.py:348
  127.9 3.6 %middle.4 = (bf16[32,2,16,128]{3,2,1,0:T(8,128)(2,1)}, bf16[32,2,16,128]{3,2,1,0:T(8,128)(2,1)}, bf16[32,2,16,128]{3,2,1,0:T(8,128)(2,1)}, bf16[32,2,16,128]{3,2,1,0:T(8,128)(2,1)}) custom-call(s32[1]{0:T(128)} %bitcast.me_ref.grid_ref, bf16[16,2,32,128]{3,2,1,0:T(8,128)(2,1)} %get-tuple-element.135.refs_0_, bf16[16,2,32,128]{3,2,1,0:T(8,128)(2,1)} %copy-done.17, ...), custom_call_target="tpu_custom_call" | custom-call | flops 536870912 | bytes 3145728 | tf_op jit(solution)/shard_map/middle/pallas_call | solution.py:258
  132.5 5.4 %forward.3 = (bf16[16,2,32,128]{3,2,1,0:T(8,128)(2,1)}, bf16[16,2,32,128]{3,2,1,0:T(8,128)(2,1)}, bf16[16,2,32,128]{3,2,1,0:T(8,128)(2,1)}, bf16[16,2,32,128]{3,...) custom-call(s32[1]{0:T(128)} %bitcast.1.me_ref, ...), custom_call_target="tpu_custom_call" | custom-call | flops 1073741824 | bytes 6291456 | tf_op jit(solution)/shard_map/forward/pallas_call | solution.py:206
  142.1 5.4 %collective-permute-done.27.refs_2_ = bf16[16,2,32,128]{3,2,1,0:T(8,128)(2,1)S(1)} collective-permute-done((bf16[16,2,32,128]{3,2,1,0:T(8,128)(2,1)}, bf16[16,2,32,128]{3,2,1,0:T(8,128)(2,1)S(1)}, u32[]{:S(2)}, u32[]{:S(2)}) %collective-permute-start.27) | collective-permute-done | bytes 262176 | tf_op jit(solution)/shard_map/ppermute | solution.py:348
  149.6 3.5 %collective-permute-done.30.refs_2_ = bf16[16,2,32,128]{3,2,1,0:T(8,128)(2,1)S(1)} collective-permute-done((bf16[16,2,32,128]{3,2,1,0:T(8,128)(2,1)}, bf16[16,2,32,128]{3,2,1,0:T(8,128)(2,1)S(1)}, u32[]{:S(2)}, u32[]{:S(2)}) %collective-permute-start.30) | collective-permute-done | bytes 262176 | tf_op jit(solution)/shard_map/ppermute | solution.py:348
  155.1 3.2 %collective-permute-done.31.refs_3_ = bf16[16,2,32,128]{3,2,1,0:T(8,128)(2,1)S(1)} collective-permute-done((bf16[16,2,32,128]{3,2,1,0:T(8,128)(2,1)}, bf16[16,2,32,128]{3,2,1,0:T(8,128)(2,1)S(1)}, u32[]{:S(2)}, u32[]{:S(2)}) %collective-permute-start.31) | collective-permute-done | bytes 262176 | tf_op jit(solution)/shard_map/ppermute | solution.py:348
  160.5 3.7 %middle.6 = (bf16[16,2,16,128]{3,2,1,0:T(8,128)(2,1)}, bf16[16,2,16,128]{3,2,1,0:T(8,128)(2,1)}, bf16[16,2,16,128]{3,2,1,0:T(8,128)(2,1)}, bf16[16,2,16,128]{3,2...) custom-call(s32[1]{0:T(128)} %bitcast.me_ref.grid_ref, ...), custom_call_target="tpu_custom_call" | custom-call | flops 536870912 | bytes 3145728 | tf_op jit(solution)/shard_map/middle/pallas_call | solution.py:258
  164.8 3.6 %middle.5 = (bf16[32,2,16,128]{3,2,1,0:T(8,128)(2,1)}, bf16[32,2,16,128]{3,2,1,0:T(8,128)(2,1)}, bf16[32,2,16,128]{3,2,1,0:T(8,128)(2,1)}, bf16[32,2,16,128]{3,2,1,0:T(8,128)(2,1)}) custom-call(s32[1]{0:T(128)} %bitcast.me_ref.grid_ref, bf16[16,2,32,128]{3,2,1,0:T(8,128)(2,1)} %get-tuple-element.155.refs_0_, bf16[16,2,32,128]{3,2,1,0:T(8,128)(2,1)} %copy-done.13, ...), custom_call_target="tpu_custom_call" | custom-call | flops 536870912 | bytes 3145728 | tf_op jit(solution)/shard_map/middle/pallas_call | solution.py:258
  171.8 3.8 %collective-permute-done.39.refs_5_ = bf16[32,2,16,128]{3,2,1,0:T(8,128)(2,1)S(1)} collective-permute-done((bf16[32,2,16,128]{3,2,1,0:T(8,128)(2,1)}, bf16[32,2,16,128]{3,2,1,0:T(8,128)(2,1)S(1)}, u32[]{:S(2)}, u32[]{:S(2)}) %collective-permute-start.39) | collective-permute-done | bytes 262176 | tf_op jit(solution)/shard_map/ppermute | solution.py:348
  175.6 5.3 %collective-permute-done.40.refs_7_ = bf16[32,2,16,128]{3,2,1,0:T(8,128)(2,1)S(1)} collective-permute-done((bf16[32,2,16,128]{3,2,1,0:T(8,128)(2,1)}, bf16[32,2,16,128]{3,2,1,0:T(8,128)(2,1)S(1)}, u32[]{:S(2)}, u32[]{:S(2)}) %collective-permute-start.40) | collective-permute-done | bytes 262176 | tf_op jit(solution)/shard_map/ppermute | solution.py:348
  185.4 4.3 %backward.4.refs_12_ = f32[2,32,128,128]{3,2,1,0:T(8,128)} custom-call(bf16[32,2,16,128]{3,2,1,0:T(8,128)(2,1)} %get-tuple-element.176.refs_0_, bf16[32,2,16,128]{3,2,1,0:T(8,128)(2,1)} %get-tuple-element.150.refs_1_, bf16[32,2,16,128]{3,2,1,0:T(8,128)(2,1)} %copy-done.4, bf16[32,2,16,128]{3,2,1,0:T(8,128)(2,1)} %copy-done.8, ...), custom_call_target="tpu_custom_call" | custom-call | flops 536870912 | bytes 6291456 | tf_op jit(solution)/shard_map/backward/pallas_call | solution.py:325
  189.7 4.3 %backward.5.refs_12_ = f32[2,32,128,128]{3,2,1,0:T(8,128)} custom-call(bf16[32,2,16,128]{3,2,1,0:T(8,128)(2,1)} %get-tuple-element.176.refs_0_, bf16[32,2,16,128]{3,2,1,0:T(8,128)(2,1)} %get-tuple-element.150.refs_1_, bf16[32,2,16,128]{3,2,1,0:T(8,128)(2,1)} %copy-done.4, bf16[32,2,16,128]{3,2,1,0:T(8,128)(2,1)} %copy-done.8, ...), custom_call_target="tpu_custom_call", output_to_operand_aliasing={{}: (12, {})} | custom-call | flops 536870912 | bytes 6291456 | tf_op jit(solution)/shard_map/backward/pallas_call | solution.py:325
  199.5 4.4 %backward.6.refs_12_ = f32[2,32,128,128]{3,2,1,0:T(8,128)} custom-call(bf16[32,2,16,128]{3,2,1,0:T(8,128)(2,1)} %get-tuple-element.159.refs_0_, bf16[16,2,16,128]{3,2,1,0:T(8,128)(2,1)} %get-tuple-element.172.refs_1_, bf16[32,2,16,128]{3,2,1,0:T(8,128)(2,1)} %copy-done.7, bf16[16,2,16,128]{3,2,1,0:T(8,128)(2,1)} %copy-done.25, ...), custom_call_target="tpu_custom_call", output_to_operand_aliasing={{}: (12, {})} | custom-call | flops 536870912 | bytes 6291456 | tf_op jit(solution)/shard_map/backward/pallas_call | solution.py:325
  205.6 4.4 %backward.7 = f32[2,32,128,128]{3,2,1,0:T(8,128)} custom-call(bf16[32,2,16,128]{3,2,1,0:T(8,128)(2,1)} %get-tuple-element.159.refs_0_, bf16[16,2,16,128]{3,2,1,0:T(8,128)(2,1)} %get-tuple-element.181.refs_1_, bf16[32,2,16,128]{3,2,1,0:T(8,128)(2,1)} %copy-done.7, bf16[16,2,16,128]{3,2,1,0:T(8,128)(2,1)} %copy-done.28, ...), custom_call_target="tpu_custom_call", output_to_operand_aliasing={{}: (12, {})} | custom-call | flops 536870912 | bytes 6291456 | tf_op jit(solution)/shard_map/backward/pallas_call | solution.py:325
  (248 shorter events, 68.1 us)
Async XLA Ops:
  4.6 42.3 %collective-permute-start.7 = (bf16[128,2048]{1,0:T(8,128)(2,1)}, bf16[128,2048]{1,0:T(8,128)(2,1)S(1)}, u32[]{:S(2)}, u32[]{:S(2)}) collective-permute-start(bf16[128,2048]{1,0:T(8,128)(2,1)} %get-tuple-element.107), channel_id=1, source_target_pairs={{0,3},{1,2},{2,1},{3,0},{4,7},{5,6},{6,5},{7,4},{8,11},{9,10},{10,... | collective-permute-start | bytes 1572872 | tf_op jit(solution)/shard_map/ppermute | solution.py:445
  11.6 16.5 %collective-permute-start.5 = (bf16[32,16,128]{2,1,0:T(8,128)(2,1)S(1)}, bf16[32,16,128]{2,1,0:T(8,128)(2,1)S(1)}, u32[]{:S(2)}, u32[]{:S(2)}) collective-permute-start(bf16[32,16,128]{2,1,0:T(8,128)(2,1)S(1)} %get-tuple-element.189), channel_id=1, source_target_pairs={{0,24},{4,28},{8,16},{12,20},{16,8},{20,12},{24,0},{28,4},{1,25},{... | collective-permute-start | bytes 393224 | tf_op jit(solution)/shard_map/ppermute | solution.py:348
  11.8 20.5 %collective-permute-start.4 = (bf16[32,16,128]{2,1,0:T(8,128)(2,1)S(1)}, bf16[32,16,128]{2,1,0:T(8,128)(2,1)S(1)}, u32[]{:S(2)}, u32[]{:S(2)}) collective-permute-start(bf16[32,16,128]{2,1,0:T(8,128)(2,1)S(1)} %get-tuple-element.190), channel_id=1, source_target_pairs={{0,20},{4,16},{8,28},{12,24},{16,4},{20,0},{24,12},{28,8},{1,21},{... | collective-permute-start | bytes 393224 | tf_op jit(solution)/shard_map/ppermute | solution.py:348
  12.5 22.3 %collective-permute-start.3 = (bf16[32,16,128]{2,1,0:T(8,128)(2,1)S(1)}, bf16[32,16,128]{2,1,0:T(8,128)(2,1)S(1)}, u32[]{:S(2)}, u32[]{:S(2)}) collective-permute-start(bf16[32,16,128]{2,1,0:T(8,128)(2,1)S(1)} %get-tuple-element.191), channel_id=1, source_target_pairs={{0,16},{4,20},{8,24},{12,28},{16,0},{20,4},{24,8},{28,12},{1,17},{... | collective-permute-start | bytes 393224 | tf_op jit(solution)/shard_map/ppermute | solution.py:348
  16.0 23.0 %collective-permute-start.2 = (bf16[32,16,128]{2,1,0:T(8,128)(2,1)S(1)}, bf16[32,16,128]{2,1,0:T(8,128)(2,1)S(1)}, u32[]{:S(2)}, u32[]{:S(2)}) collective-permute-start(bf16[32,16,128]{2,1,0:T(8,128)(2,1)S(1)} %get-tuple-element.192), channel_id=1, source_target_pairs={{0,12},{4,8},{8,4},{12,0},{16,28},{20,24},{24,20},{28,16},{1,13},{... | collective-permute-start | bytes 393224 | tf_op jit(solution)/shard_map/ppermute | solution.py:348
  42.2 16.4 %collective-permute-start.16 = (bf16[32,16,128]{2,1,0:T(8,128)(2,1)}, bf16[32,16,128]{2,1,0:T(8,128)(2,1)S(1)}, u32[]{:S(2)}, u32[]{:S(2)}) collective-permute-start(bf16[32,16,128]{2,1,0:T(8,128)(2,1)} %get-tuple-element.118), channel_id=1, source_target_pairs={{0,4},{4,0},{8,12},{12,8},{16,20},{20,16},{24,28},{28,24},{1,5},{5... | collective-permute-start | bytes 393224 | tf_op jit(solution)/shard_map/ppermute | solution.py:348
  43.3 17.8 %collective-permute-start.17 = (bf16[32,16,128]{2,1,0:T(8,128)(2,1)}, bf16[32,16,128]{2,1,0:T(8,128)(2,1)S(1)}, u32[]{:S(2)}, u32[]{:S(2)}) collective-permute-start(bf16[32,16,128]{2,1,0:T(8,128)(2,1)} %get-tuple-element.119), channel_id=1, source_target_pairs={{0,8},{4,12},{8,0},{12,4},{16,24},{20,28},{24,16},{28,20},{1,9},{5... | collective-permute-start | bytes 393224 | tf_op jit(solution)/shard_map/ppermute | solution.py:348
  43.3 19.6 %collective-permute-start.18 = (bf16[32,16,128]{2,1,0:T(8,128)(2,1)}, bf16[32,16,128]{2,1,0:T(8,128)(2,1)S(1)}, u32[]{:S(2)}, u32[]{:S(2)}) collective-permute-start(bf16[32,16,128]{2,1,0:T(8,128)(2,1)} %get-tuple-element.120), channel_id=1, source_target_pairs={{0,12},{4,8},{8,4},{12,0},{16,28},{20,24},{24,20},{28,16},{1,13},{... | collective-permute-start | bytes 393224 | tf_op jit(solution)/shard_map/ppermute | solution.py:348
  45.8 18.3 %collective-permute-start.19 = (bf16[32,16,128]{2,1,0:T(8,128)(2,1)}, bf16[32,16,128]{2,1,0:T(8,128)(2,1)S(1)}, u32[]{:S(2)}, u32[]{:S(2)}) collective-permute-start(bf16[32,16,128]{2,1,0:T(8,128)(2,1)} %get-tuple-element.121), channel_id=1, source_target_pairs={{0,16},{4,20},{8,24},{12,28},{16,0},{20,4},{24,8},{28,12},{1,17},{... | collective-permute-start | bytes 393224 | tf_op jit(solution)/shard_map/ppermute | solution.py:348
  46.9 17.9 %collective-permute-start.20 = (bf16[32,16,128]{2,1,0:T(8,128)(2,1)}, bf16[32,16,128]{2,1,0:T(8,128)(2,1)S(1)}, u32[]{:S(2)}, u32[]{:S(2)}) collective-permute-start(bf16[32,16,128]{2,1,0:T(8,128)(2,1)} %get-tuple-element.122), channel_id=1, source_target_pairs={{0,20},{4,16},{8,28},{12,24},{16,4},{20,0},{24,12},{28,8},{1,21},{... | collective-permute-start | bytes 393224 | tf_op jit(solution)/shard_map/ppermute | solution.py:348
  64.8 23.1 %collective-permute-start.11 = (bf16[32,16,128]{2,1,0:T(8,128)(2,1)S(1)}, bf16[32,16,128]{2,1,0:T(8,128)(2,1)S(1)}, u32[]{:S(2)}, u32[]{:S(2)}) collective-permute-start(bf16[32,16,128]{2,1,0:T(8,128)(2,1)S(1)} %copy-done.54), channel_id=1, source_target_pairs={{0,12},{4,8},{8,4},{12,0},{16,28},{20,24},{24,20},{28,16},{1,13},{... | collective-permute-start | bytes 393224 | tf_op jit(solution)/shard_map/ppermute | solution.py:348
  67.2 20.7 %collective-permute-start.12 = (bf16[32,16,128]{2,1,0:T(8,128)(2,1)S(1)}, bf16[32,16,128]{2,1,0:T(8,128)(2,1)S(1)}, u32[]{:S(2)}, u32[]{:S(2)}) collective-permute-start(bf16[32,16,128]{2,1,0:T(8,128)(2,1)S(1)} %copy-done.53), channel_id=1, source_target_pairs={{0,16},{4,20},{8,24},{12,28},{16,0},{20,4},{24,8},{28,12},{1,17},{... | collective-permute-start | bytes 393224 | tf_op jit(solution)/shard_map/ppermute | solution.py:348
  71.6 19.0 %collective-permute-start.13 = (bf16[32,16,128]{2,1,0:T(8,128)(2,1)S(1)}, bf16[32,16,128]{2,1,0:T(8,128)(2,1)S(1)}, u32[]{:S(2)}, u32[]{:S(2)}) collective-permute-start(bf16[32,16,128]{2,1,0:T(8,128)(2,1)S(1)} %copy-done.52), channel_id=1, source_target_pairs={{0,20},{4,16},{8,28},{12,24},{16,4},{20,0},{24,12},{28,8},{1,21},{... | collective-permute-start | bytes 393224 | tf_op jit(solution)/shard_map/ppermute | solution.py:348
  76.5 14.1 %collective-permute-start.14 = (bf16[32,16,128]{2,1,0:T(8,128)(2,1)S(1)}, bf16[32,16,128]{2,1,0:T(8,128)(2,1)S(1)}, u32[]{:S(2)}, u32[]{:S(2)}) collective-permute-start(bf16[32,16,128]{2,1,0:T(8,128)(2,1)S(1)} %copy-done.51), channel_id=1, source_target_pairs={{0,24},{4,28},{8,16},{12,20},{16,8},{20,12},{24,0},{28,4},{1,25},{... | collective-permute-start | bytes 393224 | tf_op jit(solution)/shard_map/ppermute | solution.py:348
  93.8 37.7 %all-to-all-start = ((bf16[256,16,128]{2,1,0:T(8,128)(2,1)}), bf16[256,16,128]{2,1,0:T(8,128)(2,1)S(1)}, u32[]{:S(2)}, u32[]{:S(2)}) async-start(bf16[256,16,128]{2,1,0:T(8,128)(2,1)} %bitcast.34), calls=%async_computation | async-start | bytes 2097152 | tf_op jit(solution)/shard_map/all_to_all | solution.py:428
  104.8 17.9 %collective-permute-start.23 = (bf16[16,2,32,128]{3,2,1,0:T(8,128)(2,1)}, bf16[16,2,32,128]{3,2,1,0:T(8,128)(2,1)S(1)}, u32[]{:S(2)}, u32[]{:S(2)}) collective-permute-start(bf16[16,2,32,128]{3,2,1,0:T(8,128)(2,1)} %get-tuple-element.137), channel_id=1, source_target_pairs={{0,1},{1,0},{2,3},{3,2},{4,5},{5,4},{6,7},{7,6},{8,9},{9,8},{10,11... | collective-permute-start | bytes 786440 | tf_op jit(solution)/shard_map/ppermute | solution.py:348
  104.9 17.8 %collective-permute-start.24 = (bf16[16,2,32,128]{3,2,1,0:T(8,128)(2,1)}, bf16[16,2,32,128]{3,2,1,0:T(8,128)(2,1)S(1)}, u32[]{:S(2)}, u32[]{:S(2)}) collective-permute-start(bf16[16,2,32,128]{3,2,1,0:T(8,128)(2,1)} %get-tuple-element.139), channel_id=1, source_target_pairs={{0,2},{1,3},{2,0},{3,1},{4,6},{5,7},{6,4},{7,5},{8,10},{9,11},{10,... | collective-permute-start | bytes 786440 | tf_op jit(solution)/shard_map/ppermute | solution.py:348
  106.9 20.3 %collective-permute-start.25 = (bf16[16,2,32,128]{3,2,1,0:T(8,128)(2,1)}, bf16[16,2,32,128]{3,2,1,0:T(8,128)(2,1)S(1)}, u32[]{:S(2)}, u32[]{:S(2)}) collective-permute-start(bf16[16,2,32,128]{3,2,1,0:T(8,128)(2,1)} %get-tuple-element.141), channel_id=1, source_target_pairs={{0,3},{1,2},{2,1},{3,0},{4,7},{5,6},{6,5},{7,4},{8,11},{9,10},{10,... | collective-permute-start | bytes 786440 | tf_op jit(solution)/shard_map/ppermute | solution.py:348
  120.2 19.9 %collective-permute-start.35 = (bf16[32,2,16,128]{3,2,1,0:T(8,128)(2,1)}, bf16[32,2,16,128]{3,2,1,0:T(8,128)(2,1)S(1)}, u32[]{:S(2)}, u32[]{:S(2)}) collective-permute-start(bf16[32,2,16,128]{3,2,1,0:T(8,128)(2,1)} %get-tuple-element.169), channel_id=1, source_target_pairs={{0,1},{1,0},{2,3},{3,2},{4,5},{5,4},{6,7},{7,6},{8,9},{9,8},{10,11... | collective-permute-start | bytes 786440 | tf_op jit(solution)/shard_map/ppermute | solution.py:348
  120.7 19.5 %collective-permute-start.36 = (bf16[32,2,16,128]{3,2,1,0:T(8,128)(2,1)}, bf16[32,2,16,128]{3,2,1,0:T(8,128)(2,1)S(1)}, u32[]{:S(2)}, u32[]{:S(2)}) collective-permute-start(bf16[32,2,16,128]{3,2,1,0:T(8,128)(2,1)} %get-tuple-element.170), channel_id=1, source_target_pairs={{0,2},{1,3},{2,0},{3,1},{4,6},{5,7},{6,4},{7,5},{8,10},{9,11},{10,... | collective-permute-start | bytes 786440 | tf_op jit(solution)/shard_map/ppermute | solution.py:348
  140.3 18.1 %collective-permute-start.31 = (bf16[16,2,32,128]{3,2,1,0:T(8,128)(2,1)}, bf16[16,2,32,128]{3,2,1,0:T(8,128)(2,1)S(1)}, u32[]{:S(2)}, u32[]{:S(2)}) collective-permute-start(bf16[16,2,32,128]{3,2,1,0:T(8,128)(2,1)} %get-tuple-element.163), channel_id=1, source_target_pairs={{0,3},{1,2},{2,1},{3,0},{4,7},{5,6},{6,5},{7,4},{8,11},{9,10},{10,... | collective-permute-start | bytes 786440 | tf_op jit(solution)/shard_map/ppermute | solution.py:348
  142.0 22.1 %collective-permute-start.28 = (bf16[16,2,32,128]{3,2,1,0:T(8,128)(2,1)}, bf16[16,2,32,128]{3,2,1,0:T(8,128)(2,1)S(1)}, u32[]{:S(2)}, u32[]{:S(2)}) collective-permute-start(bf16[16,2,32,128]{3,2,1,0:T(8,128)(2,1)} %get-tuple-element.158), channel_id=1, source_target_pairs={{0,3},{1,2},{2,1},{3,0},{4,7},{5,6},{6,5},{7,4},{8,11},{9,10},{10,... | collective-permute-start | bytes 786440 | tf_op jit(solution)/shard_map/ppermute | solution.py:348
  147.5 22.0 %collective-permute-start.37 = (bf16[32,2,16,128]{3,2,1,0:T(8,128)(2,1)S(1)}, bf16[32,2,16,128]{3,2,1,0:T(8,128)(2,1)S(1)}, u32[]{:S(2)}, u32[]{:S(2)}) collective-permute-start(bf16[32,2,16,128]{3,2,1,0:T(8,128)(2,1)S(1)} %copy-done.47), channel_id=1, source_target_pairs={{0,3},{1,2},{2,1},{3,0},{4,7},{5,6},{6,5},{7,4},{8,11},{9,10},{10,... | collective-permute-start | bytes 786440 | tf_op jit(solution)/shard_map/ppermute | solution.py:348
  147.5 22.3 %collective-permute-start.38 = (bf16[32,2,16,128]{3,2,1,0:T(8,128)(2,1)}, bf16[32,2,16,128]{3,2,1,0:T(8,128)(2,1)S(1)}, u32[]{:S(2)}, u32[]{:S(2)}) collective-permute-start(bf16[32,2,16,128]{3,2,1,0:T(8,128)(2,1)} %get-tuple-element.151), channel_id=1, source_target_pairs={{0,1},{1,0},{2,3},{3,2},{4,5},{5,4},{6,7},{7,6},{8,9},{9,8},{10,11... | collective-permute-start | bytes 786440 | tf_op jit(solution)/shard_map/ppermute | solution.py:348
  153.1 22.5 %collective-permute-start.39 = (bf16[32,2,16,128]{3,2,1,0:T(8,128)(2,1)}, bf16[32,2,16,128]{3,2,1,0:T(8,128)(2,1)S(1)}, u32[]{:S(2)}, u32[]{:S(2)}) collective-permute-start(bf16[32,2,16,128]{3,2,1,0:T(8,128)(2,1)} %get-tuple-element.152), channel_id=1, source_target_pairs={{0,2},{1,3},{2,0},{3,1},{4,6},{5,7},{6,4},{7,5},{8,10},{9,11},{10,... | collective-permute-start | bytes 786440 | tf_op jit(solution)/shard_map/ppermute | solution.py:348
  158.4 22.5 %collective-permute-start.40 = (bf16[32,2,16,128]{3,2,1,0:T(8,128)(2,1)}, bf16[32,2,16,128]{3,2,1,0:T(8,128)(2,1)S(1)}, u32[]{:S(2)}, u32[]{:S(2)}) collective-permute-start(bf16[32,2,16,128]{3,2,1,0:T(8,128)(2,1)} %get-tuple-element.153), channel_id=1, source_target_pairs={{0,3},{1,2},{2,1},{3,0},{4,7},{5,6},{6,5},{7,4},{8,11},{9,10},{10,... | collective-permute-start | bytes 786440 | tf_op jit(solution)/shard_map/ppermute | solution.py:348
  164.1 17.3 %collective-permute-start.47 = (bf16[16,2,16,128]{3,2,1,0:T(8,128)(2,1)}, bf16[16,2,16,128]{3,2,1,0:T(8,128)(2,1)S(1)}, u32[]{:S(2)}, u32[]{:S(2)}) collective-permute-start(bf16[16,2,16,128]{3,2,1,0:T(8,128)(2,1)} %get-tuple-element.173), channel_id=1, source_target_pairs={{0,1},{1,0},{2,3},{3,2},{4,5},{5,4},{6,7},{7,6},{8,9},{9,8},{10,11... | collective-permute-start | bytes 393224 | tf_op jit(solution)/shard_map/ppermute | solution.py:348
  169.5 28.8 %collective-permute-start.41 = (bf16[32,2,16,128]{3,2,1,0:T(8,128)(2,1)}, bf16[32,2,16,128]{3,2,1,0:T(8,128)(2,1)S(1)}, u32[]{:S(2)}, u32[]{:S(2)}) collective-permute-start(bf16[32,2,16,128]{3,2,1,0:T(8,128)(2,1)} %get-tuple-element.182), channel_id=1, source_target_pairs={{0,1},{1,0},{2,3},{3,2},{4,5},{5,4},{6,7},{7,6},{8,9},{9,8},{10,11... | collective-permute-start | bytes 786440 | tf_op jit(solution)/shard_map/ppermute | solution.py:348
  169.8 28.9 %collective-permute-start.43 = (bf16[32,2,16,128]{3,2,1,0:T(8,128)(2,1)}, bf16[32,2,16,128]{3,2,1,0:T(8,128)(2,1)S(1)}, u32[]{:S(2)}, u32[]{:S(2)}) collective-permute-start(bf16[32,2,16,128]{3,2,1,0:T(8,128)(2,1)} %get-tuple-element.184), channel_id=1, source_target_pairs={{0,2},{1,3},{2,0},{3,1},{4,6},{5,7},{6,4},{7,5},{8,10},{9,11},{10,... | collective-permute-start | bytes 786440 | tf_op jit(solution)/shard_map/ppermute | solution.py:348
  175.6 23.1 %collective-permute-start.45 = (bf16[32,2,16,128]{3,2,1,0:T(8,128)(2,1)}, bf16[32,2,16,128]{3,2,1,0:T(8,128)(2,1)S(1)}, u32[]{:S(2)}, u32[]{:S(2)}) collective-permute-start(bf16[32,2,16,128]{3,2,1,0:T(8,128)(2,1)} %get-tuple-element.186), channel_id=1, source_target_pairs={{0,3},{1,2},{2,1},{3,0},{4,7},{5,6},{6,5},{7,4},{8,11},{9,10},{10,... | collective-permute-start | bytes 786440 | tf_op jit(solution)/shard_map/ppermute | solution.py:348
  180.8 14.4 %collective-permute-start.48 = (bf16[16,2,16,128]{3,2,1,0:T(8,128)(2,1)}, bf16[16,2,16,128]{3,2,1,0:T(8,128)(2,1)S(1)}, u32[]{:S(2)}, u32[]{:S(2)}) collective-permute-start(bf16[16,2,16,128]{3,2,1,0:T(8,128)(2,1)} %get-tuple-element.174), channel_id=1, source_target_pairs={{0,2},{1,3},{2,0},{3,1},{4,6},{5,7},{6,4},{7,5},{8,10},{9,11},{10,... | collective-permute-start | bytes 393224 | tf_op jit(solution)/shard_map/ppermute | solution.py:348
  181.4 15.4 %collective-permute-start.49 = (bf16[16,2,16,128]{3,2,1,0:T(8,128)(2,1)}, bf16[16,2,16,128]{3,2,1,0:T(8,128)(2,1)S(1)}, u32[]{:S(2)}, u32[]{:S(2)}) collective-permute-start(bf16[16,2,16,128]{3,2,1,0:T(8,128)(2,1)} %get-tuple-element.175), channel_id=1, source_target_pairs={{0,3},{1,2},{2,1},{3,0},{4,7},{5,6},{6,5},{7,4},{8,11},{9,10},{10,... | collective-permute-start | bytes 393224 | tf_op jit(solution)/shard_map/ppermute | solution.py:348
  (89 other events, 1015.2 us)

commit v4 on v3

--- a/solution.py
+++ b/solution.py
@@ -428,7 +428,10 @@
         return lax.all_to_all(value, "band", split_axis=0, concat_axis=0, tiled=True)
 
     def slotwise(sent):
-        return [shift(piece, "band", bands, slot) for slot, piece in enumerate(sent)]
+        moved = []
+        for slot, piece in enumerate(sent):
+            moved.append(shift(piece, "band", bands, slot))
+        return moved
 
     my_grid = me.astype(jnp.int32).reshape(1)
     cols = col_index.reshape(1, -1)

time: 211 us -> 211 us (level)
  no operation moved by 1% of the time
where the time goes in v4:
time: 211 us; the launch traced here: 210 us
  starting transfers between devices  86.8 us (41%)
  Pallas kernels  61.9 us (29%)
  waiting for transfers between devices  45.4 us (22%)
  local copies, waits for them, and re-layouts  12.6 us (6%)
    ppermute x48, starting transfers between devices, shift(): lax.ppermute(value, axis, [(i, i ^ mask) for i in range(size)])  75.9 us
    ppermute x48, waiting for transfers between devices, shift(): lax.ppermute(value, axis, [(i, i ^ mask) for i in range(size)])  45.4 us
    pallas_call x4, Pallas kernels, backward(): pl.pallas_call(functools.partial(backward_kernel, number, has_total), gri...  17.4 us
    pallas_call x4, Pallas kernels, middle(): pl.pallas_call(functools.partial(middle_kernel, groups, halves), grid=(1,...  14.5 us
    pallas_call x2, Pallas kernels, forward(): pl.pallas_call(functools.partial(forward_kernel, parts, half * count, cut...  11.3 us
    pallas_call x1, Pallas kernels, expand(): pl.pallas_call(functools.partial(expand_kernel, scale, groups, rows * len...  9.28 us
    all_to_all x1, starting transfers between devices, exchange(): lax.all_to_all(value, 'band', split_axis=0, concat_axis=0, tiled=True)  7.14 us
    unnamed x140, local copies, waits for them, and re-layouts  5.77 us
  transfers between devices with their start and end apart: 51, of which 17 were waited for; matrix products, arithmetic and copies ran while one was open for 3% of the time, Pallas kernels for 25%

profile of v4, /device:TPU:0, one launch (start us, length us, event | category | flops | bytes accessed | tf_op | source)
XLA Modules:
  0.0 210.0 jit_solution(2601742720516270674)
XLA Ops:
  2.2 2.4 %mirror.1 = (bf16[128,2048]{1,0:T(8,128)(2,1)}, bf16[128,128]{1,0:T(8,128)(2,1)}) custom-call(s32[1]{0:T(128)} %bitcast.me_ref.grid_ref, f32[128,2048]{1,0:T(8,128)} %own_ref.2, s32[1,8192]{1,0:T(1,128)} %bitcast.40), custom_call_target="tpu_custom_call" | custom-call | flops 67108864 | bytes 1572864 | tf_op jit(solution)/shard_map/mirror/pallas_call | solution.py:86
  4.6 2.4 %collective-permute-start.7 = (bf16[128,2048]{1,0:T(8,128)(2,1)}, bf16[128,2048]{1,0:T(8,128)(2,1)S(1)}, u32[]{:S(2)}, u32[]{:S(2)}) collective-permute-start(bf16[128,2048]{1,0:T(8,128)(2,1)} %get-tuple-element.107), channel_id=1, source_target_pairs={{0,3},{1,2},{2,1},{3,0},{4,7},{5,6},{6,5},{7,4},{8,11},{9,10},{10,... | collective-permute-start | bytes 1572872 | tf_op jit(solution)/shard_map/ppermute | solution.py:448
  7.0 4.6 %collective-permute-start.6 = (bf16[32,16,128]{2,1,0:T(8,128)(2,1)S(1)}, bf16[32,16,128]{2,1,0:T(8,128)(2,1)S(1)}, u32[]{:S(2)}, u32[]{:S(2)}) collective-permute-start(bf16[32,16,128]{2,1,0:T(8,128)(2,1)S(1)} %get-tuple-element.188), channel_id=1, source_target_pairs={{0,28},{4,24},{8,20},{12,16},{16,12},{20,8},{24,4},{28,0},{1,29},{... | collective-permute-start | bytes 393224 | tf_op jit(solution)/shard_map/ppermute | solution.py:348
  16.0 12.0 %collective-permute-start.2 = (bf16[32,16,128]{2,1,0:T(8,128)(2,1)S(1)}, bf16[32,16,128]{2,1,0:T(8,128)(2,1)S(1)}, u32[]{:S(2)}, u32[]{:S(2)}) collective-permute-start(bf16[32,16,128]{2,1,0:T(8,128)(2,1)S(1)} %get-tuple-element.192), channel_id=1, source_target_pairs={{0,12},{4,8},{8,4},{12,0},{16,28},{20,24},{24,20},{28,16},{1,13},{... | collective-permute-start | bytes 393224 | tf_op jit(solution)/shard_map/ppermute | solution.py:348
  46.9 2.5 %collective-permute-start.20 = (bf16[32,16,128]{2,1,0:T(8,128)(2,1)}, bf16[32,16,128]{2,1,0:T(8,128)(2,1)S(1)}, u32[]{:S(2)}, u32[]{:S(2)}) collective-permute-start(bf16[32,16,128]{2,1,0:T(8,128)(2,1)} %get-tuple-element.122), channel_id=1, source_target_pairs={{0,20},{4,16},{8,28},{12,24},{16,4},{20,0},{24,12},{28,8},{1,21},{... | collective-permute-start | bytes 393224 | tf_op jit(solution)/shard_map/ppermute | solution.py:348
  49.3 9.3 %expand.1.refs_4_ = f32[32,128,128]{2,1,0:T(8,128)} custom-call(s32[1]{0:T(128)} %bitcast.me_ref.grid_ref, f32[128,2048]{1,0:T(8,128)} %own_ref.2, bf16[128,2048]{1,0:T(8,128)(2,1)} %copy-done.46, bf16[128,128]{1,0:T(8,128)(2,1)} %copy-done.69, s32[1,8192]{1,0:T(1,128)} %bitcast.41), custom_call_target="tpu_custom_call" | custom-call | flops 4294967296 | bytes 3145728 | tf_op jit(solution)/shard_map/expand/pallas_call | solution.py:131
  58.6 2.5 %collective-permute-start.21 = (bf16[32,16,128]{2,1,0:T(8,128)(2,1)S(1)}, bf16[32,16,128]{2,1,0:T(8,128)(2,1)S(1)}, u32[]{:S(2)}, u32[]{:S(2)}) collective-permute-start(bf16[32,16,128]{2,1,0:T(8,128)(2,1)S(1)} %copy-done.67), channel_id=1, source_target_pairs={{0,24},{4,28},{8,16},{12,20},{16,8},{20,12},{24,0},{28,4},{1,25},{... | collective-permute-start | bytes 393224 | tf_op jit(solution)/shard_map/ppermute | solution.py:348
  64.8 2.4 %collective-permute-start.11 = (bf16[32,16,128]{2,1,0:T(8,128)(2,1)S(1)}, bf16[32,16,128]{2,1,0:T(8,128)(2,1)S(1)}, u32[]{:S(2)}, u32[]{:S(2)}) collective-permute-start(bf16[32,16,128]{2,1,0:T(8,128)(2,1)S(1)} %copy-done.54), channel_id=1, source_target_pairs={{0,12},{4,8},{8,4},{12,0},{16,28},{20,24},{24,20},{28,16},{1,13},{... | collective-permute-start | bytes 393224 | tf_op jit(solution)/shard_map/ppermute | solution.py:348
  67.2 4.4 %collective-permute-start.12 = (bf16[32,16,128]{2,1,0:T(8,128)(2,1)S(1)}, bf16[32,16,128]{2,1,0:T(8,128)(2,1)S(1)}, u32[]{:S(2)}, u32[]{:S(2)}) collective-permute-start(bf16[32,16,128]{2,1,0:T(8,128)(2,1)S(1)} %copy-done.53), channel_id=1, source_target_pairs={{0,16},{4,20},{8,24},{12,28},{16,0},{20,4},{24,8},{28,12},{1,17},{... | collective-permute-start | bytes 393224 | tf_op jit(solution)/shard_map/ppermute | solution.py:348
  71.6 4.9 %collective-permute-start.13 = (bf16[32,16,128]{2,1,0:T(8,128)(2,1)S(1)}, bf16[32,16,128]{2,1,0:T(8,128)(2,1)S(1)}, u32[]{:S(2)}, u32[]{:S(2)}) collective-permute-start(bf16[32,16,128]{2,1,0:T(8,128)(2,1)S(1)} %copy-done.52), channel_id=1, source_target_pairs={{0,20},{4,16},{8,28},{12,24},{16,4},{20,0},{24,12},{28,8},{1,21},{... | collective-permute-start | bytes 393224 | tf_op jit(solution)/shard_map/ppermute | solution.py:348
  77.0 4.2 %collective-permute-start.15 = (bf16[32,16,128]{2,1,0:T(8,128)(2,1)S(1)}, bf16[32,16,128]{2,1,0:T(8,128)(2,1)S(1)}, u32[]{:S(2)}, u32[]{:S(2)}) collective-permute-start(bf16[32,16,128]{2,1,0:T(8,128)(2,1)S(1)} %copy-done.50), channel_id=1, source_target_pairs={{0,28},{4,24},{8,20},{12,16},{16,12},{20,8},{24,4},{28,0},{1,29},{... | collective-permute-start | bytes 393224 | tf_op jit(solution)/shard_map/ppermute | solution.py:348
  82.0 5.9 %forward.2 = (bf16[256,16,128]{2,1,0:T(8,128)(2,1)}, bf16[16,2,32,128]{3,2,1,0:T(8,128)(2,1)}, bf16[16,2,32,128]{3,2,1,0:T(8,128)(2,1)}, bf16[16,2,32,128]{3,2,1...) custom-call(s32[1]{0:T(128)} %bitcast.1.me_ref, ...), custom_call_target="tpu_custom_call" | custom-call | flops 1073741824 | bytes 6291456 | tf_op jit(solution)/shard_map/forward/pallas_call | solution.py:206
  87.9 2.7 %collective-permute-done.13.refs_5_ = bf16[32,16,128]{2,1,0:T(8,128)(2,1)S(1)} collective-permute-done((bf16[32,16,128]{2,1,0:T(8,128)(2,1)S(1)}, bf16[32,16,128]{2,1,0:T(8,128)(2,1)S(1)}, u32[]{:S(2)}, u32[]{:S(2)}) %collective-permute-start.13) | collective-permute-done | bytes 131104 | tf_op jit(solution)/shard_map/ppermute | solution.py:348
  91.4 2.4 %pick.3 = bf16[8,32,16,128]{3,2,1,0:T(8,128)(2,1)} custom-call(s32[8]{0:T(128)} %get-tuple-element.203.choice_ref, bf16[32,16,128]{2,1,0:T(8,128)(2,1)} %get-tuple-element.142.refs_0_, bf16[32,16,128]{2,1,0:T(8,128)(2,1)} %copy-done.31, bf16[32,16,128]{2,1,0:T(8,128)(2,1)} %copy-done.32, bf16[32,16,128]{2,1,0:T(8,128)(2,1)} %copy-done.33, ...), custom_call_target="tpu_custom_call" | custom-call | bytes 2097152 | tf_op jit(solution)/shard_map/pick/pallas_call | solution.py:401
  93.8 7.1 %all-to-all-start = ((bf16[256,16,128]{2,1,0:T(8,128)(2,1)}), bf16[256,16,128]{2,1,0:T(8,128)(2,1)S(1)}, u32[]{:S(2)}, u32[]{:S(2)}) async-start(bf16[256,16,128]{2,1,0:T(8,128)(2,1)} %bitcast.34), calls=%async_computation | async-start | bytes 2097152 | tf_op jit(solution)/shard_map/all_to_all | solution.py:428
  107.8 2.9 %collective-permute-done.33.refs_2_ = bf16[16,2,32,128]{3,2,1,0:T(8,128)(2,1)S(1)} collective-permute-done((bf16[16,2,32,128]{3,2,1,0:T(8,128)(2,1)}, bf16[16,2,32,128]{3,2,1,0:T(8,128)(2,1)S(1)}, u32[]{:S(2)}, u32[]{:S(2)}) %collective-permute-start.33) | collective-permute-done | bytes 262176 | tf_op jit(solution)/shard_map/ppermute | solution.py:348
  110.7 5.2 %collective-permute-done.34.refs_3_ = bf16[16,2,32,128]{3,2,1,0:T(8,128)(2,1)S(1)} collective-permute-done((bf16[16,2,32,128]{3,2,1,0:T(8,128)(2,1)S(1)}, bf16[16,2,32,128]{3,2,1,0:T(8,128)(2,1)S(1)}, u32[]{:S(2)}, u32[]{:S(2)}) %collective-permute-start.34) | collective-permute-done | bytes 262176 | tf_op jit(solution)/shard_map/ppermute | solution.py:348
  116.6 3.6 %middle.7 = (bf16[32,2,16,128]{3,2,1,0:T(8,128)(2,1)}, bf16[32,2,16,128]{3,2,1,0:T(8,128)(2,1)}, bf16[32,2,16,128]{3,2,1,0:T(8,128)(2,1)}, bf16[32,2,16,128]{3,2,1,0:T(8,128)(2,1)}) custom-call(s32[1]{0:T(128)} %bitcast.me_ref.grid_ref, bf16[16,2,32,128]{3,2,1,0:T(8,128)(2,1)} %get-tuple-element.134.refs_0_, bf16[16,2,32,128]{3,2,1,0:T(8,128)(2,1)} %copy-done.19, ...), custom_call_target="tpu_custom_call" | custom-call | flops 536870912 | bytes 3145728 | tf_op jit(solution)/shard_map/middle/pallas_call | solution.py:258
  122.8 4.4 %collective-permute-done.25.refs_3_ = bf16[16,2,32,128]{3,2,1,0:T(8,128)(2,1)S(1)} collective-permute-done((bf16[16,2,32,128]{3,2,1,0:T(8,128)(2,1)}, bf16[16,2,32,128]{3,2,1,0:T(8,128)(2,1)S(1)}, u32[]{:S(2)}, u32[]{:S(2)}) %collective-permute-start.25) | collective-permute-done | bytes 262176 | tf_op jit(solution)/shard_map/ppermute | solution.py:348
  127.9 3.6 %middle.4 = (bf16[32,2,16,128]{3,2,1,0:T(8,128)(2,1)}, bf16[32,2,16,128]{3,2,1,0:T(8,128)(2,1)}, bf16[32,2,16,128]{3,2,1,0:T(8,128)(2,1)}, bf16[32,2,16,128]{3,2,1,0:T(8,128)(2,1)}) custom-call(s32[1]{0:T(128)} %bitcast.me_ref.grid_ref, bf16[16,2,32,128]{3,2,1,0:T(8,128)(2,1)} %get-tuple-element.135.refs_0_, bf16[16,2,32,128]{3,2,1,0:T(8,128)(2,1)} %copy-done.17, ...), custom_call_target="tpu_custom_call" | custom-call | flops 536870912 | bytes 3145728 | tf_op jit(solution)/shard_map/middle/pallas_call | solution.py:258
  132.5 5.4 %forward.3 = (bf16[16,2,32,128]{3,2,1,0:T(8,128)(2,1)}, bf16[16,2,32,128]{3,2,1,0:T(8,128)(2,1)}, bf16[16,2,32,128]{3,2,1,0:T(8,128)(2,1)}, bf16[16,2,32,128]{3,...) custom-call(s32[1]{0:T(128)} %bitcast.1.me_ref, ...), custom_call_target="tpu_custom_call" | custom-call | flops 1073741824 | bytes 6291456 | tf_op jit(solution)/shard_map/forward/pallas_call | solution.py:206
  142.1 5.4 %collective-permute-done.27.refs_2_ = bf16[16,2,32,128]{3,2,1,0:T(8,128)(2,1)S(1)} collective-permute-done((bf16[16,2,32,128]{3,2,1,0:T(8,128)(2,1)}, bf16[16,2,32,128]{3,2,1,0:T(8,128)(2,1)S(1)}, u32[]{:S(2)}, u32[]{:S(2)}) %collective-permute-start.27) | collective-permute-done | bytes 262176 | tf_op jit(solution)/shard_map/ppermute | solution.py:348
  149.6 3.5 %collective-permute-done.30.refs_2_ = bf16[16,2,32,128]{3,2,1,0:T(8,128)(2,1)S(1)} collective-permute-done((bf16[16,2,32,128]{3,2,1,0:T(8,128)(2,1)}, bf16[16,2,32,128]{3,2,1,0:T(8,128)(2,1)S(1)}, u32[]{:S(2)}, u32[]{:S(2)}) %collective-permute-start.30) | collective-permute-done | bytes 262176 | tf_op jit(solution)/shard_map/ppermute | solution.py:348
  155.1 3.2 %collective-permute-done.31.refs_3_ = bf16[16,2,32,128]{3,2,1,0:T(8,128)(2,1)S(1)} collective-permute-done((bf16[16,2,32,128]{3,2,1,0:T(8,128)(2,1)}, bf16[16,2,32,128]{3,2,1,0:T(8,128)(2,1)S(1)}, u32[]{:S(2)}, u32[]{:S(2)}) %collective-permute-start.31) | collective-permute-done | bytes 262176 | tf_op jit(solution)/shard_map/ppermute | solution.py:348
  160.5 3.7 %middle.6 = (bf16[16,2,16,128]{3,2,1,0:T(8,128)(2,1)}, bf16[16,2,16,128]{3,2,1,0:T(8,128)(2,1)}, bf16[16,2,16,128]{3,2,1,0:T(8,128)(2,1)}, bf16[16,2,16,128]{3,2...) custom-call(s32[1]{0:T(128)} %bitcast.me_ref.grid_ref, ...), custom_call_target="tpu_custom_call" | custom-call | flops 536870912 | bytes 3145728 | tf_op jit(solution)/shard_map/middle/pallas_call | solution.py:258
  164.8 3.6 %middle.5 = (bf16[32,2,16,128]{3,2,1,0:T(8,128)(2,1)}, bf16[32,2,16,128]{3,2,1,0:T(8,128)(2,1)}, bf16[32,2,16,128]{3,2,1,0:T(8,128)(2,1)}, bf16[32,2,16,128]{3,2,1,0:T(8,128)(2,1)}) custom-call(s32[1]{0:T(128)} %bitcast.me_ref.grid_ref, bf16[16,2,32,128]{3,2,1,0:T(8,128)(2,1)} %get-tuple-element.155.refs_0_, bf16[16,2,32,128]{3,2,1,0:T(8,128)(2,1)} %copy-done.13, ...), custom_call_target="tpu_custom_call" | custom-call | flops 536870912 | bytes 3145728 | tf_op jit(solution)/shard_map/middle/pallas_call | solution.py:258
  171.8 3.8 %collective-permute-done.39.refs_5_ = bf16[32,2,16,128]{3,2,1,0:T(8,128)(2,1)S(1)} collective-permute-done((bf16[32,2,16,128]{3,2,1,0:T(8,128)(2,1)}, bf16[32,2,16,128]{3,2,1,0:T(8,128)(2,1)S(1)}, u32[]{:S(2)}, u32[]{:S(2)}) %collective-permute-start.39) | collective-permute-done | bytes 262176 | tf_op jit(solution)/shard_map/ppermute | solution.py:348
  175.6 5.3 %collective-permute-done.40.refs_7_ = bf16[32,2,16,128]{3,2,1,0:T(8,128)(2,1)S(1)} collective-permute-done((bf16[32,2,16,128]{3,2,1,0:T(8,128)(2,1)}, bf16[32,2,16,128]{3,2,1,0:T(8,128)(2,1)S(1)}, u32[]{:S(2)}, u32[]{:S(2)}) %collective-permute-start.40) | collective-permute-done | bytes 262176 | tf_op jit(solution)/shard_map/ppermute | solution.py:348
  185.4 4.3 %backward.4.refs_12_ = f32[2,32,128,128]{3,2,1,0:T(8,128)} custom-call(bf16[32,2,16,128]{3,2,1,0:T(8,128)(2,1)} %get-tuple-element.176.refs_0_, bf16[32,2,16,128]{3,2,1,0:T(8,128)(2,1)} %get-tuple-element.150.refs_1_, bf16[32,2,16,128]{3,2,1,0:T(8,128)(2,1)} %copy-done.4, bf16[32,2,16,128]{3,2,1,0:T(8,128)(2,1)} %copy-done.8, ...), custom_call_target="tpu_custom_call" | custom-call | flops 536870912 | bytes 6291456 | tf_op jit(solution)/shard_map/backward/pallas_call | solution.py:325
  189.7 4.3 %backward.5.refs_12_ = f32[2,32,128,128]{3,2,1,0:T(8,128)} custom-call(bf16[32,2,16,128]{3,2,1,0:T(8,128)(2,1)} %get-tuple-element.176.refs_0_, bf16[32,2,16,128]{3,2,1,0:T(8,128)(2,1)} %get-tuple-element.150.refs_1_, bf16[32,2,16,128]{3,2,1,0:T(8,128)(2,1)} %copy-done.4, bf16[32,2,16,128]{3,2,1,0:T(8,128)(2,1)} %copy-done.8, ...), custom_call_target="tpu_custom_call", output_to_operand_aliasing={{}: (12, {})} | custom-call | flops 536870912 | bytes 6291456 | tf_op jit(solution)/shard_map/backward/pallas_call | solution.py:325
  199.5 4.4 %backward.6.refs_12_ = f32[2,32,128,128]{3,2,1,0:T(8,128)} custom-call(bf16[32,2,16,128]{3,2,1,0:T(8,128)(2,1)} %get-tuple-element.159.refs_0_, bf16[16,2,16,128]{3,2,1,0:T(8,128)(2,1)} %get-tuple-element.172.refs_1_, bf16[32,2,16,128]{3,2,1,0:T(8,128)(2,1)} %copy-done.7, bf16[16,2,16,128]{3,2,1,0:T(8,128)(2,1)} %copy-done.25, ...), custom_call_target="tpu_custom_call", output_to_operand_aliasing={{}: (12, {})} | custom-call | flops 536870912 | bytes 6291456 | tf_op jit(solution)/shard_map/backward/pallas_call | solution.py:325
  205.6 4.4 %backward.7 = f32[2,32,128,128]{3,2,1,0:T(8,128)} custom-call(bf16[32,2,16,128]{3,2,1,0:T(8,128)(2,1)} %get-tuple-element.159.refs_0_, bf16[16,2,16,128]{3,2,1,0:T(8,128)(2,1)} %get-tuple-element.181.refs_1_, bf16[32,2,16,128]{3,2,1,0:T(8,128)(2,1)} %copy-done.7, bf16[16,2,16,128]{3,2,1,0:T(8,128)(2,1)} %copy-done.28, ...), custom_call_target="tpu_custom_call", output_to_operand_aliasing={{}: (12, {})} | custom-call | flops 536870912 | bytes 6291456 | tf_op jit(solution)/shard_map/backward/pallas_call | solution.py:325
  (248 shorter events, 68.1 us)
Async XLA Ops:
  4.6 42.3 %collective-permute-start.7 = (bf16[128,2048]{1,0:T(8,128)(2,1)}, bf16[128,2048]{1,0:T(8,128)(2,1)S(1)}, u32[]{:S(2)}, u32[]{:S(2)}) collective-permute-start(bf16[128,2048]{1,0:T(8,128)(2,1)} %get-tuple-element.107), channel_id=1, source_target_pairs={{0,3},{1,2},{2,1},{3,0},{4,7},{5,6},{6,5},{7,4},{8,11},{9,10},{10,... | collective-permute-start | bytes 1572872 | tf_op jit(solution)/shard_map/ppermute | solution.py:448
  11.6 16.5 %collective-permute-start.5 = (bf16[32,16,128]{2,1,0:T(8,128)(2,1)S(1)}, bf16[32,16,128]{2,1,0:T(8,128)(2,1)S(1)}, u32[]{:S(2)}, u32[]{:S(2)}) collective-permute-start(bf16[32,16,128]{2,1,0:T(8,128)(2,1)S(1)} %get-tuple-element.189), channel_id=1, source_target_pairs={{0,24},{4,28},{8,16},{12,20},{16,8},{20,12},{24,0},{28,4},{1,25},{... | collective-permute-start | bytes 393224 | tf_op jit(solution)/shard_map/ppermute | solution.py:348
  11.8 20.5 %collective-permute-start.4 = (bf16[32,16,128]{2,1,0:T(8,128)(2,1)S(1)}, bf16[32,16,128]{2,1,0:T(8,128)(2,1)S(1)}, u32[]{:S(2)}, u32[]{:S(2)}) collective-permute-start(bf16[32,16,128]{2,1,0:T(8,128)(2,1)S(1)} %get-tuple-element.190), channel_id=1, source_target_pairs={{0,20},{4,16},{8,28},{12,24},{16,4},{20,0},{24,12},{28,8},{1,21},{... | collective-permute-start | bytes 393224 | tf_op jit(solution)/shard_map/ppermute | solution.py:348
  12.5 22.3 %collective-permute-start.3 = (bf16[32,16,128]{2,1,0:T(8,128)(2,1)S(1)}, bf16[32,16,128]{2,1,0:T(8,128)(2,1)S(1)}, u32[]{:S(2)}, u32[]{:S(2)}) collective-permute-start(bf16[32,16,128]{2,1,0:T(8,128)(2,1)S(1)} %get-tuple-element.191), channel_id=1, source_target_pairs={{0,16},{4,20},{8,24},{12,28},{16,0},{20,4},{24,8},{28,12},{1,17},{... | collective-permute-start | bytes 393224 | tf_op jit(solution)/shard_map/ppermute | solution.py:348
  16.0 23.0 %collective-permute-start.2 = (bf16[32,16,128]{2,1,0:T(8,128)(2,1)S(1)}, bf16[32,16,128]{2,1,0:T(8,128)(2,1)S(1)}, u32[]{:S(2)}, u32[]{:S(2)}) collective-permute-start(bf16[32,16,128]{2,1,0:T(8,128)(2,1)S(1)} %get-tuple-element.192), channel_id=1, source_target_pairs={{0,12},{4,8},{8,4},{12,0},{16,28},{20,24},{24,20},{28,16},{1,13},{... | collective-permute-start | bytes 393224 | tf_op jit(solution)/shard_map/ppermute | solution.py:348
  42.2 16.4 %collective-permute-start.16 = (bf16[32,16,128]{2,1,0:T(8,128)(2,1)}, bf16[32,16,128]{2,1,0:T(8,128)(2,1)S(1)}, u32[]{:S(2)}, u32[]{:S(2)}) collective-permute-start(bf16[32,16,128]{2,1,0:T(8,128)(2,1)} %get-tuple-element.118), channel_id=1, source_target_pairs={{0,4},{4,0},{8,12},{12,8},{16,20},{20,16},{24,28},{28,24},{1,5},{5... | collective-permute-start | bytes 393224 | tf_op jit(solution)/shard_map/ppermute | solution.py:348
  43.3 17.8 %collective-permute-start.17 = (bf16[32,16,128]{2,1,0:T(8,128)(2,1)}, bf16[32,16,128]{2,1,0:T(8,128)(2,1)S(1)}, u32[]{:S(2)}, u32[]{:S(2)}) collective-permute-start(bf16[32,16,128]{2,1,0:T(8,128)(2,1)} %get-tuple-element.119), channel_id=1, source_target_pairs={{0,8},{4,12},{8,0},{12,4},{16,24},{20,28},{24,16},{28,20},{1,9},{5... | collective-permute-start | bytes 393224 | tf_op jit(solution)/shard_map/ppermute | solution.py:348
  43.3 19.6 %collective-permute-start.18 = (bf16[32,16,128]{2,1,0:T(8,128)(2,1)}, bf16[32,16,128]{2,1,0:T(8,128)(2,1)S(1)}, u32[]{:S(2)}, u32[]{:S(2)}) collective-permute-start(bf16[32,16,128]{2,1,0:T(8,128)(2,1)} %get-tuple-element.120), channel_id=1, source_target_pairs={{0,12},{4,8},{8,4},{12,0},{16,28},{20,24},{24,20},{28,16},{1,13},{... | collective-permute-start | bytes 393224 | tf_op jit(solution)/shard_map/ppermute | solution.py:348
  45.8 18.3 %collective-permute-start.19 = (bf16[32,16,128]{2,1,0:T(8,128)(2,1)}, bf16[32,16,128]{2,1,0:T(8,128)(2,1)S(1)}, u32[]{:S(2)}, u32[]{:S(2)}) collective-permute-start(bf16[32,16,128]{2,1,0:T(8,128)(2,1)} %get-tuple-element.121), channel_id=1, source_target_pairs={{0,16},{4,20},{8,24},{12,28},{16,0},{20,4},{24,8},{28,12},{1,17},{... | collective-permute-start | bytes 393224 | tf_op jit(solution)/shard_map/ppermute | solution.py:348
  46.9 17.9 %collective-permute-start.20 = (bf16[32,16,128]{2,1,0:T(8,128)(2,1)}, bf16[32,16,128]{2,1,0:T(8,128)(2,1)S(1)}, u32[]{:S(2)}, u32[]{:S(2)}) collective-permute-start(bf16[32,16,128]{2,1,0:T(8,128)(2,1)} %get-tuple-element.122), channel_id=1, source_target_pairs={{0,20},{4,16},{8,28},{12,24},{16,4},{20,0},{24,12},{28,8},{1,21},{... | collective-permute-start | bytes 393224 | tf_op jit(solution)/shard_map/ppermute | solution.py:348
  64.8 23.1 %collective-permute-start.11 = (bf16[32,16,128]{2,1,0:T(8,128)(2,1)S(1)}, bf16[32,16,128]{2,1,0:T(8,128)(2,1)S(1)}, u32[]{:S(2)}, u32[]{:S(2)}) collective-permute-start(bf16[32,16,128]{2,1,0:T(8,128)(2,1)S(1)} %copy-done.54), channel_id=1, source_target_pairs={{0,12},{4,8},{8,4},{12,0},{16,28},{20,24},{24,20},{28,16},{1,13},{... | collective-permute-start | bytes 393224 | tf_op jit(solution)/shard_map/ppermute | solution.py:348
  67.2 20.7 %collective-permute-start.12 = (bf16[32,16,128]{2,1,0:T(8,128)(2,1)S(1)}, bf16[32,16,128]{2,1,0:T(8,128)(2,1)S(1)}, u32[]{:S(2)}, u32[]{:S(2)}) collective-permute-start(bf16[32,16,128]{2,1,0:T(8,128)(2,1)S(1)} %copy-done.53), channel_id=1, source_target_pairs={{0,16},{4,20},{8,24},{12,28},{16,0},{20,4},{24,8},{28,12},{1,17},{... | collective-permute-start | bytes 393224 | tf_op jit(solution)/shard_map/ppermute | solution.py:348
  71.6 19.0 %collective-permute-start.13 = (bf16[32,16,128]{2,1,0:T(8,128)(2,1)S(1)}, bf16[32,16,128]{2,1,0:T(8,128)(2,1)S(1)}, u32[]{:S(2)}, u32[]{:S(2)}) collective-permute-start(bf16[32,16,128]{2,1,0:T(8,128)(2,1)S(1)} %copy-done.52), channel_id=1, source_target_pairs={{0,20},{4,16},{8,28},{12,24},{16,4},{20,0},{24,12},{28,8},{1,21},{... | collective-permute-start | bytes 393224 | tf_op jit(solution)/shard_map/ppermute | solution.py:348
  76.5 14.1 %collective-permute-start.14 = (bf16[32,16,128]{2,1,0:T(8,128)(2,1)S(1)}, bf16[32,16,128]{2,1,0:T(8,128)(2,1)S(1)}, u32[]{:S(2)}, u32[]{:S(2)}) collective-permute-start(bf16[32,16,128]{2,1,0:T(8,128)(2,1)S(1)} %copy-done.51), channel_id=1, source_target_pairs={{0,24},{4,28},{8,16},{12,20},{16,8},{20,12},{24,0},{28,4},{1,25},{... | collective-permute-start | bytes 393224 | tf_op jit(solution)/shard_map/ppermute | solution.py:348
  93.8 37.7 %all-to-all-start = ((bf16[256,16,128]{2,1,0:T(8,128)(2,1)}), bf16[256,16,128]{2,1,0:T(8,128)(2,1)S(1)}, u32[]{:S(2)}, u32[]{:S(2)}) async-start(bf16[256,16,128]{2,1,0:T(8,128)(2,1)} %bitcast.34), calls=%async_computation | async-start | bytes 2097152 | tf_op jit(solution)/shard_map/all_to_all | solution.py:428
  104.8 17.9 %collective-permute-start.23 = (bf16[16,2,32,128]{3,2,1,0:T(8,128)(2,1)}, bf16[16,2,32,128]{3,2,1,0:T(8,128)(2,1)S(1)}, u32[]{:S(2)}, u32[]{:S(2)}) collective-permute-start(bf16[16,2,32,128]{3,2,1,0:T(8,128)(2,1)} %get-tuple-element.137), channel_id=1, source_target_pairs={{0,1},{1,0},{2,3},{3,2},{4,5},{5,4},{6,7},{7,6},{8,9},{9,8},{10,11... | collective-permute-start | bytes 786440 | tf_op jit(solution)/shard_map/ppermute | solution.py:348
  104.9 17.8 %collective-permute-start.24 = (bf16[16,2,32,128]{3,2,1,0:T(8,128)(2,1)}, bf16[16,2,32,128]{3,2,1,0:T(8,128)(2,1)S(1)}, u32[]{:S(2)}, u32[]{:S(2)}) collective-permute-start(bf16[16,2,32,128]{3,2,1,0:T(8,128)(2,1)} %get-tuple-element.139), channel_id=1, source_target_pairs={{0,2},{1,3},{2,0},{3,1},{4,6},{5,7},{6,4},{7,5},{8,10},{9,11},{10,... | collective-permute-start | bytes 786440 | tf_op jit(solution)/shard_map/ppermute | solution.py:348
  106.9 20.3 %collective-permute-start.25 = (bf16[16,2,32,128]{3,2,1,0:T(8,128)(2,1)}, bf16[16,2,32,128]{3,2,1,0:T(8,128)(2,1)S(1)}, u32[]{:S(2)}, u32[]{:S(2)}) collective-permute-start(bf16[16,2,32,128]{3,2,1,0:T(8,128)(2,1)} %get-tuple-element.141), channel_id=1, source_target_pairs={{0,3},{1,2},{2,1},{3,0},{4,7},{5,6},{6,5},{7,4},{8,11},{9,10},{10,... | collective-permute-start | bytes 786440 | tf_op jit(solution)/shard_map/ppermute | solution.py:348
  120.2 19.9 %collective-permute-start.35 = (bf16[32,2,16,128]{3,2,1,0:T(8,128)(2,1)}, bf16[32,2,16,128]{3,2,1,0:T(8,128)(2,1)S(1)}, u32[]{:S(2)}, u32[]{:S(2)}) collective-permute-start(bf16[32,2,16,128]{3,2,1,0:T(8,128)(2,1)} %get-tuple-element.169), channel_id=1, source_target_pairs={{0,1},{1,0},{2,3},{3,2},{4,5},{5,4},{6,7},{7,6},{8,9},{9,8},{10,11... | collective-permute-start | bytes 786440 | tf_op jit(solution)/shard_map/ppermute | solution.py:348
  120.7 19.5 %collective-permute-start.36 = (bf16[32,2,16,128]{3,2,1,0:T(8,128)(2,1)}, bf16[32,2,16,128]{3,2,1,0:T(8,128)(2,1)S(1)}, u32[]{:S(2)}, u32[]{:S(2)}) collective-permute-start(bf16[32,2,16,128]{3,2,1,0:T(8,128)(2,1)} %get-tuple-element.170), channel_id=1, source_target_pairs={{0,2},{1,3},{2,0},{3,1},{4,6},{5,7},{6,4},{7,5},{8,10},{9,11},{10,... | collective-permute-start | bytes 786440 | tf_op jit(solution)/shard_map/ppermute | solution.py:348
  140.3 18.1 %collective-permute-start.31 = (bf16[16,2,32,128]{3,2,1,0:T(8,128)(2,1)}, bf16[16,2,32,128]{3,2,1,0:T(8,128)(2,1)S(1)}, u32[]{:S(2)}, u32[]{:S(2)}) collective-permute-start(bf16[16,2,32,128]{3,2,1,0:T(8,128)(2,1)} %get-tuple-element.163), channel_id=1, source_target_pairs={{0,3},{1,2},{2,1},{3,0},{4,7},{5,6},{6,5},{7,4},{8,11},{9,10},{10,... | collective-permute-start | bytes 786440 | tf_op jit(solution)/shard_map/ppermute | solution.py:348
  142.0 22.1 %collective-permute-start.28 = (bf16[16,2,32,128]{3,2,1,0:T(8,128)(2,1)}, bf16[16,2,32,128]{3,2,1,0:T(8,128)(2,1)S(1)}, u32[]{:S(2)}, u32[]{:S(2)}) collective-permute-start(bf16[16,2,32,128]{3,2,1,0:T(8,128)(2,1)} %get-tuple-element.158), channel_id=1, source_target_pairs={{0,3},{1,2},{2,1},{3,0},{4,7},{5,6},{6,5},{7,4},{8,11},{9,10},{10,... | collective-permute-start | bytes 786440 | tf_op jit(solution)/shard_map/ppermute | solution.py:348
  147.5 22.0 %collective-permute-start.37 = (bf16[32,2,16,128]{3,2,1,0:T(8,128)(2,1)S(1)}, bf16[32,2,16,128]{3,2,1,0:T(8,128)(2,1)S(1)}, u32[]{:S(2)}, u32[]{:S(2)}) collective-permute-start(bf16[32,2,16,128]{3,2,1,0:T(8,128)(2,1)S(1)} %copy-done.47), channel_id=1, source_target_pairs={{0,3},{1,2},{2,1},{3,0},{4,7},{5,6},{6,5},{7,4},{8,11},{9,10},{10,... | collective-permute-start | bytes 786440 | tf_op jit(solution)/shard_map/ppermute | solution.py:348
  147.5 22.3 %collective-permute-start.38 = (bf16[32,2,16,128]{3,2,1,0:T(8,128)(2,1)}, bf16[32,2,16,128]{3,2,1,0:T(8,128)(2,1)S(1)}, u32[]{:S(2)}, u32[]{:S(2)}) collective-permute-start(bf16[32,2,16,128]{3,2,1,0:T(8,128)(2,1)} %get-tuple-element.151), channel_id=1, source_target_pairs={{0,1},{1,0},{2,3},{3,2},{4,5},{5,4},{6,7},{7,6},{8,9},{9,8},{10,11... | collective-permute-start | bytes 786440 | tf_op jit(solution)/shard_map/ppermute | solution.py:348
  153.1 22.5 %collective-permute-start.39 = (bf16[32,2,16,128]{3,2,1,0:T(8,128)(2,1)}, bf16[32,2,16,128]{3,2,1,0:T(8,128)(2,1)S(1)}, u32[]{:S(2)}, u32[]{:S(2)}) collective-permute-start(bf16[32,2,16,128]{3,2,1,0:T(8,128)(2,1)} %get-tuple-element.152), channel_id=1, source_target_pairs={{0,2},{1,3},{2,0},{3,1},{4,6},{5,7},{6,4},{7,5},{8,10},{9,11},{10,... | collective-permute-start | bytes 786440 | tf_op jit(solution)/shard_map/ppermute | solution.py:348
  158.4 22.5 %collective-permute-start.40 = (bf16[32,2,16,128]{3,2,1,0:T(8,128)(2,1)}, bf16[32,2,16,128]{3,2,1,0:T(8,128)(2,1)S(1)}, u32[]{:S(2)}, u32[]{:S(2)}) collective-permute-start(bf16[32,2,16,128]{3,2,1,0:T(8,128)(2,1)} %get-tuple-element.153), channel_id=1, source_target_pairs={{0,3},{1,2},{2,1},{3,0},{4,7},{5,6},{6,5},{7,4},{8,11},{9,10},{10,... | collective-permute-start | bytes 786440 | tf_op jit(solution)/shard_map/ppermute | solution.py:348
  164.1 17.3 %collective-permute-start.47 = (bf16[16,2,16,128]{3,2,1,0:T(8,128)(2,1)}, bf16[16,2,16,128]{3,2,1,0:T(8,128)(2,1)S(1)}, u32[]{:S(2)}, u32[]{:S(2)}) collective-permute-start(bf16[16,2,16,128]{3,2,1,0:T(8,128)(2,1)} %get-tuple-element.173), channel_id=1, source_target_pairs={{0,1},{1,0},{2,3},{3,2},{4,5},{5,4},{6,7},{7,6},{8,9},{9,8},{10,11... | collective-permute-start | bytes 393224 | tf_op jit(solution)/shard_map/ppermute | solution.py:348
  169.5 28.8 %collective-permute-start.41 = (bf16[32,2,16,128]{3,2,1,0:T(8,128)(2,1)}, bf16[32,2,16,128]{3,2,1,0:T(8,128)(2,1)S(1)}, u32[]{:S(2)}, u32[]{:S(2)}) collective-permute-start(bf16[32,2,16,128]{3,2,1,0:T(8,128)(2,1)} %get-tuple-element.182), channel_id=1, source_target_pairs={{0,1},{1,0},{2,3},{3,2},{4,5},{5,4},{6,7},{7,6},{8,9},{9,8},{10,11... | collective-permute-start | bytes 786440 | tf_op jit(solution)/shard_map/ppermute | solution.py:348
  169.8 28.9 %collective-permute-start.43 = (bf16[32,2,16,128]{3,2,1,0:T(8,128)(2,1)}, bf16[32,2,16,128]{3,2,1,0:T(8,128)(2,1)S(1)}, u32[]{:S(2)}, u32[]{:S(2)}) collective-permute-start(bf16[32,2,16,128]{3,2,1,0:T(8,128)(2,1)} %get-tuple-element.184), channel_id=1, source_target_pairs={{0,2},{1,3},{2,0},{3,1},{4,6},{5,7},{6,4},{7,5},{8,10},{9,11},{10,... | collective-permute-start | bytes 786440 | tf_op jit(solution)/shard_map/ppermute | solution.py:348
  175.6 23.1 %collective-permute-start.45 = (bf16[32,2,16,128]{3,2,1,0:T(8,128)(2,1)}, bf16[32,2,16,128]{3,2,1,0:T(8,128)(2,1)S(1)}, u32[]{:S(2)}, u32[]{:S(2)}) collective-permute-start(bf16[32,2,16,128]{3,2,1,0:T(8,128)(2,1)} %get-tuple-element.186), channel_id=1, source_target_pairs={{0,3},{1,2},{2,1},{3,0},{4,7},{5,6},{6,5},{7,4},{8,11},{9,10},{10,... | collective-permute-start | bytes 786440 | tf_op jit(solution)/shard_map/ppermute | solution.py:348
  180.8 14.4 %collective-permute-start.48 = (bf16[16,2,16,128]{3,2,1,0:T(8,128)(2,1)}, bf16[16,2,16,128]{3,2,1,0:T(8,128)(2,1)S(1)}, u32[]{:S(2)}, u32[]{:S(2)}) collective-permute-start(bf16[16,2,16,128]{3,2,1,0:T(8,128)(2,1)} %get-tuple-element.174), channel_id=1, source_target_pairs={{0,2},{1,3},{2,0},{3,1},{4,6},{5,7},{6,4},{7,5},{8,10},{9,11},{10,... | collective-permute-start | bytes 393224 | tf_op jit(solution)/shard_map/ppermute | solution.py:348
  181.4 15.4 %collective-permute-start.49 = (bf16[16,2,16,128]{3,2,1,0:T(8,128)(2,1)}, bf16[16,2,16,128]{3,2,1,0:T(8,128)(2,1)S(1)}, u32[]{:S(2)}, u32[]{:S(2)}) collective-permute-start(bf16[16,2,16,128]{3,2,1,0:T(8,128)(2,1)} %get-tuple-element.175), channel_id=1, source_target_pairs={{0,3},{1,2},{2,1},{3,0},{4,7},{5,6},{6,5},{7,4},{8,11},{9,10},{10,... | collective-permute-start | bytes 393224 | tf_op jit(solution)/shard_map/ppermute | solution.py:348
  (89 other events, 1015.2 us)

commit v5 on v4

--- a/solution.py
+++ b/solution.py
@@ -388,27 +388,6 @@
     )(choice, *pieces)
 
 
-def pick_stacked_kernel(parts, choice_ref, *refs):
-    in_refs, out_ref, hold = refs[:parts], refs[-2], refs[-1]
-    for slot, in_ref in enumerate(in_refs):
-        hold[slot] = in_ref[...]
-    for number in range(parts):
-        out_ref[number] = hold[choice_ref[number]]
-
-
-def pick_stacked(choice, pieces):
-    parts, shape = len(pieces), pieces[0].shape
-    return pl.pallas_call(
-        functools.partial(pick_stacked_kernel, parts),
-        out_shape=jax.ShapeDtypeStruct((parts,) + shape, pieces[0].dtype),
-        in_specs=[SCALARS] + [WHOLE] * parts,
-        out_specs=WHOLE,
-        scratch_shapes=[pltpu.VMEM((parts,) + shape, pieces[0].dtype)],
-        cost_estimate=cost(0, 4 * parts * math.prod(shape)),
-        name="pick",
-    )(choice, *pieces)
-
-
 def local(orbitals, occupation, partner, col_index, kernel):
     bands, groups = lax.axis_size("band"), lax.axis_size("grid")
     slab, ny, nz = orbitals.shape[1:]
@@ -418,18 +397,16 @@
     band_slots = jnp.arange(bands, dtype=jnp.int32)
     my_band = band_pos.astype(jnp.int32).reshape(1)
     choice = jnp.take(partner, band_slots ^ band_pos) ^ band_pos
-    pick_choice = partner ^ band_pos
     tiled = orbitals.reshape(2, slab * ny // TILE, TILE, nz)
 
     def swap(value, slot):
         return shift(value, "grid", groups, slot)
 
-    def exchange(value):
-        return lax.all_to_all(value, "band", split_axis=0, concat_axis=0, tiled=True)
-
-    def slotwise(sent):
+    def slotwise(sent, near_after=None):
         moved = []
         for slot, piece in enumerate(sent):
+            if near_after is not None and slot < bands // 2:
+                piece = after(piece, near_after)
             moved.append(shift(piece, "band", bands, slot))
         return moved
 
@@ -478,8 +455,7 @@
         return their, sent, moved
 
     their0, sent, moved0 = outward(fetched)
-    picked = pick_stacked(pick_choice, after(arrived, *sent))
-    their1 = exchange(picked.reshape(tiled.shape[1:]))
+    picked = pick(choice, after(arrived, *sent))
 
     def centre(cut, moved, halves):
         return middle(my_grid, moved[cut], kern, cut, x_forward, xright, halves)
@@ -496,7 +472,8 @@
 
     answers = [centre(cut, moved0, 1) for cut in range(cuts)]
     back0 = [home(answers[cut]) for cut in range(cuts)]
-    their1, _, moved1 = outward([after(their1, *answers[-1])])
+    fetched = slotwise(picked, near_after=answers[0])
+    their1, _, moved1 = outward(after(fetched, *answers[-1]))
 
     last = cuts - 1
     answers = [centre(cut, moved1, parts if cut == last else 1) for cut in range(cuts)]

time: 211 us -> 206 us (0.976)
  starting transfers between devices: 86.8 us -> 77.1 us
  waiting for transfers between devices: 45.4 us -> 51.8 us
    all_to_all x1 -> x0, starting transfers between devices: 7.14 us -> none  [exchange(): lax.all_to_all(value, 'band', split_axis=0, concat_axis=0, tiled=True)]
    ppermute x48 -> x55, waiting for transfers between devices: 45.4 us -> 51.8 us  [shift(): lax.ppermute(value, axis, [(i, i ^ mask) for i in range(size)])]
    unnamed x140 -> x150, local copies, waits for them, and re-layouts: 5.77 us -> 3.04 us
    pallas_call x1 -> x0, Pallas kernels: 2.41 us -> none  [pick_stacked(): pl.pallas_call(functools.partial(pick_stacked_kernel, parts), out_shape=j...]
    pallas_call x1 -> x2, Pallas kernels: 2.37 us -> 4.73 us  [pick(): pl.pallas_call(functools.partial(pick_kernel, parts), out_shape=[jax.Shap...]
    ppermute x1, starting transfers between devices: 2.41 us -> 0.09 us  [local(): neg = lax.ppermute(mirrored, 'grid', mirror_of)]
    ppermute x48 -> x55, starting transfers between devices: 75.9 us -> 75.6 us  [shift(): lax.ppermute(value, axis, [(i, i ^ mask) for i in range(size)])]
  transfers between devices with their start and end apart: 51 -> 57, of which waited for: 17 -> 21; matrix products, arithmetic and copies ran while one was open for 3% -> 4% of each run, Pallas kernels for 25% -> 28%
where the time goes in v5:
time: 206 us
  starting transfers between devices  77.1 us (37%)
  Pallas kernels  62.6 us (30%)
  waiting for transfers between devices  51.8 us (25%)
  local copies, waits for them, and re-layouts  10.9 us (5%)
    ppermute x55, starting transfers between devices, shift(): lax.ppermute(value, axis, [(i, i ^ mask) for i in range(size)])  75.6 us
    ppermute x55, waiting for transfers between devices, shift(): lax.ppermute(value, axis, [(i, i ^ mask) for i in range(size)])  51.8 us
    pallas_call x4, Pallas kernels, backward(): pl.pallas_call(functools.partial(backward_kernel, number, has_total), gri...  17.4 us
    pallas_call x4, Pallas kernels, middle(): pl.pallas_call(functools.partial(middle_kernel, groups, halves), grid=(1,...  14.6 us
    pallas_call x2, Pallas kernels, forward(): pl.pallas_call(functools.partial(forward_kernel, parts, half * count, cut...  11.7 us
    pallas_call x1, Pallas kernels, expand(): pl.pallas_call(functools.partial(expand_kernel, scale, groups, rows * len...  9.45 us
    pallas_call x2, Pallas kernels, pick(): pl.pallas_call(functools.partial(pick_kernel, parts), out_shape=[jax.Shap...  4.73 us
  transfers between devices with their start and end apart: 57, of which 21 were waited for; matrix products, arithmetic and copies ran while one was open for 4% of the time, Pallas kernels for 28%

profile of v5, /device:TPU:0, one launch (start us, length us, event | category | flops | bytes accessed | tf_op | source)
XLA Modules:
  0.0 205.7 jit_solution(1118750509821940424)
XLA Ops:
  2.2 6.0 %collective-permute-start.6 = (bf16[32,16,128]{2,1,0:T(8,128)(2,1)S(1)}, bf16[32,16,128]{2,1,0:T(8,128)(2,1)S(1)}, u32[]{:S(2)}, u32[]{:S(2)}) collective-permute-start(bf16[32,16,128]{2,1,0:T(8,128)(2,1)S(1)} %get-tuple-element.228), channel_id=1, source_target_pairs={{0,28},{4,24},{8,20},{12,16},{16,12},{20,8},{24,4},{28,0},{1,29},{... | collective-permute-start | bytes 393224 | tf_op jit(solution)/shard_map/ppermute | solution.py:348
  11.2 2.4 %mirror.1 = (bf16[128,2048]{1,0:T(8,128)(2,1)}, bf16[128,128]{1,0:T(8,128)(2,1)}) custom-call(s32[1]{0:T(128)} %bitcast.me_ref.grid_ref, f32[128,2048]{1,0:T(8,128)} %own_ref.2, s32[1,8192]{1,0:T(1,128)} %bitcast.38), custom_call_target="tpu_custom_call" | custom-call | flops 67108864 | bytes 1572864 | tf_op jit(solution)/shard_map/mirror/pallas_call | solution.py:86
  14.3 2.3 %split.1 = (bf16[32,16,128]{2,1,0:T(8,128)(2,1)}, bf16[32,16,128]{2,1,0:T(8,128)(2,1)}, bf16[32,16,128]{2,1,0:T(8,128)(2,1)}, bf16[32,16,128]{2,1,0:T(8,128)(2,1...) custom-call(s32[1]{0:T(128)} %bitcast.1.me_ref, ...), custom_call_target="tpu_custom_call" | custom-call | bytes 2097152 | tf_op jit(solution)/shard_map/split/pallas_call | solution.py:359
  16.7 7.8 %collective-permute-start.2 = (bf16[32,16,128]{2,1,0:T(8,128)(2,1)S(1)}, bf16[32,16,128]{2,1,0:T(8,128)(2,1)S(1)}, u32[]{:S(2)}, u32[]{:S(2)}) collective-permute-start(bf16[32,16,128]{2,1,0:T(8,128)(2,1)S(1)} %get-tuple-element.232), channel_id=1, source_target_pairs={{0,12},{4,8},{8,4},{12,0},{16,28},{20,24},{24,20},{28,16},{1,13},{... | collective-permute-start | bytes 393224 | tf_op jit(solution)/shard_map/ppermute | solution.py:348
  26.4 2.4 %collective-permute-done.4.refs_5_ = bf16[32,16,128]{2,1,0:T(8,128)(2,1)S(1)} collective-permute-done((bf16[32,16,128]{2,1,0:T(8,128)(2,1)S(1)}, bf16[32,16,128]{2,1,0:T(8,128)(2,1)S(1)}, u32[]{:S(2)}, u32[]{:S(2)}) %collective-permute-start.4) | collective-permute-done | bytes 131104 | tf_op jit(solution)/shard_map/ppermute | solution.py:348
  35.2 2.4 %pick.2 = (bf16[32,16,128]{2,1,0:T(8,128)(2,1)}, bf16[32,16,128]{2,1,0:T(8,128)(2,1)}, bf16[32,16,128]{2,1,0:T(8,128)(2,1)}, bf16[32,16,128]{2,1,0:T(8,128)(2,1)...) custom-call(s32[8]{0:T(128)} %fusion.10.choice_ref, ...), custom_call_target="tpu_custom_call" | custom-call | bytes 2097152 | tf_op jit(solution)/shard_map/pick/pallas_call | solution.py:380
  39.1 2.5 %collective-permute-start.18 = (bf16[32,16,128]{2,1,0:T(8,128)(2,1)}, bf16[32,16,128]{2,1,0:T(8,128)(2,1)S(1)}, u32[]{:S(2)}, u32[]{:S(2)}) collective-permute-start(bf16[32,16,128]{2,1,0:T(8,128)(2,1)} %get-tuple-element.140), channel_id=1, source_target_pairs={{0,12},{4,8},{8,4},{12,0},{16,28},{20,24},{24,20},{28,16},{1,13},{... | collective-permute-start | bytes 393224 | tf_op jit(solution)/shard_map/ppermute | solution.py:348
  50.2 9.4 %expand.1.refs_4_ = f32[32,128,128]{2,1,0:T(8,128)} custom-call(s32[1]{0:T(128)} %bitcast.me_ref.grid_ref, f32[128,2048]{1,0:T(8,128)} %own_ref.2, bf16[128,2048]{1,0:T(8,128)(2,1)} %copy-done.44, bf16[128,128]{1,0:T(8,128)(2,1)} %copy-done.74, s32[1,8192]{1,0:T(1,128)} %bitcast.39), custom_call_target="tpu_custom_call" | custom-call | flops 4294967296 | bytes 3145728 | tf_op jit(solution)/shard_map/expand/pallas_call | solution.py:131
  63.4 4.4 %collective-permute-start.12 = (bf16[32,16,128]{2,1,0:T(8,128)(2,1)S(1)}, bf16[32,16,128]{2,1,0:T(8,128)(2,1)S(1)}, u32[]{:S(2)}, u32[]{:S(2)}) collective-permute-start(bf16[32,16,128]{2,1,0:T(8,128)(2,1)S(1)} %copy-done.49), channel_id=1, source_target_pairs={{0,16},{4,20},{8,24},{12,28},{16,0},{20,4},{24,8},{28,12},{1,17},{... | collective-permute-start | bytes 393224 | tf_op jit(solution)/shard_map/ppermute | solution.py:348
  68.5 6.3 %collective-permute-start.13 = (bf16[32,16,128]{2,1,0:T(8,128)(2,1)S(1)}, bf16[32,16,128]{2,1,0:T(8,128)(2,1)S(1)}, u32[]{:S(2)}, u32[]{:S(2)}) collective-permute-start(bf16[32,16,128]{2,1,0:T(8,128)(2,1)S(1)} %copy-done.48), channel_id=1, source_target_pairs={{0,20},{4,16},{8,28},{12,24},{16,4},{20,0},{24,12},{28,8},{1,21},{... | collective-permute-start | bytes 393224 | tf_op jit(solution)/shard_map/ppermute | solution.py:348
  74.8 5.8 %forward.2 = (bf16[256,16,128]{2,1,0:T(8,128)(2,1)}, bf16[16,2,32,128]{3,2,1,0:T(8,128)(2,1)}, bf16[16,2,32,128]{3,2,1,0:T(8,128)(2,1)}, bf16[16,2,32,128]{3,2,1...) custom-call(s32[1]{0:T(128)} %bitcast.1.me_ref, ...), custom_call_target="tpu_custom_call" | custom-call | flops 1073741824 | bytes 6291456 | tf_op jit(solution)/shard_map/forward/pallas_call | solution.py:206
  85.0 2.5 %collective-permute-start.15 = (bf16[32,16,128]{2,1,0:T(8,128)(2,1)S(1)}, bf16[32,16,128]{2,1,0:T(8,128)(2,1)S(1)}, u32[]{:S(2)}, u32[]{:S(2)}) collective-permute-start(bf16[32,16,128]{2,1,0:T(8,128)(2,1)S(1)} %copy-done.46), channel_id=1, source_target_pairs={{0,28},{4,24},{8,20},{12,16},{16,12},{20,8},{24,4},{28,0},{1,29},{... | collective-permute-start | bytes 393224 | tf_op jit(solution)/shard_map/ppermute | solution.py:348
  87.5 3.6 %collective-permute-done.14.refs_6_ = bf16[32,16,128]{2,1,0:T(8,128)(2,1)S(1)} collective-permute-done((bf16[32,16,128]{2,1,0:T(8,128)(2,1)S(1)}, bf16[32,16,128]{2,1,0:T(8,128)(2,1)S(1)}, u32[]{:S(2)}, u32[]{:S(2)}) %collective-permute-start.14) | collective-permute-done | bytes 131104 | tf_op jit(solution)/shard_map/ppermute | solution.py:348
  94.1 2.4 %pick.3 = (bf16[32,16,128]{2,1,0:T(8,128)(2,1)}, bf16[32,16,128]{2,1,0:T(8,128)(2,1)}, bf16[32,16,128]{2,1,0:T(8,128)(2,1)}, bf16[32,16,128]{2,1,0:T(8,128)(2,1)...) custom-call(s32[8]{0:T(128)} %fusion.10.choice_ref, ...), custom_call_target="tpu_custom_call" | custom-call | bytes 2097152 | tf_op jit(solution)/shard_map/pick/pallas_call | solution.py:380
  98.2 4.2 %collective-permute-start.29 = (bf16[32,16,128]{2,1,0:T(8,128)(2,1)}, bf16[32,16,128]{2,1,0:T(8,128)(2,1)S(1)}, u32[]{:S(2)}, u32[]{:S(2)}) collective-permute-start(bf16[32,16,128]{2,1,0:T(8,128)(2,1)} %get-tuple-element.182), channel_id=1, source_target_pairs={{0,16},{4,20},{8,24},{12,28},{16,0},{20,4},{24,8},{28,12},{1,17},{... | collective-permute-start | bytes 393224 | tf_op jit(solution)/shard_map/ppermute | solution.py:348
  105.7 3.6 %middle.4 = (bf16[32,2,16,128]{3,2,1,0:T(8,128)(2,1)}, bf16[32,2,16,128]{3,2,1,0:T(8,128)(2,1)}, bf16[32,2,16,128]{3,2,1,0:T(8,128)(2,1)}, bf16[32,2,16,128]{3,2,1,0:T(8,128)(2,1)}) custom-call(s32[1]{0:T(128)} %bitcast.me_ref.grid_ref, bf16[16,2,32,128]{3,2,1,0:T(8,128)(2,1)} %get-tuple-element.154.refs_0_, bf16[16,2,32,128]{3,2,1,0:T(8,128)(2,1)} %copy-done.12, ...), custom_call_target="tpu_custom_call" | custom-call | flops 536870912 | bytes 3145728 | tf_op jit(solution)/shard_map/middle/pallas_call | solution.py:258
  109.4 2.5 %collective-permute-start.32 = (bf16[32,16,128]{2,1,0:T(8,128)(2,1)S(1)}, bf16[32,16,128]{2,1,0:T(8,128)(2,1)S(1)}, u32[]{:S(2)}, u32[]{:S(2)}) collective-permute-start(bf16[32,16,128]{2,1,0:T(8,128)(2,1)S(1)} %copy-done.60), channel_id=1, source_target_pairs={{0,28},{4,24},{8,20},{12,16},{16,12},{20,8},{24,4},{28,0},{1,29},{... | collective-permute-start | bytes 393224 | tf_op jit(solution)/shard_map/ppermute | solution.py:348
  112.7 5.6 %collective-permute-done.29.refs_4_ = bf16[32,16,128]{2,1,0:T(8,128)(2,1)S(1)} collective-permute-done((bf16[32,16,128]{2,1,0:T(8,128)(2,1)}, bf16[32,16,128]{2,1,0:T(8,128)(2,1)S(1)}, u32[]{:S(2)}, u32[]{:S(2)}) %collective-permute-start.29) | collective-permute-done | bytes 131104 | tf_op jit(solution)/shard_map/ppermute | solution.py:348
  118.2 3.0 %collective-permute-done.30.refs_5_ = bf16[32,16,128]{2,1,0:T(8,128)(2,1)S(1)} collective-permute-done((bf16[32,16,128]{2,1,0:T(8,128)(2,1)}, bf16[32,16,128]{2,1,0:T(8,128)(2,1)S(1)}, u32[]{:S(2)}, u32[]{:S(2)}) %collective-permute-start.30) | collective-permute-done | bytes 131104 | tf_op jit(solution)/shard_map/ppermute | solution.py:348
  121.4 3.7 %middle.5 = (bf16[32,2,16,128]{3,2,1,0:T(8,128)(2,1)}, bf16[32,2,16,128]{3,2,1,0:T(8,128)(2,1)}, bf16[32,2,16,128]{3,2,1,0:T(8,128)(2,1)}, bf16[32,2,16,128]{3,2,1,0:T(8,128)(2,1)}) custom-call(s32[1]{0:T(128)} %bitcast.me_ref.grid_ref, bf16[16,2,32,128]{3,2,1,0:T(8,128)(2,1)} %get-tuple-element.155.refs_0_, bf16[16,2,32,128]{3,2,1,0:T(8,128)(2,1)} %copy-done.11, ...), custom_call_target="tpu_custom_call" | custom-call | flops 536870912 | bytes 3145728 | tf_op jit(solution)/shard_map/middle/pallas_call | solution.py:258
  127.8 5.8 %forward.3 = (bf16[256,16,128]{2,1,0:T(8,128)(2,1)}, bf16[16,2,32,128]{3,2,1,0:T(8,128)(2,1)}, bf16[16,2,32,128]{3,2,1,0:T(8,128)(2,1)}, bf16[16,2,32,128]{3,2,1...) custom-call(s32[1]{0:T(128)} %bitcast.1.me_ref, ...), custom_call_target="tpu_custom_call" | custom-call | flops 1073741824 | bytes 6291456 | tf_op jit(solution)/shard_map/forward/pallas_call | solution.py:206
  137.7 5.4 %collective-permute-done.37.refs_2_ = bf16[16,2,32,128]{3,2,1,0:T(8,128)(2,1)S(1)} collective-permute-done((bf16[16,2,32,128]{3,2,1,0:T(8,128)(2,1)}, bf16[16,2,32,128]{3,2,1,0:T(8,128)(2,1)S(1)}, u32[]{:S(2)}, u32[]{:S(2)}) %collective-permute-start.37) | collective-permute-done | bytes 262176 | tf_op jit(solution)/shard_map/ppermute | solution.py:348
  143.9 4.9 %collective-permute-done.40.refs_2_ = bf16[16,2,32,128]{3,2,1,0:T(8,128)(2,1)S(1)} collective-permute-done((bf16[16,2,32,128]{3,2,1,0:T(8,128)(2,1)}, bf16[16,2,32,128]{3,2,1,0:T(8,128)(2,1)S(1)}, u32[]{:S(2)}, u32[]{:S(2)}) %collective-permute-start.40) | collective-permute-done | bytes 262176 | tf_op jit(solution)/shard_map/ppermute | solution.py:348
  149.4 3.9 %collective-permute-done.41.refs_3_ = bf16[16,2,32,128]{3,2,1,0:T(8,128)(2,1)S(1)} collective-permute-done((bf16[16,2,32,128]{3,2,1,0:T(8,128)(2,1)}, bf16[16,2,32,128]{3,2,1,0:T(8,128)(2,1)S(1)}, u32[]{:S(2)}, u32[]{:S(2)}) %collective-permute-start.41) | collective-permute-done | bytes 262176 | tf_op jit(solution)/shard_map/ppermute | solution.py:348
  154.7 3.7 %middle.7 = (bf16[16,2,16,128]{3,2,1,0:T(8,128)(2,1)}, bf16[16,2,16,128]{3,2,1,0:T(8,128)(2,1)}, bf16[16,2,16,128]{3,2,1,0:T(8,128)(2,1)}, bf16[16,2,16,128]{3,2...) custom-call(s32[1]{0:T(128)} %bitcast.me_ref.grid_ref, ...), custom_call_target="tpu_custom_call" | custom-call | flops 536870912 | bytes 3145728 | tf_op jit(solution)/shard_map/middle/pallas_call | solution.py:258
  160.1 3.6 %middle.6 = (bf16[32,2,16,128]{3,2,1,0:T(8,128)(2,1)}, bf16[32,2,16,128]{3,2,1,0:T(8,128)(2,1)}, bf16[32,2,16,128]{3,2,1,0:T(8,128)(2,1)}, bf16[32,2,16,128]{3,2,1,0:T(8,128)(2,1)}) custom-call(s32[1]{0:T(128)} %bitcast.me_ref.grid_ref, bf16[16,2,32,128]{3,2,1,0:T(8,128)(2,1)} %get-tuple-element.198.refs_0_, bf16[16,2,32,128]{3,2,1,0:T(8,128)(2,1)} %copy-done.15, ...), custom_call_target="tpu_custom_call" | custom-call | flops 536870912 | bytes 3145728 | tf_op jit(solution)/shard_map/middle/pallas_call | solution.py:258
  166.1 5.2 %collective-permute-done.46.refs_5_ = bf16[32,2,16,128]{3,2,1,0:T(8,128)(2,1)S(1)} collective-permute-done((bf16[32,2,16,128]{3,2,1,0:T(8,128)(2,1)}, bf16[32,2,16,128]{3,2,1,0:T(8,128)(2,1)S(1)}, u32[]{:S(2)}, u32[]{:S(2)}) %collective-permute-start.46) | collective-permute-done | bytes 262176 | tf_op jit(solution)/shard_map/ppermute | solution.py:348
  171.3 4.5 %collective-permute-done.47.refs_7_ = bf16[32,2,16,128]{3,2,1,0:T(8,128)(2,1)S(1)} collective-permute-done((bf16[32,2,16,128]{3,2,1,0:T(8,128)(2,1)}, bf16[32,2,16,128]{3,2,1,0:T(8,128)(2,1)S(1)}, u32[]{:S(2)}, u32[]{:S(2)}) %collective-permute-start.47) | collective-permute-done | bytes 262176 | tf_op jit(solution)/shard_map/ppermute | solution.py:348
  180.7 4.2 %backward.4.refs_12_ = f32[2,32,128,128]{3,2,1,0:T(8,128)} custom-call(bf16[32,2,16,128]{3,2,1,0:T(8,128)(2,1)} %get-tuple-element.215.refs_0_, bf16[32,2,16,128]{3,2,1,0:T(8,128)(2,1)} %get-tuple-element.186.refs_1_, bf16[32,2,16,128]{3,2,1,0:T(8,128)(2,1)} %copy-done.2, bf16[32,2,16,128]{3,2,1,0:T(8,128)(2,1)} %copy-done.6, ...), custom_call_target="tpu_custom_call" | custom-call | flops 536870912 | bytes 6291456 | tf_op jit(solution)/shard_map/backward/pallas_call | solution.py:325
  185.0 4.3 %backward.5.refs_12_ = f32[2,32,128,128]{3,2,1,0:T(8,128)} custom-call(bf16[32,2,16,128]{3,2,1,0:T(8,128)(2,1)} %get-tuple-element.215.refs_0_, bf16[32,2,16,128]{3,2,1,0:T(8,128)(2,1)} %get-tuple-element.186.refs_1_, bf16[32,2,16,128]{3,2,1,0:T(8,128)(2,1)} %copy-done.2, bf16[32,2,16,128]{3,2,1,0:T(8,128)(2,1)} %copy-done.6, ...), custom_call_target="tpu_custom_call", output_to_operand_aliasing={{}: (12, {})} | custom-call | flops 536870912 | bytes 6291456 | tf_op jit(solution)/shard_map/backward/pallas_call | solution.py:325
  195.2 4.4 %backward.6.refs_12_ = f32[2,32,128,128]{3,2,1,0:T(8,128)} custom-call(bf16[32,2,16,128]{3,2,1,0:T(8,128)(2,1)} %get-tuple-element.202.refs_0_, bf16[16,2,16,128]{3,2,1,0:T(8,128)(2,1)} %get-tuple-element.211.refs_1_, bf16[32,2,16,128]{3,2,1,0:T(8,128)(2,1)} %copy-done.5, bf16[16,2,16,128]{3,2,1,0:T(8,128)(2,1)} %copy-done.23, ...), custom_call_target="tpu_custom_call", output_to_operand_aliasing={{}: (12, {})} | custom-call | flops 536870912 | bytes 6291456 | tf_op jit(solution)/shard_map/backward/pallas_call | solution.py:325
  201.3 4.5 %backward.7 = f32[2,32,128,128]{3,2,1,0:T(8,128)} custom-call(bf16[32,2,16,128]{3,2,1,0:T(8,128)(2,1)} %get-tuple-element.202.refs_0_, bf16[16,2,16,128]{3,2,1,0:T(8,128)(2,1)} %get-tuple-element.220.refs_1_, bf16[32,2,16,128]{3,2,1,0:T(8,128)(2,1)} %copy-done.5, bf16[16,2,16,128]{3,2,1,0:T(8,128)(2,1)} %copy-done.26, ...), custom_call_target="tpu_custom_call", output_to_operand_aliasing={{}: (12, {})} | custom-call | flops 536870912 | bytes 6291456 | tf_op jit(solution)/shard_map/backward/pallas_call | solution.py:325
  (270 shorter events, 67.1 us)
Async XLA Ops:
  8.2 16.2 %collective-permute-start.5 = (bf16[32,16,128]{2,1,0:T(8,128)(2,1)S(1)}, bf16[32,16,128]{2,1,0:T(8,128)(2,1)S(1)}, u32[]{:S(2)}, u32[]{:S(2)}) collective-permute-start(bf16[32,16,128]{2,1,0:T(8,128)(2,1)S(1)} %get-tuple-element.229), channel_id=1, source_target_pairs={{0,24},{4,28},{8,16},{12,20},{16,8},{20,12},{24,0},{28,4},{1,25},{... | collective-permute-start | bytes 393224 | tf_op jit(solution)/shard_map/ppermute | solution.py:348
  8.5 20.3 %collective-permute-start.4 = (bf16[32,16,128]{2,1,0:T(8,128)(2,1)S(1)}, bf16[32,16,128]{2,1,0:T(8,128)(2,1)S(1)}, u32[]{:S(2)}, u32[]{:S(2)}) collective-permute-start(bf16[32,16,128]{2,1,0:T(8,128)(2,1)S(1)} %get-tuple-element.230), channel_id=1, source_target_pairs={{0,20},{4,16},{8,28},{12,24},{16,4},{20,0},{24,12},{28,8},{1,21},{... | collective-permute-start | bytes 393224 | tf_op jit(solution)/shard_map/ppermute | solution.py:348
  9.2 21.6 %collective-permute-start.3 = (bf16[32,16,128]{2,1,0:T(8,128)(2,1)S(1)}, bf16[32,16,128]{2,1,0:T(8,128)(2,1)S(1)}, u32[]{:S(2)}, u32[]{:S(2)}) collective-permute-start(bf16[32,16,128]{2,1,0:T(8,128)(2,1)S(1)} %get-tuple-element.231), channel_id=1, source_target_pairs={{0,16},{4,20},{8,24},{12,28},{16,0},{20,4},{24,8},{28,12},{1,17},{... | collective-permute-start | bytes 393224 | tf_op jit(solution)/shard_map/ppermute | solution.py:348
  13.6 34.4 %collective-permute-start.7 = (bf16[128,2048]{1,0:T(8,128)(2,1)}, bf16[128,2048]{1,0:T(8,128)(2,1)S(1)}, u32[]{:S(2)}, u32[]{:S(2)}) collective-permute-start(bf16[128,2048]{1,0:T(8,128)(2,1)} %get-tuple-element.127), channel_id=1, source_target_pairs={{0,3},{1,2},{2,1},{3,0},{4,7},{5,6},{6,5},{7,4},{8,11},{9,10},{10,... | collective-permute-start | bytes 1572872 | tf_op jit(solution)/shard_map/ppermute | solution.py:425
  16.7 16.7 %collective-permute-start.2 = (bf16[32,16,128]{2,1,0:T(8,128)(2,1)S(1)}, bf16[32,16,128]{2,1,0:T(8,128)(2,1)S(1)}, u32[]{:S(2)}, u32[]{:S(2)}) collective-permute-start(bf16[32,16,128]{2,1,0:T(8,128)(2,1)S(1)} %get-tuple-element.232), channel_id=1, source_target_pairs={{0,12},{4,8},{8,4},{12,0},{16,28},{20,24},{24,20},{28,16},{1,13},{... | collective-permute-start | bytes 393224 | tf_op jit(solution)/shard_map/ppermute | solution.py:348
  39.1 20.5 %collective-permute-start.18 = (bf16[32,16,128]{2,1,0:T(8,128)(2,1)}, bf16[32,16,128]{2,1,0:T(8,128)(2,1)S(1)}, u32[]{:S(2)}, u32[]{:S(2)}) collective-permute-start(bf16[32,16,128]{2,1,0:T(8,128)(2,1)} %get-tuple-element.140), channel_id=1, source_target_pairs={{0,12},{4,8},{8,4},{12,0},{16,28},{20,24},{24,20},{28,16},{1,13},{... | collective-permute-start | bytes 393224 | tf_op jit(solution)/shard_map/ppermute | solution.py:348
  41.7 20.0 %collective-permute-start.19 = (bf16[32,16,128]{2,1,0:T(8,128)(2,1)}, bf16[32,16,128]{2,1,0:T(8,128)(2,1)S(1)}, u32[]{:S(2)}, u32[]{:S(2)}) collective-permute-start(bf16[32,16,128]{2,1,0:T(8,128)(2,1)} %get-tuple-element.141), channel_id=1, source_target_pairs={{0,16},{4,20},{8,24},{12,28},{16,0},{20,4},{24,8},{28,12},{1,17},{... | collective-permute-start | bytes 393224 | tf_op jit(solution)/shard_map/ppermute | solution.py:348
  44.1 18.4 %collective-permute-start.20 = (bf16[32,16,128]{2,1,0:T(8,128)(2,1)}, bf16[32,16,128]{2,1,0:T(8,128)(2,1)S(1)}, u32[]{:S(2)}, u32[]{:S(2)}) collective-permute-start(bf16[32,16,128]{2,1,0:T(8,128)(2,1)} %get-tuple-element.142), channel_id=1, source_target_pairs={{0,20},{4,16},{8,28},{12,24},{16,4},{20,0},{24,12},{28,8},{1,21},{... | collective-permute-start | bytes 393224 | tf_op jit(solution)/shard_map/ppermute | solution.py:348
  46.8 16.6 %collective-permute-start.21 = (bf16[32,16,128]{2,1,0:T(8,128)(2,1)}, bf16[32,16,128]{2,1,0:T(8,128)(2,1)S(1)}, u32[]{:S(2)}, u32[]{:S(2)}) collective-permute-start(bf16[32,16,128]{2,1,0:T(8,128)(2,1)} %get-tuple-element.143), channel_id=1, source_target_pairs={{0,24},{4,28},{8,16},{12,20},{16,8},{20,12},{24,0},{28,4},{1,25},{... | collective-permute-start | bytes 393224 | tf_op jit(solution)/shard_map/ppermute | solution.py:348
  48.0 20.5 %collective-permute-start.22 = (bf16[32,16,128]{2,1,0:T(8,128)(2,1)}, bf16[32,16,128]{2,1,0:T(8,128)(2,1)S(1)}, u32[]{:S(2)}, u32[]{:S(2)}) collective-permute-start(bf16[32,16,128]{2,1,0:T(8,128)(2,1)} %get-tuple-element.144), channel_id=1, source_target_pairs={{0,28},{4,24},{8,20},{12,16},{16,12},{20,8},{24,4},{28,0},{1,29},{... | collective-permute-start | bytes 393224 | tf_op jit(solution)/shard_map/ppermute | solution.py:348
  59.7 21.0 %collective-permute-start.9 = (bf16[32,16,128]{2,1,0:T(8,128)(2,1)S(1)}, bf16[32,16,128]{2,1,0:T(8,128)(2,1)S(1)}, u32[]{:S(2)}, u32[]{:S(2)}) collective-permute-start(bf16[32,16,128]{2,1,0:T(8,128)(2,1)S(1)} %copy-done.52), channel_id=1, source_target_pairs={{0,4},{4,0},{8,12},{12,8},{16,20},{20,16},{24,28},{28,24},{1,5},{5... | collective-permute-start | bytes 393224 | tf_op jit(solution)/shard_map/ppermute | solution.py:348
  61.7 19.1 %collective-permute-start.10 = (bf16[32,16,128]{2,1,0:T(8,128)(2,1)S(1)}, bf16[32,16,128]{2,1,0:T(8,128)(2,1)S(1)}, u32[]{:S(2)}, u32[]{:S(2)}) collective-permute-start(bf16[32,16,128]{2,1,0:T(8,128)(2,1)S(1)} %copy-done.51), channel_id=1, source_target_pairs={{0,8},{4,12},{8,0},{12,4},{16,24},{20,28},{24,16},{28,20},{1,9},{5... | collective-permute-start | bytes 393224 | tf_op jit(solution)/shard_map/ppermute | solution.py:348
  62.6 18.7 %collective-permute-start.11 = (bf16[32,16,128]{2,1,0:T(8,128)(2,1)S(1)}, bf16[32,16,128]{2,1,0:T(8,128)(2,1)S(1)}, u32[]{:S(2)}, u32[]{:S(2)}) collective-permute-start(bf16[32,16,128]{2,1,0:T(8,128)(2,1)S(1)} %copy-done.50), channel_id=1, source_target_pairs={{0,12},{4,8},{8,4},{12,0},{16,28},{20,24},{24,20},{28,16},{1,13},{... | collective-permute-start | bytes 393224 | tf_op jit(solution)/shard_map/ppermute | solution.py:348
  63.4 19.4 %collective-permute-start.12 = (bf16[32,16,128]{2,1,0:T(8,128)(2,1)S(1)}, bf16[32,16,128]{2,1,0:T(8,128)(2,1)S(1)}, u32[]{:S(2)}, u32[]{:S(2)}) collective-permute-start(bf16[32,16,128]{2,1,0:T(8,128)(2,1)S(1)} %copy-done.49), channel_id=1, source_target_pairs={{0,16},{4,20},{8,24},{12,28},{16,0},{20,4},{24,8},{28,12},{1,17},{... | collective-permute-start | bytes 393224 | tf_op jit(solution)/shard_map/ppermute | solution.py:348
  68.5 16.5 %collective-permute-start.13 = (bf16[32,16,128]{2,1,0:T(8,128)(2,1)S(1)}, bf16[32,16,128]{2,1,0:T(8,128)(2,1)S(1)}, u32[]{:S(2)}, u32[]{:S(2)}) collective-permute-start(bf16[32,16,128]{2,1,0:T(8,128)(2,1)S(1)} %copy-done.48), channel_id=1, source_target_pairs={{0,20},{4,16},{8,28},{12,24},{16,4},{20,0},{24,12},{28,8},{1,21},{... | collective-permute-start | bytes 393224 | tf_op jit(solution)/shard_map/ppermute | solution.py:348
  80.8 17.4 %collective-permute-start.33 = (bf16[16,2,32,128]{3,2,1,0:T(8,128)(2,1)}, bf16[16,2,32,128]{3,2,1,0:T(8,128)(2,1)S(1)}, u32[]{:S(2)}, u32[]{:S(2)}) collective-permute-start(bf16[16,2,32,128]{3,2,1,0:T(8,128)(2,1)} %get-tuple-element.157), channel_id=1, source_target_pairs={{0,1},{1,0},{2,3},{3,2},{4,5},{5,4},{6,7},{7,6},{8,9},{9,8},{10,11... | collective-permute-start | bytes 786440 | tf_op jit(solution)/shard_map/ppermute | solution.py:348
  81.3 21.1 %collective-permute-start.24 = (bf16[16,2,32,128]{3,2,1,0:T(8,128)(2,1)}, bf16[16,2,32,128]{3,2,1,0:T(8,128)(2,1)S(1)}, u32[]{:S(2)}, u32[]{:S(2)}) collective-permute-start(bf16[16,2,32,128]{3,2,1,0:T(8,128)(2,1)} %get-tuple-element.158), channel_id=1, source_target_pairs={{0,2},{1,3},{2,0},{3,1},{4,6},{5,7},{6,4},{7,5},{8,10},{9,11},{10,... | collective-permute-start | bytes 786440 | tf_op jit(solution)/shard_map/ppermute | solution.py:348
  93.5 15.8 %collective-permute-start.34 = (bf16[16,2,32,128]{3,2,1,0:T(8,128)(2,1)}, bf16[16,2,32,128]{3,2,1,0:T(8,128)(2,1)S(1)}, u32[]{:S(2)}, u32[]{:S(2)}) collective-permute-start(bf16[16,2,32,128]{3,2,1,0:T(8,128)(2,1)} %get-tuple-element.159), channel_id=1, source_target_pairs={{0,2},{1,3},{2,0},{3,1},{4,6},{5,7},{6,4},{7,5},{8,10},{9,11},{10,... | collective-permute-start | bytes 786440 | tf_op jit(solution)/shard_map/ppermute | solution.py:348
  98.2 20.0 %collective-permute-start.29 = (bf16[32,16,128]{2,1,0:T(8,128)(2,1)}, bf16[32,16,128]{2,1,0:T(8,128)(2,1)S(1)}, u32[]{:S(2)}, u32[]{:S(2)}) collective-permute-start(bf16[32,16,128]{2,1,0:T(8,128)(2,1)} %get-tuple-element.182), channel_id=1, source_target_pairs={{0,16},{4,20},{8,24},{12,28},{16,0},{20,4},{24,8},{28,12},{1,17},{... | collective-permute-start | bytes 393224 | tf_op jit(solution)/shard_map/ppermute | solution.py:348
  102.4 18.9 %collective-permute-start.30 = (bf16[32,16,128]{2,1,0:T(8,128)(2,1)}, bf16[32,16,128]{2,1,0:T(8,128)(2,1)S(1)}, u32[]{:S(2)}, u32[]{:S(2)}) collective-permute-start(bf16[32,16,128]{2,1,0:T(8,128)(2,1)} %get-tuple-element.183), channel_id=1, source_target_pairs={{0,20},{4,16},{8,28},{12,24},{16,4},{20,0},{24,12},{28,8},{1,21},{... | collective-permute-start | bytes 393224 | tf_op jit(solution)/shard_map/ppermute | solution.py:348
  103.6 17.7 %collective-permute-start.31 = (bf16[32,16,128]{2,1,0:T(8,128)(2,1)}, bf16[32,16,128]{2,1,0:T(8,128)(2,1)S(1)}, u32[]{:S(2)}, u32[]{:S(2)}) collective-permute-start(bf16[32,16,128]{2,1,0:T(8,128)(2,1)} %get-tuple-element.184), channel_id=1, source_target_pairs={{0,24},{4,28},{8,16},{12,20},{16,8},{20,12},{24,0},{28,4},{1,25},{... | collective-permute-start | bytes 393224 | tf_op jit(solution)/shard_map/ppermute | solution.py:348
  136.0 17.4 %collective-permute-start.41 = (bf16[16,2,32,128]{3,2,1,0:T(8,128)(2,1)}, bf16[16,2,32,128]{3,2,1,0:T(8,128)(2,1)S(1)}, u32[]{:S(2)}, u32[]{:S(2)}) collective-permute-start(bf16[16,2,32,128]{3,2,1,0:T(8,128)(2,1)} %get-tuple-element.206), channel_id=1, source_target_pairs={{0,3},{1,2},{2,1},{3,0},{4,7},{5,6},{6,5},{7,4},{8,11},{9,10},{10,... | collective-permute-start | bytes 786440 | tf_op jit(solution)/shard_map/ppermute | solution.py:348
  136.3 22.7 %collective-permute-start.38 = (bf16[16,2,32,128]{3,2,1,0:T(8,128)(2,1)}, bf16[16,2,32,128]{3,2,1,0:T(8,128)(2,1)S(1)}, u32[]{:S(2)}, u32[]{:S(2)}) collective-permute-start(bf16[16,2,32,128]{3,2,1,0:T(8,128)(2,1)} %get-tuple-element.201), channel_id=1, source_target_pairs={{0,3},{1,2},{2,1},{3,0},{4,7},{5,6},{6,5},{7,4},{8,11},{9,10},{10,... | collective-permute-start | bytes 786440 | tf_op jit(solution)/shard_map/ppermute | solution.py:348
  143.2 21.4 %collective-permute-start.44 = (bf16[32,2,16,128]{3,2,1,0:T(8,128)(2,1)S(1)}, bf16[32,2,16,128]{3,2,1,0:T(8,128)(2,1)S(1)}, u32[]{:S(2)}, u32[]{:S(2)}) collective-permute-start(bf16[32,2,16,128]{3,2,1,0:T(8,128)(2,1)S(1)} %copy-done.45), channel_id=1, source_target_pairs={{0,3},{1,2},{2,1},{3,0},{4,7},{5,6},{6,5},{7,4},{8,11},{9,10},{10,... | collective-permute-start | bytes 786440 | tf_op jit(solution)/shard_map/ppermute | solution.py:348
  143.2 22.3 %collective-permute-start.45 = (bf16[32,2,16,128]{3,2,1,0:T(8,128)(2,1)}, bf16[32,2,16,128]{3,2,1,0:T(8,128)(2,1)S(1)}, u32[]{:S(2)}, u32[]{:S(2)}) collective-permute-start(bf16[32,2,16,128]{3,2,1,0:T(8,128)(2,1)} %get-tuple-element.187), channel_id=1, source_target_pairs={{0,1},{1,0},{2,3},{3,2},{4,5},{5,4},{6,7},{7,6},{8,9},{9,8},{10,11... | collective-permute-start | bytes 786440 | tf_op jit(solution)/shard_map/ppermute | solution.py:348
  148.8 22.5 %collective-permute-start.46 = (bf16[32,2,16,128]{3,2,1,0:T(8,128)(2,1)}, bf16[32,2,16,128]{3,2,1,0:T(8,128)(2,1)S(1)}, u32[]{:S(2)}, u32[]{:S(2)}) collective-permute-start(bf16[32,2,16,128]{3,2,1,0:T(8,128)(2,1)} %get-tuple-element.188), channel_id=1, source_target_pairs={{0,2},{1,3},{2,0},{3,1},{4,6},{5,7},{6,4},{7,5},{8,10},{9,11},{10,... | collective-permute-start | bytes 786440 | tf_op jit(solution)/shard_map/ppermute | solution.py:348
  153.3 22.5 %collective-permute-start.47 = (bf16[32,2,16,128]{3,2,1,0:T(8,128)(2,1)}, bf16[32,2,16,128]{3,2,1,0:T(8,128)(2,1)S(1)}, u32[]{:S(2)}, u32[]{:S(2)}) collective-permute-start(bf16[32,2,16,128]{3,2,1,0:T(8,128)(2,1)} %get-tuple-element.189), channel_id=1, source_target_pairs={{0,3},{1,2},{2,1},{3,0},{4,7},{5,6},{6,5},{7,4},{8,11},{9,10},{10,... | collective-permute-start | bytes 786440 | tf_op jit(solution)/shard_map/ppermute | solution.py:348
  158.9 17.6 %collective-permute-start.54 = (bf16[16,2,16,128]{3,2,1,0:T(8,128)(2,1)}, bf16[16,2,16,128]{3,2,1,0:T(8,128)(2,1)S(1)}, u32[]{:S(2)}, u32[]{:S(2)}) collective-permute-start(bf16[16,2,16,128]{3,2,1,0:T(8,128)(2,1)} %get-tuple-element.212), channel_id=1, source_target_pairs={{0,1},{1,0},{2,3},{3,2},{4,5},{5,4},{6,7},{7,6},{8,9},{9,8},{10,11... | collective-permute-start | bytes 393224 | tf_op jit(solution)/shard_map/ppermute | solution.py:348
  164.5 28.7 %collective-permute-start.48 = (bf16[32,2,16,128]{3,2,1,0:T(8,128)(2,1)}, bf16[32,2,16,128]{3,2,1,0:T(8,128)(2,1)S(1)}, u32[]{:S(2)}, u32[]{:S(2)}) collective-permute-start(bf16[32,2,16,128]{3,2,1,0:T(8,128)(2,1)} %get-tuple-element.221), channel_id=1, source_target_pairs={{0,1},{1,0},{2,3},{3,2},{4,5},{5,4},{6,7},{7,6},{8,9},{9,8},{10,11... | collective-permute-start | bytes 786440 | tf_op jit(solution)/shard_map/ppermute | solution.py:348
  165.5 29.0 %collective-permute-start.50 = (bf16[32,2,16,128]{3,2,1,0:T(8,128)(2,1)}, bf16[32,2,16,128]{3,2,1,0:T(8,128)(2,1)S(1)}, u32[]{:S(2)}, u32[]{:S(2)}) collective-permute-start(bf16[32,2,16,128]{3,2,1,0:T(8,128)(2,1)} %get-tuple-element.223), channel_id=1, source_target_pairs={{0,2},{1,3},{2,0},{3,1},{4,6},{5,7},{6,4},{7,5},{8,10},{9,11},{10,... | collective-permute-start | bytes 786440 | tf_op jit(solution)/shard_map/ppermute | solution.py:348
  171.2 23.2 %collective-permute-start.52 = (bf16[32,2,16,128]{3,2,1,0:T(8,128)(2,1)}, bf16[32,2,16,128]{3,2,1,0:T(8,128)(2,1)S(1)}, u32[]{:S(2)}, u32[]{:S(2)}) collective-permute-start(bf16[32,2,16,128]{3,2,1,0:T(8,128)(2,1)} %get-tuple-element.225), channel_id=1, source_target_pairs={{0,3},{1,2},{2,1},{3,0},{4,7},{5,6},{6,5},{7,4},{8,11},{9,10},{10,... | collective-permute-start | bytes 786440 | tf_op jit(solution)/shard_map/ppermute | solution.py:348
  176.5 16.1 %collective-permute-start.56 = (bf16[16,2,16,128]{3,2,1,0:T(8,128)(2,1)}, bf16[16,2,16,128]{3,2,1,0:T(8,128)(2,1)S(1)}, u32[]{:S(2)}, u32[]{:S(2)}) collective-permute-start(bf16[16,2,16,128]{3,2,1,0:T(8,128)(2,1)} %get-tuple-element.214), channel_id=1, source_target_pairs={{0,3},{1,2},{2,1},{3,0},{4,7},{5,6},{6,5},{7,4},{8,11},{9,10},{10,... | collective-permute-start | bytes 393224 | tf_op jit(solution)/shard_map/ppermute | solution.py:348
  (100 other events, 1164.0 us)
